TPU v7x, 32 devices: a whole 2x2x4 slice. The times are simulated.
32 devices in a mesh: gx: 4 (over z), gy: 8 (over y, x, core).
Axes of the slice: x: 2, y: 2, z: 4, core: 2. Of those that a mesh axis runs over, the one named last changes fastest.
Arguments:
- patches: bfloat16 [39168, 768], P(('gx', 'gy')), may hold values from -6 to 6
- lengths: int32 [32], P(('gx', 'gy')), may hold values from 122 to 1224, as said below
- cotangent: bfloat16 [39168, 768], P(('gx', 'gy')), may hold values from -6 to 6
- w_qkv: bfloat16 [768, 2304], P('gx', 'gy'), may hold values from -0.21875 to 0.21875
- w_out: bfloat16 [768, 768], P('gx', 'gy'), may hold values from -4 to 4
- w_up: bfloat16 [768, 3072], P('gx', 'gy'), may hold values from -0.21875 to 0.21875
- w_down: bfloat16 [3072, 768], P('gx', 'gy'), may hold values from -0.109375 to 0.109375
- bias_q: bfloat16 [768], P(('gx', 'gy')), may hold values from -3 to 3
- bias_v: bfloat16 [768], P(('gx', 'gy')), may hold values from -3 to 3
- bias_o: bfloat16 [768], P(('gx', 'gy')), may hold values from -1.75 to 1.75
- bias_up: bfloat16 [3072], P(('gx', 'gy')), may hold values from -3 to 3
- bias_down: bfloat16 [768], P(('gx', 'gy')), may hold values from -1.75 to 1.75
- gain_one: bfloat16 [768], P(('gx', 'gy')), may hold values from 0.5 to 1.5
- shift_one: bfloat16 [768], P(('gx', 'gy')), may hold values from -1.75 to 1.75
- gain_two: bfloat16 [768], P(('gx', 'gy')), may hold values from 0.5 to 1.5
- shift_two: bfloat16 [768], P(('gx', 'gy')), may hold values from -1.75 to 1.75
Outputs:
- out_rows: bfloat16 [39168, 768], P(('gx', 'gy'))
- grad_rows: float32 [39168, 768], P(('gx', 'gy'))
- grad_w_qkv: float32 [768, 2304], P('gx', 'gy')
- grad_w_out: float32 [768, 768], P('gx', 'gy')
- grad_w_up: float32 [768, 3072], P('gx', 'gy')
- grad_w_down: float32 [3072, 768], P('gx', 'gy')
- grad_bias_q: float32 [768], P(('gx', 'gy'))
- grad_bias_v: float32 [768], P(('gx', 'gy'))
- grad_bias_o: float32 [768], P(('gx', 'gy'))
- grad_bias_up: float32 [3072], P(('gx', 'gy'))
- grad_bias_down: float32 [768], P(('gx', 'gy'))
- grad_gain_one: float32 [768], P(('gx', 'gy'))
- grad_shift_one: float32 [768], P(('gx', 'gy'))
- grad_gain_two: float32 [768], P(('gx', 'gy'))
- grad_shift_two: float32 [768], P(('gx', 'gy'))
Inputs may be any that keep to these rules, and one draw needn't show every extreme that they name: `lengths`: each clip's true patch count; some clip fills all 1224 slots and some clip has 122 patches in every draw.
All inputs are finite; a program needn't handle non-finite values.
Results may differ from a plain program's by a relative error of at most 0.02.
Values may be sent and summed in bfloat16 or wider, within the bound.
No kernel may reach another device: no remote copies, remote signals or barrier semaphores. Data moves between devices by JAX's collectives and lax.ppermute only.
A program may use at most 192 MiB of HBM per device.

v0:
```python
import jax
import jax.numpy as jnp
from jax import lax
from jax.sharding import PartitionSpec as P

HEADS = 12
HEAD_DIM = 64


EPSILON = 1e-06
NEG_FILL = -1e30


def layer_norm(values, gain_vec, shift_vec):
    centre = values - jnp.mean(values, axis=-1, keepdims=True)
    spread = jnp.mean(centre * centre, axis=-1, keepdims=True)
    return centre * lax.rsqrt(spread + EPSILON) * gain_vec + shift_vec


def exact_gelu(values):
    return jax.nn.gelu(values, approximate=False)


def to_blocks(columns, clip_count, pair_count):
    slot_count = columns.shape[0] // clip_count
    pair_width = columns.shape[1] // pair_count
    shaped = columns.reshape(clip_count, slot_count, pair_count, pair_width)
    return jnp.transpose(shaped, (0, 2, 1, 3)).reshape(
        clip_count * pair_count, slot_count, pair_width
    )


def from_blocks(blocks_in, clip_count, pair_count):
    slot_count = blocks_in.shape[1]
    pair_width = blocks_in.shape[2]
    shaped = blocks_in.reshape(clip_count, pair_count, slot_count, pair_width)
    return jnp.transpose(shaped, (0, 2, 1, 3)).reshape(
        clip_count * slot_count, pair_count * pair_width
    )


def block_scores(queries, key_rows, length):
    slot_count = queries.shape[0]
    query_heads = queries.reshape(slot_count, 2, HEAD_DIM)
    key_heads = key_rows.reshape(slot_count, 2, HEAD_DIM)
    scores = jnp.einsum(
        "qhd,khd->hqk", query_heads, key_heads, preferred_element_type=jnp.float32
    ) * HEAD_DIM ** (-0.5)
    live_keys = jnp.arange(slot_count) < length
    return (jnp.where(live_keys[None, None, :], scores, NEG_FILL), query_heads, key_heads)


def attend(block_in):
    queries, key_rows, values, length = block_in
    scores, query_heads, key_heads = block_scores(queries, key_rows, length)
    maximum = jnp.max(scores, axis=-1, keepdims=True)
    exponent = jnp.exp(scores - maximum)
    summed = jnp.sum(exponent, axis=-1, keepdims=True)
    weights = (exponent / summed).astype(jnp.bfloat16)
    value_heads = values.reshape(values.shape[0], 2, HEAD_DIM)
    mixed_heads = jnp.einsum(
        "hqk,khd->qhd", weights, value_heads, preferred_element_type=jnp.float32
    )
    return (
        mixed_heads.reshape(queries.shape[0], 2 * HEAD_DIM),
        (maximum + jnp.log(summed))[..., 0],
    )


def attend_back(block_in):
    queries, key_rows, values, grad_out, log_total, length = block_in
    slot_count = queries.shape[0]
    scores, query_heads, key_heads = block_scores(queries, key_rows, length)
    weights = jnp.exp(scores - log_total[..., None])
    value_heads = values.reshape(slot_count, 2, HEAD_DIM)
    grad_heads = grad_out.reshape(slot_count, 2, HEAD_DIM)
    d_weights = jnp.einsum(
        "qhd,khd->hqk", grad_heads, value_heads, preferred_element_type=jnp.float32
    )
    d_values = jnp.einsum(
        "hqk,qhd->khd", weights.astype(jnp.bfloat16), grad_heads, preferred_element_type=jnp.float32
    )
    row_dots = jnp.sum(weights * d_weights, axis=-1, keepdims=True)
    d_scores = (weights * (d_weights - row_dots)).astype(jnp.bfloat16)
    d_queries = jnp.einsum(
        "hqk,khd->qhd", d_scores, key_heads, preferred_element_type=jnp.float32
    ) * HEAD_DIM ** (-0.5)
    d_keys = jnp.einsum(
        "hqk,qhd->khd", d_scores, query_heads, preferred_element_type=jnp.float32
    ) * HEAD_DIM ** (-0.5)
    return (
        d_queries.reshape(slot_count, 2 * HEAD_DIM),
        d_keys.reshape(slot_count, 2 * HEAD_DIM),
        d_values.reshape(slot_count, 2 * HEAD_DIM),
    )


def per_device(
    patches,
    lengths,
    cotangent,
    w_qkv,
    w_out,
    w_up,
    w_down,
    bias_q,
    bias_v,
    bias_o,
    bias_up,
    bias_down,
    gain_one,
    shift_one,
    gain_two,
    shift_two,
):
    by_cols = (
        lax.all_gather(w_qkv, "gy", axis=1, tiled=True),
        lax.all_gather(w_out, "gy", axis=1, tiled=True),
        lax.all_gather(w_up, "gy", axis=1, tiled=True),
        lax.all_gather(w_down, "gy", axis=1, tiled=True),
        lax.all_gather(bias_q, "gy", axis=0, tiled=True),
        lax.all_gather(bias_v, "gy", axis=0, tiled=True),
        lax.all_gather(bias_o, "gy", axis=0, tiled=True),
        lax.all_gather(bias_up, "gy", axis=0, tiled=True),
        lax.all_gather(bias_down, "gy", axis=0, tiled=True),
        lax.all_gather(gain_one, "gy", axis=0, tiled=True),
        lax.all_gather(shift_one, "gy", axis=0, tiled=True),
        lax.all_gather(gain_two, "gy", axis=0, tiled=True),
        lax.all_gather(shift_two, "gy", axis=0, tiled=True),
    )
    gathered = (
        lax.all_gather(by_cols[0], "gx", axis=0, tiled=True),
        lax.all_gather(by_cols[1], "gx", axis=0, tiled=True),
        lax.all_gather(by_cols[2], "gx", axis=0, tiled=True),
        lax.all_gather(by_cols[3], "gx", axis=0, tiled=True),
        lax.all_gather(by_cols[4], "gx", axis=0, tiled=True),
        lax.all_gather(by_cols[5], "gx", axis=0, tiled=True),
        lax.all_gather(by_cols[6], "gx", axis=0, tiled=True),
        lax.all_gather(by_cols[7], "gx", axis=0, tiled=True),
        lax.all_gather(by_cols[8], "gx", axis=0, tiled=True),
        lax.all_gather(by_cols[9], "gx", axis=0, tiled=True),
        lax.all_gather(by_cols[10], "gx", axis=0, tiled=True),
        lax.all_gather(by_cols[11], "gx", axis=0, tiled=True),
        lax.all_gather(by_cols[12], "gx", axis=0, tiled=True),
    )
    mat_qkv, mat_out, mat_up, mat_down = (gathered[0], gathered[1], gathered[2], gathered[3])
    vec_q, vec_v, vec_o, vec_up, vec_down, gain_a, shift_a, gain_b, shift_b = [
        member.astype(jnp.float32) for member in gathered[4:]
    ]
    clip_count = lengths.shape[0]
    slot_count = patches.shape[0] // clip_count
    model_width = patches.shape[1]
    pair_count = HEADS // 2
    inputs32 = patches.astype(jnp.float32)
    normed, norm_pull = jax.vjp(layer_norm, inputs32, gain_a, shift_a)
    normed_low = normed.astype(jnp.bfloat16)
    bias_all = jnp.concatenate([vec_q, jnp.zeros_like(vec_q), vec_v])
    project = (jnp.dot(normed_low, mat_qkv, preferred_element_type=jnp.float32) + bias_all).astype(
        jnp.bfloat16
    )
    query_blocks = to_blocks(project[:, :model_width], clip_count, pair_count)
    key_blocks = to_blocks(project[:, model_width : 2 * model_width], clip_count, pair_count)
    value_blocks = to_blocks(project[:, 2 * model_width :], clip_count, pair_count)
    pair_lengths = jnp.repeat(lengths, pair_count)
    mixed_blocks, total_blocks = lax.map(
        attend, (query_blocks, key_blocks, value_blocks, pair_lengths)
    )
    mixed_low = from_blocks(mixed_blocks, clip_count, pair_count).astype(jnp.bfloat16)
    residual = inputs32 + jnp.dot(mixed_low, mat_out, preferred_element_type=jnp.float32) + vec_o
    normed_two, norm_pull_two = jax.vjp(layer_norm, residual, gain_b, shift_b)
    normed_two_low = normed_two.astype(jnp.bfloat16)
    inner_pre = jnp.dot(normed_two_low, mat_up, preferred_element_type=jnp.float32) + vec_up
    active, gelu_pull = jax.vjp(exact_gelu, inner_pre)
    active_low = active.astype(jnp.bfloat16)
    outputs = (
        residual + jnp.dot(active_low, mat_down, preferred_element_type=jnp.float32) + vec_down
    ).astype(jnp.bfloat16)
    regather_cols = (
        lax.all_gather(w_qkv, "gy", axis=1, tiled=True),
        lax.all_gather(w_out, "gy", axis=1, tiled=True),
        lax.all_gather(w_up, "gy", axis=1, tiled=True),
        lax.all_gather(w_down, "gy", axis=1, tiled=True),
    )
    regathered = (
        lax.all_gather(regather_cols[0], "gx", axis=0, tiled=True),
        lax.all_gather(regather_cols[1], "gx", axis=0, tiled=True),
        lax.all_gather(regather_cols[2], "gx", axis=0, tiled=True),
        lax.all_gather(regather_cols[3], "gx", axis=0, tiled=True),
    )
    back_qkv, back_out, back_up, back_down = (
        regathered[0],
        regathered[1],
        regathered[2],
        regathered[3],
    )
    live_rows = (
        (jnp.arange(slot_count)[None, :] < lengths[:, None]).astype(jnp.float32).reshape(-1, 1)
    )
    seed_grad = cotangent.astype(jnp.float32) * live_rows
    seed_low = seed_grad.astype(jnp.bfloat16)
    grad_bias_down = jnp.sum(seed_grad, axis=0)
    grad_w_down = jnp.einsum("tf,td->fd", active_low, seed_low, preferred_element_type=jnp.float32)
    d_active = jnp.einsum("td,fd->tf", seed_low, back_down, preferred_element_type=jnp.float32)
    d_inner = gelu_pull(d_active)[0].astype(jnp.bfloat16)
    grad_bias_up = jnp.sum(d_inner.astype(jnp.float32), axis=0)
    grad_w_up = jnp.einsum("td,tf->df", normed_two_low, d_inner, preferred_element_type=jnp.float32)
    d_normed_two = jnp.einsum("tf,df->td", d_inner, back_up, preferred_element_type=jnp.float32)
    d_resid_norm, grad_gain_two, grad_shift_two = norm_pull_two(d_normed_two)
    d_residual = seed_grad + d_resid_norm
    grad_bias_o = jnp.sum(d_residual, axis=0)
    d_branch = d_residual.astype(jnp.bfloat16)
    grad_w_out = jnp.einsum("te,td->ed", mixed_low, d_branch, preferred_element_type=jnp.float32)
    d_mixed = jnp.einsum(
        "td,ed->te", d_branch, back_out, preferred_element_type=jnp.float32
    ).astype(jnp.bfloat16)
    grad_blocks = to_blocks(d_mixed, clip_count, pair_count)
    d_queries, d_keys, d_values = lax.map(
        attend_back,
        (query_blocks, key_blocks, value_blocks, grad_blocks, total_blocks, pair_lengths),
    )
    d_project = jnp.concatenate(
        [
            from_blocks(d_queries, clip_count, pair_count),
            from_blocks(d_keys, clip_count, pair_count),
            from_blocks(d_values, clip_count, pair_count),
        ],
        axis=1,
    ).astype(jnp.bfloat16)
    column_sums = jnp.sum(d_project.astype(jnp.float32), axis=0)
    grad_bias_q = column_sums[:model_width]
    grad_bias_v = column_sums[2 * model_width :]
    grad_w_qkv = jnp.einsum("td,te->de", normed_low, d_project, preferred_element_type=jnp.float32)
    d_normed = jnp.einsum("te,de->td", d_project, back_qkv, preferred_element_type=jnp.float32)
    d_input_norm, grad_gain_one, grad_shift_one = norm_pull(d_normed)
    grad_rows = d_residual + d_input_norm
    section_one = (
        lax.psum_scatter(
            grad_w_qkv.astype(jnp.bfloat16), "gx", scatter_dimension=0, tiled=True
        ).astype(jnp.float32),
        lax.psum_scatter(
            grad_w_out.astype(jnp.bfloat16), "gx", scatter_dimension=0, tiled=True
        ).astype(jnp.float32),
        lax.psum_scatter(
            grad_w_up.astype(jnp.bfloat16), "gx", scatter_dimension=0, tiled=True
        ).astype(jnp.float32),
        lax.psum_scatter(
            grad_w_down.astype(jnp.bfloat16), "gx", scatter_dimension=0, tiled=True
        ).astype(jnp.float32),
        lax.psum_scatter(
            grad_bias_q.astype(jnp.bfloat16), "gx", scatter_dimension=0, tiled=True
        ).astype(jnp.float32),
        lax.psum_scatter(
            grad_bias_v.astype(jnp.bfloat16), "gx", scatter_dimension=0, tiled=True
        ).astype(jnp.float32),
        lax.psum_scatter(
            grad_bias_o.astype(jnp.bfloat16), "gx", scatter_dimension=0, tiled=True
        ).astype(jnp.float32),
        lax.psum_scatter(
            grad_bias_up.astype(jnp.bfloat16), "gx", scatter_dimension=0, tiled=True
        ).astype(jnp.float32),
        lax.psum_scatter(
            grad_bias_down.astype(jnp.bfloat16), "gx", scatter_dimension=0, tiled=True
        ).astype(jnp.float32),
        lax.psum_scatter(
            grad_gain_one.astype(jnp.bfloat16), "gx", scatter_dimension=0, tiled=True
        ).astype(jnp.float32),
        lax.psum_scatter(
            grad_shift_one.astype(jnp.bfloat16), "gx", scatter_dimension=0, tiled=True
        ).astype(jnp.float32),
        lax.psum_scatter(
            grad_gain_two.astype(jnp.bfloat16), "gx", scatter_dimension=0, tiled=True
        ).astype(jnp.float32),
        lax.psum_scatter(
            grad_shift_two.astype(jnp.bfloat16), "gx", scatter_dimension=0, tiled=True
        ).astype(jnp.float32),
    )
    reduced = (
        lax.psum_scatter(
            section_one[0].astype(jnp.bfloat16), "gy", scatter_dimension=1, tiled=True
        ).astype(jnp.float32),
        lax.psum_scatter(
            section_one[1].astype(jnp.bfloat16), "gy", scatter_dimension=1, tiled=True
        ).astype(jnp.float32),
        lax.psum_scatter(
            section_one[2].astype(jnp.bfloat16), "gy", scatter_dimension=1, tiled=True
        ).astype(jnp.float32),
        lax.psum_scatter(
            section_one[3].astype(jnp.bfloat16), "gy", scatter_dimension=1, tiled=True
        ).astype(jnp.float32),
        lax.psum_scatter(
            section_one[4].astype(jnp.bfloat16), "gy", scatter_dimension=0, tiled=True
        ).astype(jnp.float32),
        lax.psum_scatter(
            section_one[5].astype(jnp.bfloat16), "gy", scatter_dimension=0, tiled=True
        ).astype(jnp.float32),
        lax.psum_scatter(
            section_one[6].astype(jnp.bfloat16), "gy", scatter_dimension=0, tiled=True
        ).astype(jnp.float32),
        lax.psum_scatter(
            section_one[7].astype(jnp.bfloat16), "gy", scatter_dimension=0, tiled=True
        ).astype(jnp.float32),
        lax.psum_scatter(
            section_one[8].astype(jnp.bfloat16), "gy", scatter_dimension=0, tiled=True
        ).astype(jnp.float32),
        lax.psum_scatter(
            section_one[9].astype(jnp.bfloat16), "gy", scatter_dimension=0, tiled=True
        ).astype(jnp.float32),
        lax.psum_scatter(
            section_one[10].astype(jnp.bfloat16), "gy", scatter_dimension=0, tiled=True
        ).astype(jnp.float32),
        lax.psum_scatter(
            section_one[11].astype(jnp.bfloat16), "gy", scatter_dimension=0, tiled=True
        ).astype(jnp.float32),
        lax.psum_scatter(
            section_one[12].astype(jnp.bfloat16), "gy", scatter_dimension=0, tiled=True
        ).astype(jnp.float32),
    )
    return (
        outputs,
        grad_rows,
        reduced[0],
        reduced[1],
        reduced[2],
        reduced[3],
        reduced[4],
        reduced[5],
        reduced[6],
        reduced[7],
        reduced[8],
        reduced[9],
        reduced[10],
        reduced[11],
        reduced[12],
    )


def solution(mesh):
    in_specs = (
        P(("gx", "gy"), None),
        P(("gx", "gy")),
        P(("gx", "gy"), None),
        P("gx", "gy"),
        P("gx", "gy"),
        P("gx", "gy"),
        P("gx", "gy"),
        P(("gx", "gy")),
        P(("gx", "gy")),
        P(("gx", "gy")),
        P(("gx", "gy")),
        P(("gx", "gy")),
        P(("gx", "gy")),
        P(("gx", "gy")),
        P(("gx", "gy")),
        P(("gx", "gy")),
    )
    out_specs = (
        P(("gx", "gy"), None),
        P(("gx", "gy"), None),
        P("gx", "gy"),
        P("gx", "gy"),
        P("gx", "gy"),
        P("gx", "gy"),
        P(("gx", "gy")),
        P(("gx", "gy")),
        P(("gx", "gy")),
        P(("gx", "gy")),
        P(("gx", "gy")),
        P(("gx", "gy")),
        P(("gx", "gy")),
        P(("gx", "gy")),
        P(("gx", "gy")),
    )
    return jax.shard_map(
        per_device, mesh=mesh, in_specs=in_specs, out_specs=out_specs, check_vma=False
    )
```

profile of v0, /device:TPU:0, one launch (start us, length us, event | category | flops | bytes accessed | tf_op | source)
XLA Modules:
  0.0 970.7 jit_solution(14444285091718010703)
XLA Ops:
  10.0 13.0 %all_gather.90 = bf16[192,2304]{0,1:T(8,128)(2,1)S(1)} all-gather(bf16[192,288]{0,1:T(8,128)(2,1)S(1)} %copy.64), channel_id=1, replica_groups=mesh['gx'=4,'gy'=8] {'gy'}, dimensions={1}, use_global_device_ids=true | all-gather | bytes 995328 | tf_op jit(solution)/shard_map/all_gather | solution.py:117
  42.0 13.4 %all-reduce.36 = (bf16[768]{0:T(1024)(128)(2,1)S(1)}, bf16[192]{0:T(256)(128)(2,1)S(1)}, bf16[192]{0:T(256)(128)(2,1)S(1)}, bf16[192]{0:T(256)(128)(2,1)S(1)}, b...) all-reduce(bf16[768]{0:T(1024)(128)(2,1)S(1)} %dynamic-update-slice, ...), channel_id=1, replica_groups=mesh['gx'=4,'gy'=8] {'gy'}, use_global_device_ids=true, to_apply=%add.14 | all-reduce | flops 2112 | bytes 8448
  56.9 19.1 %all-reduce.38 = (bf16[768]{0:T(1024)(128)(2,1)S(1)}, bf16[768]{0:T(1024)(128)(2,1)S(1)}, bf16[768]{0:T(1024)(128)(2,1)S(1)}, bf16[768]{0:T(1024)(128)(2,1)S(1)}...) all-reduce(bf16[768]{0:T(1024)(128)(2,1)S(1)} %dynamic-update-slice, ...), channel_id=1, replica_groups=mesh['gx'=4,'gy'=8] {'gx'}, use_global_device_ids=true, to_apply=%add.7 | all-reduce | flops 5376 | bytes 21504
  76.8 13.6 %all-gather = bf16[4,1,768]{2,1,0:T(2,128)(2,1)S(1)} all-gather(bf16[1,1,768]{2,1,0:T(2,128)(2,1)S(1)} %reshape.302), channel_id=1, replica_groups=mesh['gx'=4,'gy'=8] {'gx'}, dimensions={0}, use_global_device_ids=true | all-gather | bytes 7680 | tf_op jit(solution)/shard_map/all_gather | solution.py:139
  93.0 43.1 %all-gather.8.cloned.1.call-done = bf16[768,2304]{1,0:T(8,128)(2,1)} async-done(((bf16[192,2304]{1,0:T(8,128)(2,1)}), bf16[768,2304]{1,0:T(8,128)(2,1)}) %all-gather.8.cloned.1.call-update) | async-done | bytes 3538960 | tf_op jit(solution)/shard_map/all_gather | solution.py:132
  159.5 65.9 %while.26 = (s32[]{:T(128)}, bf16[6,1224,128]{1,2,0:T(8,128)(2,1)}, f32[6,2,1224]{2,1,0:T(2,128)}, bf16[6,1224,128]{1,2,0:T(8,128)(2,1)}, s32[6]{0:T(128)S(1)}, ...) while((s32[]{:T(128)}, bf16[6,1224,128]{1,2,0:T(8,128)(2,1)}, ...), condition=%wide.region_5.6_spmd, body=%wide.region_2.5_spmd.sunk | while | flops 791035712 | bytes 39813052 | solution.py:165
  231.7 25.5 %all-gather.14.cloned.1.call-done = bf16[768,3072]{1,0:T(8,128)(2,1)} async-done(((bf16[192,3072]{1,0:T(8,128)(2,1)}), bf16[768,3072]{1,0:T(8,128)(2,1)}) %all-gather.14.cloned.1.call-update) | async-done | bytes 4718608 | tf_op jit(solution)/shard_map/all_gather | solution.py:134
  257.2 42.4 %multiply_convert_fusion.1 = (bf16[1224,3072]{1,0:T(8,128)(2,1)}, f32[1224,3072]{1,0:T(8,128)}, f32[1224,3072]{1,0:T(8,128)}) fusion(f32[3072]{0:T(1024)S(1)} %bitcast.196, bf16[768,3072]{1,0:T(8,128)(2,1)} %all-gather.14.cloned.1.call-done, f32[1224,768]{1,0:T(8,128)} %copy-done.2, f32[768]{0:T(1024)S(1)} %convert_element_type.206, ...), kind=kOutput, calls=%fused_computation.34 | convolution fusion | flops 6028425216 | bytes 46108224 | tf_op jit(solution)/shard_map/dot_general | solution.py:172
  299.6 46.9 %all-gather.18.cloned.1.call-done = bf16[3072,768]{0,1:T(8,128)(2,1)} async-done(((bf16[768,768]{0,1:T(8,128)(2,1)}), bf16[3072,768]{0,1:T(8,128)(2,1)}) %all-gather.18.cloned.1.call-update) | async-done | bytes 4718608 | tf_op jit(solution)/shard_map/all_gather | solution.py:135
  346.5 19.9 %fusion.53 = (bf16[3072]{0:T(1024)(128)(2,1)}, bf16[1224,3072]{1,0:T(8,128)(2,1)}) fusion(f32[1224,3072]{1,0:T(8,128)} %get-tuple-element.252, f32[1224,3072]{1,0:T(8,128)} %get-tuple-element.273, bf16[3072,768]{0,1:T(8,128)(2,1)} %all-gather.18.cloned.1.call-done, bf16[1224,768]{1,0:T(8,128)(2,1)S(1)} %copy-done.7, f32[1224]{0:T(1024)S(1)} %copy-done.21), kind=kOutput, calls=%fused_computation.122 | convolution fusion | flops 5834775552 | bytes 44210976 | tf_op jit(solution)/shard_map/td,fd->tf/dot_general | solution.py:203
  366.4 12.7 %multiply_reduce_fusion.1 = (bf16[768]{0:T(1024)(128)(2,1)}, f32[1224]{0:T(1024)S(1)}, bf16[768]{0:T(1024)(128)(2,1)}, f32[1224,768]{1,0:T(8,128)S(1)}) fusion(f32[1224,768]{1,0:T(8,128)} %copy-done.2, f32[1224]{0:T(1024)S(1)} %fusion.37, f32[1224]{0:T(1024)S(1)} %broadcast_multiply_fusion, f32[768]{0:T(1024)S(1)} %convert_element_type.205, ...), kind=kOutput, calls=%fused_computation.74 | convolution fusion | flops 5783073792 | bytes 19779936 | tf_op jit(solution)/shard_map/tf,df->td/dot_general | solution.py:207
  399.1 150.7 %while.27 = (s32[]{:T(128)}, bf16[6,1224,128]{1,2,0:T(8,128)(2,1)}, bf16[6,1224,128]{1,2,0:T(8,128)(2,1)}, bf16[6,1224,128]{1,2,0:T(8,128)(2,1)}, bf16[6,1224,12...) while((s32[]{:T(128)}, bf16[6,1224,128]{1,2,0:T(8,128)(2,1)}, ...), condition=%wide.region_12.13_spmd, body=%wide.region_10.12_spmd.sunk | while | flops 1945257856 | bytes 116307088 | solution.py:217
  560.0 12.1 %convolution_convert_fusion.2 = bf16[768,3072]{1,0:T(8,128)(2,1)} fusion(bf16[1224,3072]{1,0:T(8,128)(2,1)} %get-tuple-element.277, f32[1224,768]{1,0:T(8,128)} %copy-done.2, f32[768]{0:T(1024)S(1)} %copy-done.31, f32[768]{0:T(1024)S(1)} %copy-done.28, f32[1224]{0:T(1024)S(1)} %copy-done.26, f32[1224]{0:T(1024)S(1)} %copy-done.17), kind=kOutput, calls=%fused_computation.63 | convolution fusion | flops 5782616064 | bytes 16014912 | tf_op jit(solution)/shard_map/td,tf->df/dot_general | solution.py:206
  572.9 11.4 %convolution_convert_fusion.1 = bf16[3072,768]{1,0:T(8,128)(2,1)} fusion(bf16[1224,3072]{1,0:T(8,128)(2,1)} %get-tuple-element.251, bf16[1224,768]{1,0:T(8,128)(2,1)} %param.22, f32[1224]{0:T(1024)S(1)} %copy-done.22), kind=kOutput, calls=%fused_computation.62 | convolution fusion | flops 5780736000 | bytes 14123808 | tf_op jit(solution)/shard_map/tf,td->fd/dot_general | solution.py:202
  599.1 25.7 %reduce-scatter.17.cloned.1.call-done = bf16[192,2304]{1,0:T(8,128)(2,1)} async-done(((bf16[768,2304]{1,0:T(8,128)(2,1)}), bf16[192,2304]{1,0:T(8,128)(2,1)}) %reduce-scatter.17.cloned.1.call-update) | async-done | bytes 884752 | tf_op jit(solution)/shard_map/reduce_scatter | solution.py:237
  633.5 79.2 %reduce-scatter.21.cloned.1.call-done = bf16[192,3072]{1,0:T(8,128)(2,1)} async-done(((bf16[768,3072]{1,0:T(8,128)(2,1)}), bf16[192,3072]{1,0:T(8,128)(2,1)}) %reduce-scatter.21.cloned.1.call-update) | async-done | bytes 1179664 | tf_op jit(solution)/shard_map/reduce_scatter | solution.py:243
  722.7 19.6 %all-reduce.37 = (bf16[768]{0:T(1024)(128)(2,1)S(1)}, bf16[768]{0:T(1024)(128)(2,1)S(1)}, bf16[768]{0:T(1024)(128)(2,1)S(1)}, bf16[3072]{0:T(1024)(128)(2,1)S(1)...) all-reduce(bf16[768]{0:T(1024)(128)(2,1)S(1)} %get-tuple-element.26, ...), channel_id=10, replica_groups=mesh['gx'=4,'gy'=8] {'gx'}, use_global_device_ids=true, to_apply=%region_24.25.clone | all-reduce | flops 9216 | bytes 36864
  742.9 13.2 %all-reduce.35 = (bf16[192]{0:T(256)(128)(2,1)S(1)}, bf16[192]{0:T(256)(128)(2,1)S(1)}, bf16[192]{0:T(256)(128)(2,1)S(1)}, bf16[192]{0:T(256)(128)(2,1)S(1)}, bf...) all-reduce(bf16[192]{0:T(256)(128)(2,1)S(1)} %dynamic-update-slice., ...), channel_id=1, replica_groups=mesh['gx'=4,'gy'=8] {'gy'}, use_global_device_ids=true, to_apply=%add.15 | all-reduce | flops 2496 | bytes 9984
  772.4 29.6 %reduce-scatter.23.cloned.1.call-done = bf16[768,768]{1,0:T(8,128)(2,1)} async-done(((bf16[3072,768]{1,0:T(8,128)(2,1)}), bf16[768,768]{1,0:T(8,128)(2,1)}) %reduce-scatter.23.cloned.1.call-update) | async-done | bytes 1179664 | tf_op jit(solution)/shard_map/reduce_scatter | solution.py:246
  804.4 11.3 %fusion.30 = bf16[1224,768]{1,0:T(8,128)(2,1)} fusion(f32[1224,768]{1,0:T(8,128)} %copy-done.2, bf16[1224,3072]{1,0:T(8,128)(2,1)} %get-tuple-element.251, bf16[3072,768]{0,1:T(8,128)(2,1)} %all-gather.18.cloned.1.call-done, f32[768]{0:T(1024)S(1)} %convert_element_type.210), kind=kOutput, calls=%fused_computation.83 | convolution fusion | flops 5778376704 | bytes 17882112 | tf_op jit(solution)/shard_map/dot_general | solution.py:176
  815.7 23.8 %reduce-scatter.27.cloned.1.call-done = bf16[96,192]{1,0:T(8,128)(2,1)} async-done(((bf16[768,192]{1,0:T(8,128)(2,1)}), bf16[96,192]{1,0:T(8,128)(2,1)}) %reduce-scatter.27.cloned.1.call-update) | async-done | bytes 36880
  841.1 38.3 %reduce-scatter.25.cloned.1.call-done = bf16[288,192]{1,0:T(8,128)(2,1)} async-done(((bf16[2304,192]{1,0:T(8,128)(2,1)}), bf16[288,192]{1,0:T(8,128)(2,1)}) %reduce-scatter.25.cloned.1.call-update) | async-done | bytes 110608
  881.1 40.4 %reduce-scatter.29.cloned.1.call-done = bf16[384,192]{1,0:T(8,128)(2,1)} async-done(((bf16[3072,192]{1,0:T(8,128)(2,1)}), bf16[384,192]{1,0:T(8,128)(2,1)}) %reduce-scatter.29.cloned.1.call-update) | async-done | bytes 147472
  923.3 38.4 %reduce-scatter.31.cloned.1.call-done = bf16[96,768]{1,0:T(8,128)(2,1)} async-done(((bf16[768,768]{1,0:T(8,128)(2,1)}), bf16[96,768]{1,0:T(8,128)(2,1)}) %reduce-scatter.31.cloned.1.call-update) | async-done | bytes 147472
  (423 shorter events, 356.7 us)
Async XLA Ops:
  7.2 30.1 %all-gather.12.cloned.1.call-start = ((), (), s32[]{:S(2)}) async-start(), calls=%async_computation.10 | async-start | bytes 1327104 | tf_op jit(solution)/shard_map/all_gather | solution.py:119
  8.0 84.7 %all-gather.16.cloned.1.call-start = ((), (), s32[]{:S(2)}) async-start(), calls=%async_computation.12 | async-start | bytes 1327104 | tf_op jit(solution)/shard_map/all_gather | solution.py:120
  8.8 127.3 %all-gather.8.cloned.1.call-start = ((), (), s32[]{:S(2)}) async-start(), calls=%async_computation.8 | async-start | bytes 4423680 | tf_op jit(solution)/shard_map/all_gather | solution.py:132
  24.4 201.0 %all-gather.10.cloned.1.call-start = ((), (), s32[]{:S(2)}) async-start(), calls=%async_computation.9 | async-start | bytes 1474560 | tf_op jit(solution)/shard_map/all_gather | solution.py:133
  35.9 221.3 %all-gather.14.cloned.1.call-start = ((), (), s32[]{:S(2)}) async-start(), calls=%async_computation.11 | async-start | bytes 5898240 | tf_op jit(solution)/shard_map/all_gather | solution.py:134
  37.4 309.1 %all-gather.18.cloned.1.call-start = ((), (), s32[]{:S(2)}) async-start(), calls=%async_computation.13 | async-start | bytes 5898240 | tf_op jit(solution)/shard_map/all_gather | solution.py:135
  76.8 302.4 %copy-start.27 = (f32[768]{0:T(1024)}, f32[768]{0:T(1024)S(1)}, u32[]{:S(2)}) copy-start(f32[768]{0:T(1024)S(1)} %convert_element_type.205) | copy-start | bytes 9220
  76.8 180.4 %copy-start.30 = (f32[768]{0:T(1024)}, f32[768]{0:T(1024)S(1)}, u32[]{:S(2)}) copy-start(f32[768]{0:T(1024)S(1)} %convert_element_type.206) | copy-start | bytes 9220
  92.7 494.4 %reduce-scatter.19.cloned.1.call-start = ((), (), s32[]{:S(2)}) async-start(), calls=%async_computation.15 | async-start | bytes 1474560 | tf_op jit(solution)/shard_map/reduce_scatter | solution.py:240
  229.2 149.9 %copy-start.16 = (f32[1224]{0:T(1024)}, f32[1224]{0:T(1024)S(1)}, u32[]{:S(2)}) copy-start(f32[1224]{0:T(1024)S(1)} %broadcast_multiply_fusion) | copy-start | bytes 14692
  231.6 147.6 %copy-start.25 = (f32[1224]{0:T(1024)}, f32[1224]{0:T(1024)S(1)}, u32[]{:S(2)}) copy-start(f32[1224]{0:T(1024)S(1)} %fusion.37) | copy-start | bytes 14692
  257.2 89.3 %copy-start.21 = (f32[1224]{0:T(1024)S(1)}, f32[1224]{0:T(1024)}, u32[]{:S(2)}) copy-start(f32[1224]{0:T(1024)} %fusion.35) | copy-start | bytes 14692
  387.6 237.2 %reduce-scatter.17.cloned.1.call-start = ((), (), s32[]{:S(2)}) async-start(), calls=%async_computation.14 | async-start | bytes 4423680 | tf_op jit(solution)/shard_map/reduce_scatter | solution.py:237
  399.0 150.8 %copy-start.1 = (bf16[1224,768]{1,0:T(8,128)(2,1)S(1)}, bf16[1224,768]{1,0:T(8,128)(2,1)}, u32[]{:S(2)}) copy-start(bf16[1224,768]{1,0:T(8,128)(2,1)} %param.20) | copy-start | bytes 5640196
  399.0 150.8 %copy-start.9 = (f32[1224]{0:T(1024)S(1)}, f32[1224]{0:T(1024)}, u32[]{:S(2)}) copy-start(f32[1224]{0:T(1024)} %copy-done.8) | copy-start | bytes 14692
  399.0 150.8 %copy-start.15 = (f32[1224]{0:T(1024)S(1)}, f32[1224]{0:T(1024)}, u32[]{:S(2)}) copy-start(f32[1224]{0:T(1024)} %copy-done.14) | copy-start | bytes 14692
  399.0 150.8 %copy-start.20 = (f32[768]{0:T(1024)S(1)}, f32[768]{0:T(1024)}, u32[]{:S(2)}) copy-start(f32[768]{0:T(1024)} %copy-done.19) | copy-start | bytes 9220
  399.1 150.8 %copy-start.33 = (f32[768]{0:T(1024)S(1)}, f32[768]{0:T(1024)}, u32[]{:S(2)}) copy-start(f32[768]{0:T(1024)} %copy-done.32) | copy-start | bytes 9220
  560.0 152.8 %reduce-scatter.21.cloned.1.call-start = ((), (), s32[]{:S(2)}) async-start(), calls=%async_computation.16 | async-start | bytes 5898240 | tf_op jit(solution)/shard_map/reduce_scatter | solution.py:243
  572.2 229.8 %reduce-scatter.23.cloned.1.call-start = ((), (), s32[]{:S(2)}) async-start(), calls=%async_computation.17 | async-start | bytes 5898240 | tf_op jit(solution)/shard_map/reduce_scatter | solution.py:246
  584.3 255.3 %reduce-scatter.27.cloned.1.call-start = ((), (), s32[]{:S(2)}) async-start(), calls=%async_computation.19 | async-start | bytes 442368
  589.1 290.3 %reduce-scatter.25.cloned.1.call-start = ((), (), s32[]{:S(2)}) async-start(), calls=%async_computation.18 | async-start | bytes 1327104
  627.2 294.3 %reduce-scatter.29.cloned.1.call-start = ((), (), s32[]{:S(2)}) async-start(), calls=%async_computation.20 | async-start | bytes 1769472
  715.3 246.4 %reduce-scatter.31.cloned.1.call-start = ((), (), s32[]{:S(2)}) async-start(), calls=%async_computation.21 | async-start | bytes 1327104
  (52 other events, 1078.7 us)
Sparse Core Ops, SparseCore 0:
  9.9 27.3 all-gather.11
  39.2 24.6 all-gather.15
  66.0 70.0 all-gather.7
  138.1 29.0 all-gather.9
  168.6 88.5 all-gather.13
  258.6 87.8 all-gather.17
  387.8 27.5 reduce-scatter.18
  560.1 64.7 reduce-scatter.16
  627.2 85.5 reduce-scatter.20
  714.9 87.0 reduce-scatter.22
  805.1 34.3 reduce-scatter.26
  842.6 36.7 reduce-scatter.24
  883.0 38.4 reduce-scatter.28
  924.9 36.7 reduce-scatter.30
where the time goes:
time: 979 us; the launch traced here: 971 us
  waiting for transfers between devices  394 us (40%)
  matrix products  259 us (26%)
  local copies, waits for them, and re-layouts  113 us (12%)
  blocking collectives  113 us (12%)
  other arithmetic  69.5 us (7%)
  between operations  20.5 us (2%)
    unnamed x18, waiting for transfers between devices  142 us
    reduce_scatter x1, waiting for transfers between devices, per_device(): lax.psum_scatter(grad_w_up.astype(jnp.bfloat16), 'gx', scatter_dimension=...  79.2 us
    unnamed x5, blocking collectives  76.1 us
    all_gather x1, waiting for transfers between devices, per_device(): lax.all_gather(by_cols[3], 'gx', axis=0, tiled=True)  46.9 us
    dynamic_slice x48, local copies, waits for them, and re-layouts, per_device(): lax.map(attend, (query_blocks, key_blocks, value_blocks, pair_lengths))  43.8 us
    all_gather x1, waiting for transfers between devices, per_device(): lax.all_gather(by_cols[0], 'gx', axis=0, tiled=True)  43.1 us
    dot_general x1, matrix products, per_device(): jnp.dot(normed_two_low, mat_up, preferred_element_type=jnp.float32) + vec_up  42.4 us
    dot_general x12, matrix products, block_scores(): jnp.einsum('qhd,khd->hqk', query_heads, key_heads, preferred_element_type...  35.3 us
  transfers between devices with their start and end apart: 14, of which 11 were waited for; matrix products, arithmetic and copies ran while one was open for 41% of the time, Pallas kernels for 0%

commit v1 on v0

v1 whole, which is shorter than its diff:
```python
import functools

import jax
import jax.numpy as jnp
from jax import lax
from jax.experimental import pallas as pl
from jax.experimental.pallas import tpu as pltpu
from jax.sharding import PartitionSpec as P

HEADS = 12
HEAD_DIM = 64
PAIR = 2 * HEAD_DIM
EPSILON = 1e-06
NEG_FILL = -1e30
BF = jnp.bfloat16
F32 = jnp.float32
AXES = ("gx", "gy")
BLOCKS = 8
AUX = 8
VMEM_BYTES = 60 << 20
MASKS_A = (0, 2, 4, 6, 1, 3, 5, 7)
MASKS_B = (0, 4, 2, 6, 1, 5, 3, 7)
ANY = pl.BlockSpec(memory_space=pl.ANY)


def nt(left, right):
    return lax.dot_general(left, right, (((1,), (1,)), ((), ())), preferred_element_type=F32)


def nn(left, right):
    return lax.dot_general(left, right, (((1,), (0,)), ((), ())), preferred_element_type=F32)


def tn(left, right):
    return lax.dot_general(left, right, (((0,), (0,)), ((), ())), preferred_element_type=F32)


def params(**extra):
    return pltpu.CompilerParams(vmem_limit_bytes=VMEM_BYTES, **extra)


def cost(flops, bytes_moved, transcendentals=0):
    return pl.CostEstimate(
        flops=int(flops), bytes_accessed=int(bytes_moved), transcendentals=int(transcendentals)
    )


def whole(shape):
    return pl.BlockSpec(shape, lambda *_: (0,) * len(shape))


def normalise(values):
    centre = values - jnp.mean(values, axis=-1, keepdims=True)
    spread = jnp.mean(centre * centre, axis=-1, keepdims=True)
    scale = lax.rsqrt(spread + EPSILON)
    return centre * scale, scale


def norm_back(grads, nhat, scale, gain):
    e = grads * gain
    return scale * (
        e
        - jnp.mean(e, axis=-1, keepdims=True)
        - nhat * jnp.mean(e * nhat, axis=-1, keepdims=True)
    )


def arrange_qkv_kernel(pos, *refs):
    pieces, (first_ref, second_ref), stacked = refs[:4], refs[4:6], refs[6]
    width, columns = first_ref.shape[1], pieces[0].shape[1]
    rows = width // 4
    vec_rows = []
    for k in range(4):
        place = pos[0] ^ k
        stacked[pl.ds(pl.multiple_of(place * rows, 8), rows), :] = pieces[k][0:rows, :].astype(F32)
        vec_rows.append(pieces[k][rows : rows + 1, :].astype(F32))
    turned = stacked[...].T.astype(BF)
    half = columns // 2
    first_ref[0:half, :] = turned[0:half]
    second_ref[0:half, :] = turned[half:columns]
    vec = jnp.concatenate(vec_rows, axis=0).astype(BF)
    lane = lax.broadcasted_iota(jnp.int32, (columns, width), 1)
    source = lax.broadcasted_iota(jnp.int32, (columns, width), 0)
    lane4 = lax.broadcasted_iota(jnp.int32, (4, width), 1)
    order = lax.broadcasted_iota(jnp.int32, (4, 1), 0)
    piece = width // (4 * BLOCKS)
    device = (pos[0] ^ order) * BLOCKS + pos[1]
    rows_out = []
    for j in range(8):
        pick = (source == piece * j + lane % piece).astype(BF)
        spread = nn(vec, pick)
        rows_out.append(
            jnp.sum(jnp.where(lane4 // piece == device, spread, 0.0), axis=0, keepdims=True)
        )
    first_ref[half : half + AUX, :] = jnp.concatenate(rows_out, axis=0).astype(BF)
    pick = (source == piece * 8 + lane % (4 * piece)).astype(BF)
    spread = jnp.where(lane4 // (4 * piece) == pos[1], nn(vec, pick), 0.0)
    rows_up = []
    for row in range(4):
        rows_up.append(
            jnp.sum(jnp.where((pos[0] ^ order) == row, spread, 0.0), axis=0, keepdims=True)
        )
    rows_up.append(jnp.zeros((AUX - 4, width), F32))
    second_ref[half : half + AUX, :] = jnp.concatenate(rows_up, axis=0).astype(BF)


def arrange_qkv(pos, pieces, width):
    rows, columns = pieces[0].shape
    out = jax.ShapeDtypeStruct((columns // 2 + AUX, width), BF)
    return pl.pallas_call(
        arrange_qkv_kernel,
        grid_spec=pltpu.PrefetchScalarGridSpec(
            num_scalar_prefetch=1,
            grid=(1,),
            in_specs=[whole((rows, columns))] * 4,
            out_specs=[whole(out.shape)] * 2,
            scratch_shapes=[pltpu.VMEM((width, columns), F32)],
        ),
        out_shape=[out, out],
        compiler_params=params(),
        cost_estimate=cost(4e6, 4 * rows * columns * 2 * 2),
        name="arrange_qkv",
    )(pos, *pieces)


def arrange_rest_kernel(pos, *refs):
    pieces, (first_ref, second_ref), up_all, out_all = refs[:4], refs[4:6], refs[6], refs[7]
    width = first_ref.shape[1]
    rows = width // 4
    wide, narrow = up_all.shape[1], out_all.shape[1]
    for k in range(4):
        place = pos[0] ^ k
        start = pl.multiple_of(place * rows, 8)
        up_all[pl.ds(start, rows), :] = pieces[k][:, 0:wide].astype(F32)
        out_all[pl.ds(start, rows), :] = pieces[k][:, 2 * wide : 2 * wide + narrow].astype(F32)
        down = pieces[k][:, wide : 2 * wide]
        at = pl.multiple_of(narrow // 2 + place * narrow, 16)
        second_ref[pl.ds(at, narrow), 0 : width // 2] = down[0:narrow]
        second_ref[pl.ds(at, narrow), width // 2 : width] = down[narrow : 2 * narrow]
    first_ref[0:wide, :] = up_all[...].T.astype(BF)
    turned = out_all[...].T.astype(BF)
    first_ref[wide : wide + narrow // 2, :] = turned[0 : narrow // 2]
    second_ref[0 : narrow // 2, :] = turned[narrow // 2 : narrow]


def arrange_rest(pos, pieces, width, wide, narrow):
    out = jax.ShapeDtypeStruct((wide + narrow // 2, width), BF)
    return pl.pallas_call(
        arrange_rest_kernel,
        grid_spec=pltpu.PrefetchScalarGridSpec(
            num_scalar_prefetch=1,
            grid=(1,),
            in_specs=[whole(pieces[0].shape)] * 4,
            out_specs=[whole(out.shape)] * 2,
            scratch_shapes=[pltpu.VMEM((width, wide), F32), pltpu.VMEM((width, narrow), F32)],
        ),
        out_shape=[out, out],
        compiler_params=params(),
        cost_estimate=cost(1e6, out.shape[0] * width * 2 * 4),
        name="arrange_rest",
    )(pos, *pieces)


def qkv_copies(table, halves, weights, sems):
    step = weights.shape[0] // (2 * BLOCKS)
    copies = []
    for j in range(2 * BLOCKS):
        source = halves[j // 2]
        size = source.shape[0] // 2
        copies.append(
            pltpu.make_async_copy(
                source.at[pl.ds((j % 2) * size, step)],
                weights.at[pl.ds(pl.multiple_of(table[j] * step, 16), step)],
                sems.at[j],
            )
        )
    return copies


def project_kernel(table, x_ref, *refs):
    halves, (proj_ref, normed_ref, vec_ref), (weights, aux, sems) = refs[:8], refs[8:11], refs[11:]
    j = pl.program_id(0)
    half = weights.shape[0] // (2 * BLOCKS)
    tile = proj_ref.shape[1]
    width = x_ref.shape[1]

    @pl.when(j == 0)
    def _():
        small = []
        for i in range(2 * BLOCKS):
            source = halves[i // 2]
            size = source.shape[0] // 2
            small.append(
                pltpu.make_async_copy(
                    source.at[pl.ds((i % 2) * size + half, AUX)],
                    aux.at[i],
                    sems.at[2 * BLOCKS + i],
                )
            )
        large = qkv_copies(table, halves, weights, sems)
        for copy in small + large:
            copy.start()
        nhat, _ = normalise(x_ref[...].astype(F32))
        for copy in small:
            copy.wait()
        vec_ref[0:AUX, :] = jnp.sum(aux[0:BLOCKS].astype(F32), axis=0)
        vec_ref[AUX : 2 * AUX, :] = jnp.sum(aux[BLOCKS : 2 * BLOCKS].astype(F32), axis=0)
        normed_ref[...] = (nhat * vec_ref[4:5, :] + vec_ref[5:6, :]).astype(BF)
        for copy in large:
            copy.wait()

    per = width // tile
    start = pl.multiple_of(j * tile, tile)
    lanes = pl.ds(pl.multiple_of(lax.rem(j, per) * tile, tile), tile)
    section = j // per
    bias = jnp.where(
        section == 0, vec_ref[0:1, lanes], jnp.where(section == 2, vec_ref[1:2, lanes], 0.0)
    )
    proj_ref[...] = (nt(normed_ref[...], weights[pl.ds(start, tile), :]) + bias).astype(BF)


def project(table, x, halves, tile=256):
    slots, width = x.shape
    columns = 3 * width
    return pl.pallas_call(
        project_kernel,
        grid_spec=pltpu.PrefetchScalarGridSpec(
            num_scalar_prefetch=1,
            grid=(columns // tile,),
            in_specs=[whole((slots, width))] + [ANY] * 8,
            out_specs=[
                pl.BlockSpec((slots, tile), lambda j, _: (0, j)),
                whole((slots, width)),
                whole((2 * AUX, width)),
            ],
            scratch_shapes=[
                pltpu.VMEM((columns, width), BF),
                pltpu.VMEM((2 * BLOCKS, AUX, width), BF),
                pltpu.SemaphoreType.DMA((4 * BLOCKS,)),
            ],
        ),
        out_shape=[
            jax.ShapeDtypeStruct((slots, columns), BF),
            jax.ShapeDtypeStruct((slots, width), BF),
            jax.ShapeDtypeStruct((2 * AUX, width), F32),
        ],
        compiler_params=params(),
        cost_estimate=cost(2 * slots * width * columns, slots * width * 10),
        name="project",
    )(table, x, *halves)


def attend_kernel(len_ref, q_ref, k_ref, v_ref, o_ref, lse_ref, qp, *, slots, padded):
    length = len_ref[0]
    lane = lax.broadcasted_iota(jnp.int32, (slots, PAIR), 1)
    row = lax.broadcasted_iota(jnp.int32, (slots, PAIR), 0)
    bias = jnp.where(row < length, 0.0, NEG_FILL)
    keys = k_ref[...].astype(F32)
    values = v_ref[...].astype(F32)
    queries = q_ref[...].astype(F32) * HEAD_DIM**-0.5
    outs = []
    for h in range(2):
        mine = (lane // HEAD_DIM) == h
        spare = (1 - h) * HEAD_DIM
        flag = lane == spare
        key_ext = jnp.where(mine, keys, jnp.where(flag, bias, 0.0)).astype(BF)
        value_ext = jnp.where(mine, values, jnp.where(flag, 1.0, 0.0)).astype(BF)
        qp[h, 0:slots, :] = jnp.where(mine, queries, jnp.where(flag, 1.0, 0.0)).astype(BF)
        if padded > slots:
            qp[h, slots:padded, :] = jnp.zeros((padded - slots, PAIR), BF)
        scores = nt(key_ext, qp[h])
        top = jnp.max(scores, axis=0, keepdims=True)
        weights = jnp.exp(scores - top).astype(BF)
        mixed = nn(value_ext.T, weights)
        total = mixed[spare : spare + 1, :]
        outs.append(mixed[h * HEAD_DIM : (h + 1) * HEAD_DIM, :] / total)
        lse_ref[0, h : h + 1, :] = top + jnp.log(total)
    o_ref[...] = jnp.concatenate(outs, axis=0).T[0:slots].astype(BF)


def attend(length, proj):
    slots = proj.shape[0]
    padded = -(-slots // 128) * 128
    width = proj.shape[1] // 3
    pairs = width // PAIR

    def spec(off):
        return pl.BlockSpec((slots, PAIR), lambda p, _: (0, off + p))

    return pl.pallas_call(
        functools.partial(attend_kernel, slots=slots, padded=padded),
        grid_spec=pltpu.PrefetchScalarGridSpec(
            num_scalar_prefetch=1,
            grid=(pairs,),
            in_specs=[spec(0), spec(pairs), spec(2 * pairs)],
            out_specs=[spec(0), pl.BlockSpec((1, 8, padded), lambda p, _: (p, 0, 0))],
            scratch_shapes=[pltpu.VMEM((2, padded, PAIR), BF)],
        ),
        out_shape=[
            jax.ShapeDtypeStruct((slots, width), BF),
            jax.ShapeDtypeStruct((pairs, 8, padded), F32),
        ],
        compiler_params=params(),
        cost_estimate=cost(
            2 * pairs * 8 * slots * slots * PAIR, slots * width * 8, 2 * pairs * slots * slots
        ),
        name="attend",
    )(length, proj, proj, proj)


def parts(values):
    high = values.astype(BF).astype(F32)
    rest = values - high
    mid = rest.astype(BF).astype(F32)
    return high, mid, (rest - mid).astype(BF).astype(F32)


def attend_back_kernel(
    len_ref,
    q_ref,
    k_ref,
    v_ref,
    g_ref,
    o_ref,
    lse_ref,
    dq_ref,
    dk_ref,
    dv_ref,
    qp,
    gp,
    *,
    slots,
    padded,
    tile,
):
    length = len_ref[0]
    lane = lax.broadcasted_iota(jnp.int32, (slots, PAIR), 1)
    row = lax.broadcasted_iota(jnp.int32, (slots, PAIR), 0)
    bias = jnp.where(row < length, 0.0, NEG_FILL)
    keys = k_ref[...].astype(F32)
    values = v_ref[...].astype(F32)
    queries = q_ref[...].astype(F32) * HEAD_DIM**-0.5
    grads = g_ref[...].astype(F32)
    products = grads * o_ref[...].astype(F32)
    d_queries, d_keys, d_values = [], [], []
    for h in range(2):
        mine = (lane // HEAD_DIM) == h
        spare = (1 - h) * HEAD_DIM
        flag = lane == spare
        dots = jnp.sum(jnp.where(mine, products, 0.0), axis=1, keepdims=True)
        high, mid, low = parts(-dots)
        ones = (lane >= spare) & (lane < spare + 3)
        value_ext = jnp.where(mine, values, jnp.where(ones, 1.0, 0.0)).astype(BF)
        tail = jnp.where(
            flag, high, jnp.where(lane == spare + 1, mid, jnp.where(lane == spare + 2, low, 0.0))
        )
        gp[h, 0:slots, :] = jnp.where(mine, grads, tail).astype(BF)
        key_ext = jnp.where(mine, keys, jnp.where(flag, bias, 0.0)).astype(BF)
        qp[h, 0:slots, :] = jnp.where(mine, queries, jnp.where(flag, 1.0, 0.0)).astype(BF)
        if padded > slots:
            gp[h, slots:padded, :] = jnp.zeros((padded - slots, PAIR), BF)
            qp[h, slots:padded, :] = jnp.zeros((padded - slots, PAIR), BF)
        keys_turned = key_ext.T[h * HEAD_DIM : (h + 1) * HEAD_DIM]
        d_key = d_value = None
        d_query = []
        for j in range(padded // tile):
            at = slice(j * tile, (j + 1) * tile)
            weights = jnp.exp(nt(key_ext, qp[h, at, :]) - lse_ref[0, h : h + 1, at])
            d_scores = (weights * nt(value_ext, gp[h, at, :])).astype(BF)
            more_value = nn(weights.astype(BF), gp[h, at, :])
            more_key = nn(d_scores, qp[h, at, :])
            d_value = more_value if d_value is None else d_value + more_value
            d_key = more_key if d_key is None else d_key + more_key
            d_query.append(nn(keys_turned, d_scores))
        d_queries.append(jnp.concatenate(d_query, axis=1))
        d_keys.append(d_key)
        d_values.append(d_value)
    turned = jnp.concatenate(d_queries, axis=0) * HEAD_DIM**-0.5
    dq_ref[...] = turned.T[0:slots].astype(BF)
    dk_ref[...] = jnp.where(lane < HEAD_DIM, d_keys[0], d_keys[1]).astype(BF)
    dv_ref[...] = jnp.where(lane < HEAD_DIM, d_values[0], d_values[1]).astype(BF)


def attend_back(length, proj, grads, mixed, totals, tile=256, first=0, count=None):
    slots = proj.shape[0]
    padded = -(-slots // 128) * 128
    width = proj.shape[1] // 3
    pairs = width // PAIR
    count = pairs if count is None else count

    def spec(off):
        return pl.BlockSpec((slots, PAIR), lambda p, _: (0, off + p))

    return pl.pallas_call(
        functools.partial(attend_back_kernel, slots=slots, padded=padded, tile=tile),
        grid_spec=pltpu.PrefetchScalarGridSpec(
            num_scalar_prefetch=1,
            grid=(count,),
            in_specs=[
                spec(first),
                spec(first + pairs),
                spec(first + 2 * pairs),
                spec(first),
                spec(first),
                pl.BlockSpec((1, 8, padded), lambda p, _: (first + p, 0, 0)),
            ],
            out_specs=[spec(0)] * 3,
            scratch_shapes=[pltpu.VMEM((2, padded, PAIR), BF)] * 2,
        ),
        out_shape=[jax.ShapeDtypeStruct((slots, count * PAIR), BF)] * 3,
        compiler_params=params(),
        cost_estimate=cost(
            2 * count * 20 * slots * slots * PAIR, slots * width * 16, 2 * count * slots * slots
        ),
        name="attend_back",
    )(length, proj, proj, proj, grads, mixed, totals)


def rest_copies(table, halves, w_out, w_up, w_down, sems):
    width = w_out.shape[0]
    narrow = width // BLOCKS
    wide = w_up.shape[0] // BLOCKS
    half = narrow // 2
    copies_out, copies_up, copies_down = [], [], []
    for j in range(2 * BLOCKS):
        source = halves[j // 2]
        size = source.shape[0] // 2
        base = (j % 2) * size
        block = table[j] // 2
        if j < BLOCKS:
            copies_up.append(
                pltpu.make_async_copy(
                    source.at[pl.ds(base, wide)],
                    w_up.at[pl.ds(pl.multiple_of(block * wide, 16), wide)],
                    sems.at[j],
                )
            )
            copies_out.append(
                pltpu.make_async_copy(
                    source.at[pl.ds(base + wide, half)],
                    w_out.at[pl.ds(pl.multiple_of(block * narrow, 16), half)],
                    sems.at[BLOCKS + j],
                )
            )
        else:
            copies_out.append(
                pltpu.make_async_copy(
                    source.at[pl.ds(base, half)],
                    w_out.at[pl.ds(pl.multiple_of(block * narrow + half, 16), half)],
                    sems.at[BLOCKS + j],
                )
            )
            for q in range(4):
                copies_down.append(
                    pltpu.make_async_copy(
                        source.at[pl.ds(base + half + q * narrow, narrow)],
                        w_down.at[
                            pl.ds(pl.multiple_of(block * narrow, 16), narrow),
                            pl.ds(q * width, width),
                        ],
                        sems.at[3 * BLOCKS + (j - BLOCKS) * 4 + q],
                    )
                )
    return copies_out, copies_up, copies_down


def middle_kernel(len_ref, table, x_ref, mixed_ref, cot_ref, vec_ref, *refs, chunk):
    halves = refs[:8]
    (
        out_ref,
        active_ref,
        d_inner_ref,
        normed_ref,
        d_resid_ref,
        d_branch_ref,
        d_mixed_ref,
        sums_ref,
    ) = refs[8:16]
    w_out, w_up, w_down, sems = refs[16:]
    i = pl.program_id(0)
    tile, width = x_ref.shape
    hidden = w_up.shape[0]

    copies_out, copies_up, copies_down = rest_copies(table, halves, w_out, w_up, w_down, sems)

    @pl.when(i == 0)
    def _():
        for copy in copies_out + copies_up + copies_down:
            copy.start()
        sums_ref[...] = jnp.zeros_like(sums_ref)
        for copy in copies_out:
            copy.wait()

    residual = x_ref[...].astype(F32) + nt(mixed_ref[...], w_out[...]) + vec_ref[2:3, :]
    nhat, scale = normalise(residual)
    normed = (nhat * vec_ref[6:7, :] + vec_ref[7:8, :]).astype(BF)
    normed_ref[...] = normed
    rows = lax.broadcasted_iota(jnp.int32, (tile, 1), 0) + i * tile
    seed_low = jnp.where(rows < len_ref[0], cot_ref[...], jnp.zeros_like(cot_ref))
    seed = seed_low.astype(F32)
    ones = jnp.ones((8, tile), BF)

    @pl.when(i == 0)
    def _():
        for copy in copies_up + copies_down:
            copy.wait()

    per = width // chunk

    def step(c, carry):
        out_sum, d_normed = carry
        at = pl.ds(pl.multiple_of(c * chunk, chunk), chunk)
        row = pl.ds(8 + c // per, 1)
        lanes = pl.ds(pl.multiple_of(lax.rem(c, per) * chunk, chunk), chunk)
        inner = nt(normed, w_up[at, :]) + vec_ref[row, lanes]
        cdf = 0.5 + 0.5 * lax.erf(inner * 0.5**0.5)
        active = (inner * cdf).astype(BF)
        active_ref[:, at] = active
        d_active = nn(seed_low, w_down[:, at])
        slope = cdf + inner * (jnp.exp(-0.5 * inner * inner) * 0.3989422804014327)
        d_inner = (d_active * slope).astype(BF)
        d_inner_ref[:, at] = d_inner
        sums_ref[row, lanes] += nn(ones, d_inner)[0:1]
        return (out_sum + nt(active, w_down[:, at]), d_normed + nn(d_inner, w_up[at, :]))

    zero = jnp.zeros((tile, width), F32)
    out_sum, d_normed = lax.fori_loop(0, hidden // chunk, step, (zero, zero))
    out_ref[...] = (residual + out_sum + vec_ref[3:4, :]).astype(BF)
    d_resid = seed + norm_back(d_normed, nhat, scale, vec_ref[6:7, :])
    d_resid_ref[...] = d_resid
    d_branch = d_resid.astype(BF)
    d_branch_ref[...] = d_branch
    d_mixed_ref[...] = nn(d_branch, w_out[...]).astype(BF)
    sums_ref[2:3, :] += jnp.sum(d_resid, axis=0, keepdims=True)
    sums_ref[3:4, :] += jnp.sum(seed, axis=0, keepdims=True)
    sums_ref[6:7, :] += jnp.sum(d_normed * nhat, axis=0, keepdims=True)
    sums_ref[7:8, :] += jnp.sum(d_normed, axis=0, keepdims=True)


def middle(length, table, x, mixed, cot, vec, halves, hidden, tile, chunk=768):
    slots, width = x.shape

    def rows(columns):
        return pl.BlockSpec((tile, columns), lambda i, *_: (i, 0))

    return pl.pallas_call(
        functools.partial(middle_kernel, chunk=chunk),
        grid_spec=pltpu.PrefetchScalarGridSpec(
            num_scalar_prefetch=2,
            grid=(slots // tile,),
            in_specs=[rows(width)] * 3 + [whole(vec.shape)] + [ANY] * 8,
            out_specs=[
                rows(width),
                rows(hidden),
                rows(hidden),
                rows(width),
                rows(width),
                rows(width),
                rows(width),
                whole(vec.shape),
            ],
            scratch_shapes=[
                pltpu.VMEM((width, width), BF),
                pltpu.VMEM((hidden, width), BF),
                pltpu.VMEM((width, hidden), BF),
                pltpu.SemaphoreType.DMA((7 * BLOCKS,)),
            ],
        ),
        out_shape=[
            jax.ShapeDtypeStruct((slots, width), BF),
            jax.ShapeDtypeStruct((slots, hidden), BF),
            jax.ShapeDtypeStruct((slots, hidden), BF),
            jax.ShapeDtypeStruct((slots, width), BF),
            jax.ShapeDtypeStruct((slots, width), F32),
            jax.ShapeDtypeStruct((slots, width), BF),
            jax.ShapeDtypeStruct((slots, width), BF),
            jax.ShapeDtypeStruct(vec.shape, F32),
        ],
        compiler_params=params(),
        cost_estimate=cost(
            2 * slots * width * (4 * hidden + 2 * width),
            slots * (hidden * 4 + width * 18) + hidden * width * 4,
            2 * slots * hidden,
        ),
        name="middle",
    )(length, table, x, mixed, cot, vec, *halves)


def rest_grads_kernel(
    len_ref,
    table,
    active_ref,
    d_inner_ref,
    normed_ref,
    cot_ref,
    d_branch_ref,
    mixed_ref,
    keep_ref,
    send_ref,
    sums,
    sems,
):
    z = pl.program_id(0)
    slots, width = normed_ref.shape
    narrow = width // BLOCKS
    wide = sums.shape[1] // 2 - narrow // 2
    rows = lax.broadcasted_iota(jnp.int32, (slots, 1), 0)
    seed = jnp.where(rows < len_ref[0], cot_ref[...], jnp.zeros_like(cot_ref))
    up = tn(d_inner_ref[...], normed_ref[...]).astype(BF)
    per = width // wide
    for j in range(per):
        sums[z * per + j, 0:wide, :] = up[j * wide : (j + 1) * wide]
    down = tn(seed, active_ref[...]).astype(BF)
    at = pl.ds(pl.multiple_of(wide + narrow + z * narrow, 16), narrow)
    for g in range(BLOCKS):
        sums[g, at, :] = down[g * narrow : (g + 1) * narrow]

    @pl.when(z == 0)
    def _():
        out = tn(d_branch_ref[...], mixed_ref[...]).astype(BF)
        for g in range(BLOCKS):
            sums[g, wide : wide + narrow, :] = out[g * narrow : (g + 1) * narrow]

    @pl.when(z == pl.num_programs(0) - 1)
    def _():
        copies = []
        for j in range(BLOCKS):
            target = keep_ref if j < BLOCKS // 2 else send_ref
            copies.append(
                pltpu.make_async_copy(
                    sums.at[table[j] // 2], target.at[j % (BLOCKS // 2)], sems.at[j]
                )
            )
        for copy in copies:
            copy.start()
        for copy in copies:
            copy.wait()


def rest_grads(length, table, active, d_inner, normed, cot, d_branch, mixed):
    slots, width = normed.shape
    hidden = active.shape[1]
    rows = 2 * (hidden // BLOCKS) + width // BLOCKS
    out = jax.ShapeDtypeStruct((BLOCKS // 2, rows, width), BF)
    return pl.pallas_call(
        rest_grads_kernel,
        grid_spec=pltpu.PrefetchScalarGridSpec(
            num_scalar_prefetch=2,
            grid=(hidden // width,),
            in_specs=[pl.BlockSpec((slots, width), lambda z, *_: (0, z))] * 2
            + [whole((slots, width))] * 4,
            out_specs=[ANY] * 2,
            scratch_shapes=[
                pltpu.VMEM((BLOCKS, rows, width), BF),
                pltpu.SemaphoreType.DMA((BLOCKS,)),
            ],
        ),
        out_shape=[out, out],
        compiler_params=params(),
        cost_estimate=cost(
            2 * slots * width * (2 * hidden + width), slots * hidden * 4 + out.size * 4
        ),
        name="rest_grads",
    )(length, table, active, d_inner, normed, cot, d_branch, mixed)


def qkv_grads_kernel(table, dq_ref, dk_ref, dv_ref, normed_ref, keep_ref, send_ref, sums, sems):
    width = normed_ref.shape[1]
    block = sums.shape[0] // BLOCKS
    for s, ref in enumerate((dq_ref, dk_ref, dv_ref)):
        sums[s * width : (s + 1) * width, :] = tn(ref[...], normed_ref[...]).astype(BF)
    copies = []
    for j in range(BLOCKS):
        target = keep_ref if j < BLOCKS // 2 else send_ref
        at = pl.ds(pl.multiple_of(table[j] // 2 * block, 16), block)
        copies.append(
            pltpu.make_async_copy(sums.at[at], target.at[j % (BLOCKS // 2)], sems.at[j])
        )
    for copy in copies:
        copy.start()
    for copy in copies:
        copy.wait()


def qkv_grads(table, d_parts, normed):
    slots, width = normed.shape
    out = jax.ShapeDtypeStruct((BLOCKS // 2, 3 * width // BLOCKS, width), BF)
    return pl.pallas_call(
        qkv_grads_kernel,
        grid_spec=pltpu.PrefetchScalarGridSpec(
            num_scalar_prefetch=1,
            grid=(1,),
            in_specs=[whole((slots, width))] * 4,
            out_specs=[ANY] * 2,
            scratch_shapes=[
                pltpu.VMEM((3 * width, width), BF),
                pltpu.SemaphoreType.DMA((BLOCKS,)),
            ],
        ),
        out_shape=[out, out],
        compiler_params=params(),
        cost_estimate=cost(6 * slots * width * width, slots * width * 8 + out.size * 4),
        name="qkv_grads",
    )(table, *d_parts, normed)


def last_kernel(
    table, dq_ref, dk_ref, dv_ref, x_ref, d_resid_ref, vec_ref, sums_in, *refs
):
    halves, (grad_ref, sums_ref), (weights, sems) = refs[:8], refs[8:10], refs[10:]
    i = pl.program_id(0)
    tile, width = x_ref.shape
    copies = qkv_copies(table, halves, weights, sems)

    @pl.when(i == 0)
    def _():
        for copy in copies:
            copy.start()
        sums_ref[...] = sums_in[...]
        for copy in copies:
            copy.wait()

    d_normed = nn(dq_ref[...], weights[0:width, :])
    d_normed += nn(dk_ref[...], weights[width : 2 * width, :])
    d_normed += nn(dv_ref[...], weights[2 * width : 3 * width, :])
    nhat, scale = normalise(x_ref[...].astype(F32))
    grad_ref[...] = d_resid_ref[...] + norm_back(d_normed, nhat, scale, vec_ref[4:5, :])
    ones = jnp.ones((8, tile), BF)
    sums_ref[0:1, :] += nn(ones, dq_ref[...])[0:1]
    sums_ref[1:2, :] += nn(ones, dv_ref[...])[0:1]
    sums_ref[4:5, :] += jnp.sum(d_normed * nhat, axis=0, keepdims=True)
    sums_ref[5:6, :] += jnp.sum(d_normed, axis=0, keepdims=True)


def last(table, d_parts, x, d_resid, vec, sums, halves, tile):
    slots, width = x.shape
    rows = pl.BlockSpec((tile, width), lambda i, _: (i, 0))
    return pl.pallas_call(
        last_kernel,
        grid_spec=pltpu.PrefetchScalarGridSpec(
            num_scalar_prefetch=1,
            grid=(slots // tile,),
            in_specs=[rows] * 5 + [whole(vec.shape)] * 2 + [ANY] * 8,
            out_specs=[rows, whole(vec.shape)],
            scratch_shapes=[
                pltpu.VMEM((3 * width, width), BF),
                pltpu.SemaphoreType.DMA((2 * BLOCKS,)),
            ],
        ),
        out_shape=[
            jax.ShapeDtypeStruct((slots, width), F32),
            jax.ShapeDtypeStruct(vec.shape, F32),
        ],
        compiler_params=params(),
        cost_estimate=cost(6 * slots * width * width, slots * width * 16),
        name="last",
    )(table, *d_parts, x, d_resid, vec, sums, *halves)


def swap(values, axis, mask, size):
    return lax.ppermute(values, axis, [(i, i ^ mask) for i in range(size)])


def gather_planes(message):
    return [message] + [swap(message, "gx", k, 4) for k in (1, 2, 3)]


def gather_blocks(first, second):
    from_x = swap(first, "gy", 2, BLOCKS)
    from_y = swap(second, "gy", 4, BLOCKS)
    a = jnp.concatenate([first, from_x], axis=0)
    b = jnp.concatenate([second, from_y], axis=0)
    a_y = swap(a, "gy", 4, BLOCKS)
    b_x = swap(b, "gy", 2, BLOCKS)
    a_c, b_c = swap(a, "gy", 1, BLOCKS), swap(b, "gy", 1, BLOCKS)
    a_yc, b_xc = swap(a_y, "gy", 1, BLOCKS), swap(b_x, "gy", 1, BLOCKS)
    return [a, a_y, a_c, a_yc, b, b_x, b_c, b_xc]


def add(left, right):
    return left.astype(F32) + right.astype(F32)


def scatter_blocks(keep, send):
    rows = keep.shape[1]
    half = rows // 2
    other = swap(send, "gy", 1, BLOCKS)

    def total(index, at):
        return add(keep[index, at], other[index, at]).astype(BF)

    top, bottom = slice(0, half), slice(half, rows)
    a_send = jnp.stack([total(2, top), total(3, top)])
    b_send = jnp.stack([total(1, bottom), total(3, bottom)])
    a_got = swap(a_send, "gy", 4, BLOCKS)
    b_got = swap(b_send, "gy", 2, BLOCKS)
    a_next = add(total(1, top), a_got[1]).astype(BF)
    b_next = add(total(2, bottom), b_got[1]).astype(BF)
    a_last = swap(a_next, "gy", 2, BLOCKS)
    b_last = swap(b_next, "gy", 4, BLOCKS)
    a = add(add(total(0, top), a_got[0]), a_last)
    b = add(add(total(0, bottom), b_got[0]), b_last)
    return jnp.concatenate([a, b], axis=0)


def scatter_planes(stacked):
    z = lax.axis_index("gx")
    mine = lax.dynamic_index_in_dim(stacked, z, 0, keepdims=False)
    low = stacked.astype(BF)
    total = mine.astype(F32)
    for k in (1, 2, 3):
        piece = lax.dynamic_index_in_dim(low, z ^ k, 0, keepdims=False)
        total = total + swap(piece, "gx", k, 4).astype(F32)
    return total


def per_device(
    patches,
    lengths,
    cotangent,
    w_qkv,
    w_out,
    w_up,
    w_down,
    bias_q,
    bias_v,
    bias_o,
    bias_up,
    bias_down,
    gain_one,
    shift_one,
    gain_two,
    shift_two,
    *,
    planes,
    columns,
):
    slots, width = patches.shape
    hidden = w_up.shape[1] * columns
    wide, narrow = hidden // BLOCKS, width // BLOCKS
    tile = slots // 3
    z, g = lax.axis_index("gx"), lax.axis_index("gy")
    fast = planes == 4 and columns == BLOCKS
    vectors = (bias_q, bias_v, bias_o, bias_down, gain_one, shift_one, gain_two, shift_two)
    if fast:
        pos = jnp.stack([z, g]).astype(jnp.int32)
        table = jnp.concatenate(
            [2 * (g ^ jnp.array(MASKS_A)), 2 * (g ^ jnp.array(MASKS_B)) + 1]
        ).astype(jnp.int32)
        grad_table = (2 * (g ^ jnp.array(MASKS_A))).astype(jnp.int32)
        vec_row = jnp.concatenate(vectors + (bias_up,))[None, :]
        message = jnp.concatenate(
            [w_qkv, vec_row, jnp.zeros((AUX - 1, w_qkv.shape[1]), BF)], axis=0
        )
        pieces = gather_planes(message)
        qkv_halves = gather_blocks(*arrange_qkv(pos, pieces, width))
        turned = w_down.T
        down = jnp.concatenate([turned[:, : width // 2], turned[:, width // 2 :]], axis=0)
        message = jnp.concatenate(
            [w_up, down, w_out, jnp.zeros((width // 4, 128 - narrow), BF)], axis=1
        )
        message, pieces[1] = lax.optimization_barrier((message, pieces[1]))
        pieces = gather_planes(message)
        rest_halves = gather_blocks(*arrange_rest(pos, pieces, width, wide, narrow))
    else:

        def everything(shard):
            return lax.all_gather(
                lax.all_gather(shard, "gx", axis=0, tiled=True), "gy", axis=1, tiled=True
            ).T

        table = jnp.concatenate([2 * jnp.arange(BLOCKS), 2 * jnp.arange(BLOCKS) + 1]).astype(
            jnp.int32
        )
        grad_table = (2 * jnp.arange(BLOCKS)).astype(jnp.int32)
        rows = jnp.stack([lax.all_gather(v, AXES, axis=0, tiled=True) for v in vectors])
        up_rows = lax.all_gather(bias_up, AXES, axis=0, tiled=True).reshape(4, width)
        up_rows = jnp.concatenate([up_rows, jnp.zeros((AUX - 4, width), BF)])
        qkv = everything(w_qkv).reshape(BLOCKS, 2, -1, width)

        def with_aux(blocks, aux):
            rest = jnp.zeros((BLOCKS - 1, AUX, width), BF)
            both = jnp.concatenate([blocks, jnp.concatenate([aux[None], rest])], axis=1)
            return list(both.reshape(4, -1, width))

        qkv_halves = with_aux(qkv[:, 0], rows) + with_aux(qkv[:, 1], up_rows)
        down = everything(w_down).reshape(BLOCKS, narrow, 4, width)
        down = jnp.transpose(down, (0, 2, 1, 3)).reshape(BLOCKS, wide, width)
        rest = jnp.concatenate(
            [
                everything(w_up).reshape(BLOCKS, wide, width),
                everything(w_out).reshape(BLOCKS, narrow, width),
                down,
            ],
            axis=1,
        ).reshape(BLOCKS, 2, -1, width)
        rest_halves = list(rest[:, 0].reshape(4, -1, width)) + list(
            rest[:, 1].reshape(4, -1, width)
        )

    proj, normed, vec = project(table, patches, qkv_halves)
    mixed, totals = attend(lengths, proj)
    out_rows, active, d_inner, normed_two, d_resid, d_branch, d_mixed, sums = middle(
        lengths, table, patches, mixed, cotangent, vec, rest_halves, hidden, tile
    )
    rest_keep, rest_send = rest_grads(
        lengths, grad_table, active, d_inner, normed_two, cotangent, d_branch, mixed
    )
    d_parts = attend_back(lengths, proj, d_mixed, mixed, totals)
    qkv_keep, qkv_send = qkv_grads(grad_table, d_parts, normed)
    grad_rows, sums = last(table, d_parts, patches, d_resid, vec, sums, qkv_halves, tile)

    if fast:
        rest = scatter_blocks(rest_keep, rest_send)
        up = rest[:wide].T.reshape(4, width // 4, wide)
        out = rest[wide : wide + narrow].T.reshape(4, width // 4, narrow)
        down = jnp.transpose(rest[wide + narrow :].reshape(4, narrow, width), (0, 2, 1))
        grad_up, grad_out, grad_down = scatter_planes(up), scatter_planes(out), scatter_planes(down)
        qkv = scatter_blocks(qkv_keep, qkv_send)
        grad_qkv = scatter_planes(qkv.T.reshape(4, width // 4, -1))
        for axis, mask, size in (
            ("gy", 1, 8),
            ("gy", 2, 8),
            ("gy", 4, 8),
            ("gx", 1, 4),
            ("gx", 2, 4),
        ):
            sums = sums + swap(sums, axis, mask, size)
        device = z * columns + g
        own = lax.dynamic_slice(sums, (0, device * (narrow // 4)), (8, narrow // 4))
        own_up = lax.dynamic_slice(sums, (8 + z, g * narrow), (1, narrow))[0]
        own = [own[j] for j in range(8)]
    else:

        def spread(grads, axis_size):
            low = grads.astype(BF)
            part = lax.psum_scatter(low, "gy", scatter_dimension=0, tiled=True)
            return lax.psum_scatter(part.T, "gx", scatter_dimension=0, tiled=True).astype(F32)

        rest = jnp.concatenate([rest_keep, rest_send], axis=0)
        grad_up = spread(rest[:, :wide].reshape(hidden, width), columns)
        grad_out = spread(rest[:, wide : wide + narrow].reshape(width, width), columns)
        down = rest[:, wide + narrow :].reshape(BLOCKS, 4, narrow, width)
        grad_down = spread(jnp.transpose(down, (0, 2, 1, 3)).reshape(width, hidden), columns)
        qkv = jnp.concatenate([qkv_keep, qkv_send], axis=0).reshape(3 * width, width)
        grad_qkv = spread(qkv, columns)

        def share(vector):
            return lax.psum_scatter(vector, AXES, scatter_dimension=0, tiled=True)

        own = [share(sums[j]) for j in range(8)]
        own_up = share(sums[8:12].reshape(hidden))

    return (
        out_rows,
        grad_rows,
        grad_qkv,
        grad_out,
        grad_up,
        grad_down,
        own[0],
        own[1],
        own[2],
        own_up,
        own[3],
        own[4],
        own[5],
        own[6],
        own[7],
    )


def solution(mesh):
    by_rows = P(AXES, None)
    by_parts = P(AXES)
    matrix = P("gx", "gy")
    in_specs = (by_rows, by_parts, by_rows) + (matrix,) * 4 + (by_parts,) * 9
    out_specs = (by_rows, by_rows) + (matrix,) * 4 + (by_parts,) * 9
    body = functools.partial(per_device, planes=mesh.shape["gx"], columns=mesh.shape["gy"])
    return jax.shard_map(body, mesh=mesh, in_specs=in_specs, out_specs=out_specs, check_vma=False)
```

time: 979 us -> 434 us (0.44)
  waiting for transfers between devices: 394 us -> 119 us
  matrix products: 259 us -> 0 us
  Pallas kernels: 0 us -> 199 us
  blocking collectives: 113 us -> 0 us
  local copies, waits for them, and re-layouts: 113 us -> 19.2 us
  starting transfers between devices: 0.78 us -> 61.2 us
  other arithmetic: 69.5 us -> 24.4 us
  between operations: 20.5 us -> 2.35 us
    dot_general x54 -> x0, matrix products: 259 us -> none  [the longest x1 42.4 us: per_device(): jnp.dot(normed_two_low, mat_up, preferred_element_type=jnp.float32) + vec_up]
    pallas_call x0 -> x9, Pallas kernels: none -> 199 us  [the longest x1 52.9 us: attend_back(): pl.pallas_call(functools.partial(attend_back_kernel, slots=slots, padded=...]
    unnamed x18 -> x0, waiting for transfers between devices: 142 us -> none
    reduce_scatter x4 -> x0, waiting for transfers between devices: 135 us -> none  [the longest x1 79.2 us: per_device(): lax.psum_scatter(grad_w_up.astype(jnp.bfloat16), 'gx', scatter_dimension=...]
    ppermute x0 -> x49, waiting for transfers between devices: none -> 119 us  [swap(): return lax.ppermute(values, axis, [(i, i ^ mask) for i in range(size)])]
    all_gather x6 -> x0, waiting for transfers between devices: 117 us -> none  [the longest x1 46.9 us: per_device(): lax.all_gather(by_cols[3], 'gx', axis=0, tiled=True)]
    unnamed x5 -> x0, blocking collectives: 76.1 us -> none
    ppermute x0 -> x49, starting transfers between devices: none -> 61.2 us  [swap(): return lax.ppermute(values, axis, [(i, i ^ mask) for i in range(size)])]
  transfers between devices with their start and end apart: 14 -> 49, of which waited for: 11 -> 17; matrix products, arithmetic and copies ran while one was open for 41% -> 6% of each run, Pallas kernels for 0% -> 29%
where the time goes in v1:
time: 434 us; the launch traced here: 425 us
  Pallas kernels  199 us (46%)
  waiting for transfers between devices  119 us (27%)
  starting transfers between devices  61.2 us (14%)
  other arithmetic  24.4 us (6%)
  local copies, waits for them, and re-layouts  19.2 us (4%)
    ppermute x49, waiting for transfers between devices, swap(): return lax.ppermute(values, axis, [(i, i ^ mask) for i in range(size)])  119 us
    ppermute x49, starting transfers between devices, swap(): return lax.ppermute(values, axis, [(i, i ^ mask) for i in range(size)])  61.2 us
    pallas_call x1, Pallas kernels, attend_back(): pl.pallas_call(functools.partial(attend_back_kernel, slots=slots, padded=...  52.9 us
    pallas_call x1, Pallas kernels, middle(): pl.pallas_call(functools.partial(middle_kernel, chunk=chunk), grid_spec=p...  50.9 us
    pallas_call x1, Pallas kernels, attend(): pl.pallas_call(functools.partial(attend_kernel, slots=slots, padded=padde...  27.6 us
    pallas_call x1, Pallas kernels, rest_grads(): pl.pallas_call(rest_grads_kernel, grid_spec=pltpu.PrefetchScalarGridSpec(...  24 us
    pallas_call x1, Pallas kernels, last(): pl.pallas_call(last_kernel, grid_spec=pltpu.PrefetchScalarGridSpec(num_sc...  13.6 us
    pallas_call x1, Pallas kernels, project(): pl.pallas_call(project_kernel, grid_spec=pltpu.PrefetchScalarGridSpec(num...  12.6 us
  transfers between devices with their start and end apart: 49, of which 17 were waited for; matrix products, arithmetic and copies ran while one was open for 6% of the time, Pallas kernels for 29%

profile of v1, /device:TPU:0, one launch (start us, length us, event | category | flops | bytes accessed | tf_op | source)
XLA Modules:
  0.0 425.1 jit_solution(8796301833827293746)
XLA Ops:
  0.6 6.1 %concatenate.34 = bf16[288]{0:T(512)(128)(2,1)S(1)} concatenate(bf16[24]{0:T(256)(128)(2,1)} %param.26, bf16[24]{0:T(256)(128)(2,1)} %param.27, bf16[24]{0:T(256)(128)(2,1)} %param.28, bf16[24]{0:T(256)(128)(2,1)} %param.30, bf16[24]{0:T(256)(128)(2,1)} %param.31, bf16[24]{0:T(256)(128)(2,1)} %param.32, bf16[24]{0:T(256)(128)(2,1)} %param.33, bf16[24]{0:T(256)(128)(2,1)} %param.34, ...), dimensions={0} | concatenate | bytes 1152 | tf_op jit(solution)/shard_map/concatenate | solution.py:851
  23.7 36.2 %collective-permute-done.1.refs_2_ = bf16[200,288]{1,0:T(8,128)(2,1)S(1)} collective-permute-done((bf16[200,288]{1,0:T(8,128)(2,1)S(1)}, bf16[200,288]{1,0:T(8,128)(2,1)S(1)}, u32[]{:S(2)}, u32[]{:S(2)}) %collective-permute-start.1) | collective-permute-done | bytes 115232 | tf_op jit(solution)/shard_map/ppermute | solution.py:761
  61.2 3.6 arrange_qkv.1
  67.9 3.4 arrange_rest.1
  75.5 18.8 %collective-permute-done.3 = bf16[152,768]{1,0:T(8,128)(2,1)S(1)} collective-permute-done((bf16[152,768]{1,0:T(8,128)(2,1)S(1)}, bf16[152,768]{1,0:T(8,128)(2,1)S(1)}, u32[]{:S(2)}, u32[]{:S(2)}) %collective-permute-start.3) | collective-permute-done | bytes 233504 | tf_op jit(solution)/shard_map/ppermute | solution.py:761
  98.4 6.0 %collective-permute-done.8.refs_5_ = bf16[304,768]{1,0:T(8,128)(2,1)S(1)} collective-permute-done((bf16[304,768]{1,0:T(8,128)(2,1)S(1)}, bf16[304,768]{1,0:T(8,128)(2,1)S(1)}, u32[]{:S(2)}, u32[]{:S(2)}) %collective-permute-start.8) | collective-permute-done | bytes 466976 | tf_op jit(solution)/shard_map/ppermute | solution.py:761
  104.4 3.7 collective-permute-done.4.refs_1_
  110.8 12.6 %project.1 = (bf16[1224,2304]{1,0:T(8,128)(2,1)}, bf16[1224,768]{1,0:T(8,128)(2,1)}, f32[16,768]{1,0:T(8,128)}) custom-call(s32[16]{0:T(128)} %pad_add_fusion.table, bf16[1224,768]{1,0:T(8,128)(2,1)} %x_ref.5, bf16[304,768]{1,0:T(8,128)(2,1)} %copy-done.17, bf16[304,768]{1,0:T(8,128)(2,1)} %copy-done.25, bf16[304,768]{1,0:T(8,128)(2,1)} %copy-done.26, ...), custom_call_target="tpu_custom_call" | custom-call | flops 4331667456 | bytes 9400320 | tf_op jit(solution)/shard_map/project/pallas_call | solution.py:225
  127.4 27.6 %attend.1 = (bf16[1224,768]{1,0:T(8,128)(2,1)}, f32[6,8,1280]{2,1,0:T(8,128)}) custom-call(s32[1]{0:T(128)S(6)} %copy.59.len_ref, bf16[1224,2304]{1,0:T(8,128)(2,1)} %get-tuple-element.44.q_ref.k_ref.v_ref, bf16[1224,2304]{1,0:T(8,128)(2,1)} %get-tuple-element.44.q_ref.k_ref.v_ref, bf16[1224,2304]{1,0:T(8,128)(2,1)} %get-tuple-element.44.q_ref.k_ref.v_ref), custom_call_target="tpu_custom_call" | custom-call | flops 18409586688 | bytes 7520256 | tf_op jit(solution)/shard_map/attend/pallas_call | solution.py:290
  156.2 50.9 %middle.1 = (bf16[1224,768]{1,0:T(8,128)(2,1)}, bf16[1224,3072]{1,0:T(8,128)(2,1)}, bf16[1224,3072]{1,0:T(8,128)(2,1)}, bf16[1224,768]{1,0:T(8,128)(2,1)}, f32[1...) custom-call(s32[1]{0:T(128)S(6)} %copy.59.len_ref, ...), custom_call_target="tpu_custom_call" | custom-call | flops 25990004736 | bytes 41398272 | tf_op jit(solution)/shard_map/middle/pallas_call | solution.py:546
  207.1 24.0 %rest_grads.1 = (bf16[4,864,768]{2,1,0:T(8,128)(2,1)}, bf16[4,864,768]{2,1,0:T(8,128)(2,1)}) custom-call(s32[1]{0:T(128)S(6)} %copy.59.len_ref, s32[8]{0:T(128)} %copy-done.21, bf16[1224,3072]{1,0:T(8,128)(2,1)} %get-tuple-element.62.active_ref, bf16[1224,3072]{1,0:T(8,128)(2,1)} %get-tuple-element.63.d_inner_ref, ...), custom_call_target="tpu_custom_call" | custom-call | flops 12995002368 | bytes 25657344 | tf_op jit(solution)/shard_map/rest_grads/pallas_call | solution.py:645
  231.6 52.9 %attend_back.1 = (bf16[1224,768]{1,0:T(8,128)(2,1)}, bf16[1224,768]{1,0:T(8,128)(2,1)}, bf16[1224,768]{1,0:T(8,128)(2,1)}) custom-call(s32[1]{0:T(128)S(6)} %copy.59.len_ref, bf16[1224,2304]{1,0:T(8,128)(2,1)} %get-tuple-element.44.q_ref.k_ref.v_ref, bf16[1224,2304]{1,0:T(8,128)(2,1)} %get-tuple-element.44.q_ref.k_ref.v_ref, ...), custom_call_target="tpu_custom_call" | custom-call | flops 46023966720 | bytes 15040512 | tf_op jit(solution)/shard_map/attend_back/pallas_call | solution.py:394
  284.5 10.5 %qkv_grads.1 = (bf16[4,288,768]{2,1,0:T(8,128)(2,1)}, bf16[4,288,768]{2,1,0:T(8,128)(2,1)}) custom-call(s32[8]{0:T(128)} %copy-done.21, bf16[1224,768]{1,0:T(8,128)(2,1)} %get-tuple-element.53.dq_ref, bf16[1224,768]{1,0:T(8,128)(2,1)} %get-tuple-element.54.dk_ref, bf16[1224,768]{1,0:T(8,128)(2,1)} %get-tuple-element.55.dv_ref, ...), custom_call_target="tpu_custom_call" | custom-call | flops 4331667456 | bytes 11059200 | tf_op jit(solution)/shard_map/qkv_grads/pallas_call | solution.py:688
  295.1 13.6 %last.1 = (f32[1224,768]{1,0:T(8,128)}, f32[16,768]{1,0:T(8,128)}) custom-call(s32[16]{0:T(128)} %pad_add_fusion.table, bf16[1224,768]{1,0:T(8,128)(2,1)} %get-tuple-element.53.dq_ref, bf16[1224,768]{1,0:T(8,128)(2,1)} %get-tuple-element.54.dk_ref, bf16[1224,768]{1,0:T(8,128)(2,1)} %get-tuple-element.55.dv_ref, bf16[1224,768]{1,0:T(8,128)(2,1)} %x_ref.5, ...), custom_call_target="tpu_custom_call" | custom-call | flops 4331667456 | bytes 15040512 | tf_op jit(solution)/shard_map/last/pallas_call | solution.py:738
  315.9 3.1 add_convert_fusion.8
  324.4 3.3 collective-permute-start.47
  339.3 20.5 %collective-permute-done.25 = bf16[2,144,768]{2,1,0:T(8,128)(2,1)S(1)} collective-permute-done((bf16[2,144,768]{2,1,0:T(8,128)(2,1)S(1)}, bf16[2,144,768]{2,1,0:T(8,128)(2,1)S(1)}, u32[]{:S(2)}, u32[]{:S(2)}) %collective-permute-start.25) | collective-permute-done | bytes 442400 | tf_op jit(solution)/shard_map/ppermute | solution.py:761
  364.5 3.7 fusion
  372.7 3.3 collective-permute-start.27
  381.2 5.9 %collective-permute-done.28 = bf16[192,288]{1,0:T(8,128)(2,1)S(1)} collective-permute-done((bf16[192,288]{1,0:T(8,128)(2,1)S(1)}, bf16[192,288]{1,0:T(8,128)(2,1)S(1)}, u32[]{:S(2)}, u32[]{:S(2)}) %collective-permute-start.28) | collective-permute-done | bytes 110624 | tf_op jit(solution)/shard_map/ppermute | solution.py:761
  387.9 3.1 bitcast_add_fusion.1
  404.8 3.8 collective-permute-done.36
  409.8 5.1 %collective-permute-start.39 = (bf16[192,384]{1,0:T(8,128)(2,1)S(1)}, bf16[192,384]{1,0:T(8,128)(2,1)S(1)}, u32[]{:S(2)}, u32[]{:S(2)}) collective-permute-start(bf16[192,384]{1,0:T(8,128)(2,1)S(1)} %get-tuple-element.90), channel_id=1, source_target_pairs={{0,16},{8,24},{16,0},{24,8},{1,17},{9,25},{17,1},{25,9},{2,18},{10... | collective-permute-start | bytes 442376 | tf_op jit(solution)/shard_map/ppermute | solution.py:761
  418.2 5.7 %collective-permute-done.39 = bf16[192,384]{1,0:T(8,128)(2,1)S(1)} collective-permute-done((bf16[192,384]{1,0:T(8,128)(2,1)S(1)}, bf16[192,384]{1,0:T(8,128)(2,1)S(1)}, u32[]{:S(2)}, u32[]{:S(2)}) %collective-permute-start.39) | collective-permute-done | bytes 147488 | tf_op jit(solution)/shard_map/ppermute | solution.py:761
  (206 shorter events, 95.4 us)
Async XLA Ops:
  14.9 51.4 %collective-permute-start.11 = (bf16[192,896]{1,0:T(8,128)(2,1)S(1)}, bf16[192,896]{1,0:T(8,128)(2,1)S(1)}, u32[]{:S(2)}, u32[]{:S(2)}) collective-permute-start(bf16[192,896]{1,0:T(8,128)(2,1)S(1)} %maximum_maximum_fusion.refs_0_), channel_id=1, source_target_pairs={{0,8},{8,0},{16,24},{24,16},{1,9},{9,1},{17,25},{25,17},{2,10},{10... | collective-permute-start | bytes 1032200 | tf_op jit(solution)/shard_map/ppermute | solution.py:761
  16.7 49.7 %collective-permute-start.12 = (bf16[192,896]{1,0:T(8,128)(2,1)S(1)}, bf16[192,896]{1,0:T(8,128)(2,1)S(1)}, u32[]{:S(2)}, u32[]{:S(2)}) collective-permute-start(bf16[192,896]{1,0:T(8,128)(2,1)S(1)} %maximum_maximum_fusion.refs_0_), channel_id=1, source_target_pairs={{0,16},{8,24},{16,0},{24,8},{1,17},{9,25},{17,1},{25,9},{2,18},{10... | collective-permute-start | bytes 1032200 | tf_op jit(solution)/shard_map/ppermute | solution.py:761
  19.3 47.1 %collective-permute-start.13 = (bf16[192,896]{1,0:T(8,128)(2,1)S(1)}, bf16[192,896]{1,0:T(8,128)(2,1)S(1)}, u32[]{:S(2)}, u32[]{:S(2)}) collective-permute-start(bf16[192,896]{1,0:T(8,128)(2,1)S(1)} %maximum_maximum_fusion.refs_0_), channel_id=1, source_target_pairs={{0,24},{8,16},{16,8},{24,0},{1,25},{9,17},{17,9},{25,1},{2,26},{10... | collective-permute-start | bytes 1032200 | tf_op jit(solution)/shard_map/ppermute | solution.py:761
  19.3 40.6 %collective-permute-start.1 = (bf16[200,288]{1,0:T(8,128)(2,1)S(1)}, bf16[200,288]{1,0:T(8,128)(2,1)S(1)}, u32[]{:S(2)}, u32[]{:S(2)}) collective-permute-start(bf16[200,288]{1,0:T(8,128)(2,1)S(1)} %maximum_maximum_fusion.1.refs_0_), channel_id=1, source_target_pairs={{0,16},{8,24},{16,0},{24,8},{1,17},{9,25},{17,1},{25,9},{2,18},{10... | collective-permute-start | bytes 345608 | tf_op jit(solution)/shard_map/ppermute | solution.py:761
  21.2 38.7 %collective-permute-start.2 = (bf16[200,288]{1,0:T(8,128)(2,1)S(1)}, bf16[200,288]{1,0:T(8,128)(2,1)S(1)}, u32[]{:S(2)}, u32[]{:S(2)}) collective-permute-start(bf16[200,288]{1,0:T(8,128)(2,1)S(1)} %maximum_maximum_fusion.1.refs_0_), channel_id=1, source_target_pairs={{0,24},{8,16},{16,8},{24,0},{1,25},{9,17},{17,9},{25,1},{2,26},{10... | collective-permute-start | bytes 345608 | tf_op jit(solution)/shard_map/ppermute | solution.py:761
  71.3 23.8 %collective-permute-start.14 = (bf16[432,768]{1,0:T(8,128)(2,1)}, bf16[432,768]{1,0:T(8,128)(2,1)S(1)}, u32[]{:S(2)}, u32[]{:S(2)}) collective-permute-start(bf16[432,768]{1,0:T(8,128)(2,1)} %get-tuple-element.48), channel_id=1, source_target_pairs={{0,2},{1,3},{2,0},{3,1},{4,6},{5,7},{6,4},{7,5},{8,10},{9,11},{10,... | collective-permute-start | bytes 1990664 | tf_op jit(solution)/shard_map/ppermute | solution.py:761
  72.8 21.5 %collective-permute-start.3 = (bf16[152,768]{1,0:T(8,128)(2,1)S(1)}, bf16[152,768]{1,0:T(8,128)(2,1)S(1)}, u32[]{:S(2)}, u32[]{:S(2)}) collective-permute-start(bf16[152,768]{1,0:T(8,128)(2,1)S(1)} %copy-done.11), channel_id=1, source_target_pairs={{0,2},{1,3},{2,0},{3,1},{4,6},{5,7},{6,4},{7,5},{8,10},{9,11},{10,... | collective-permute-start | bytes 700424 | tf_op jit(solution)/shard_map/ppermute | solution.py:761
  73.4 23.3 %collective-permute-start.18 = (bf16[432,768]{1,0:T(8,128)(2,1)}, bf16[432,768]{1,0:T(8,128)(2,1)S(1)}, u32[]{:S(2)}, u32[]{:S(2)}) collective-permute-start(bf16[432,768]{1,0:T(8,128)(2,1)} %get-tuple-element.49), channel_id=1, source_target_pairs={{0,4},{1,5},{2,6},{3,7},{4,0},{5,1},{6,2},{7,3},{8,12},{9,13},{10,... | collective-permute-start | bytes 1990664 | tf_op jit(solution)/shard_map/ppermute | solution.py:761
  74.0 30.4 %collective-permute-start.8 = (bf16[304,768]{1,0:T(8,128)(2,1)S(1)}, bf16[304,768]{1,0:T(8,128)(2,1)S(1)}, u32[]{:S(2)}, u32[]{:S(2)}) collective-permute-start(bf16[304,768]{1,0:T(8,128)(2,1)S(1)} %constant_dynamic-update-slice_fusion.2.refs_4_), channel_id=1, source_target_pairs={{0,2},{1,3},{2,0},{3,1},{4,6},{5,7},{6,4},{7,5},{8,10},{9,11},{10,... | collective-permute-start | bytes 1400840 | tf_op jit(solution)/shard_map/ppermute | solution.py:761
  75.5 32.5 %collective-permute-start.9 = (bf16[304,768]{1,0:T(8,128)(2,1)S(1)}, bf16[304,768]{1,0:T(8,128)(2,1)S(1)}, u32[]{:S(2)}, u32[]{:S(2)}) collective-permute-start(bf16[304,768]{1,0:T(8,128)(2,1)S(1)} %constant_dynamic-update-slice_fusion.2.refs_4_), channel_id=1, source_target_pairs={{0,1},{1,0},{2,3},{3,2},{4,5},{5,4},{6,7},{7,6},{8,9},{9,8},{10,11... | collective-permute-start | bytes 1400840 | tf_op jit(solution)/shard_map/ppermute | solution.py:761
  95.2 29.6 %collective-permute-start.15 = (bf16[864,768]{1,0:T(8,128)(2,1)S(1)}, bf16[864,768]{1,0:T(8,128)(2,1)}, u32[]{:S(2)}, u32[]{:S(2)}) collective-permute-start(bf16[864,768]{1,0:T(8,128)(2,1)S(1)} %constant_dynamic-update-slice_fusion.4.refs_0_), channel_id=1, source_target_pairs={{0,4},{1,5},{2,6},{3,7},{4,0},{5,1},{6,2},{7,3},{8,12},{9,13},{10,... | collective-permute-start | bytes 3981320 | tf_op jit(solution)/shard_map/ppermute | solution.py:761
  96.8 30.6 %collective-permute-start.19 = (bf16[864,768]{1,0:T(8,128)(2,1)S(1)}, bf16[864,768]{1,0:T(8,128)(2,1)}, u32[]{:S(2)}, u32[]{:S(2)}) collective-permute-start(bf16[864,768]{1,0:T(8,128)(2,1)S(1)} %constant_dynamic-update-slice_fusion.6.refs_4_), channel_id=1, source_target_pairs={{0,2},{1,3},{2,0},{3,1},{4,6},{5,7},{6,4},{7,5},{8,10},{9,11},{10,... | collective-permute-start | bytes 3981320 | tf_op jit(solution)/shard_map/ppermute | solution.py:761
  109.9 45.2 %collective-permute-start.16 = (bf16[864,768]{1,0:T(8,128)(2,1)S(1)}, bf16[864,768]{1,0:T(8,128)(2,1)}, u32[]{:S(2)}, u32[]{:S(2)}) collective-permute-start(bf16[864,768]{1,0:T(8,128)(2,1)S(1)} %constant_dynamic-update-slice_fusion.4.refs_0_), channel_id=1, source_target_pairs={{0,1},{1,0},{2,3},{3,2},{4,5},{5,4},{6,7},{7,6},{8,9},{9,8},{10,11... | collective-permute-start | bytes 3981320 | tf_op jit(solution)/shard_map/ppermute | solution.py:761
  110.0 45.1 %collective-permute-start.20 = (bf16[864,768]{1,0:T(8,128)(2,1)S(1)}, bf16[864,768]{1,0:T(8,128)(2,1)}, u32[]{:S(2)}, u32[]{:S(2)}) collective-permute-start(bf16[864,768]{1,0:T(8,128)(2,1)S(1)} %constant_dynamic-update-slice_fusion.6.refs_4_), channel_id=1, source_target_pairs={{0,1},{1,0},{2,3},{3,2},{4,5},{5,4},{6,7},{7,6},{8,9},{9,8},{10,11... | collective-permute-start | bytes 3981320 | tf_op jit(solution)/shard_map/ppermute | solution.py:761
  124.8 30.3 %collective-permute-start.17 = (bf16[864,768]{1,0:T(8,128)(2,1)}, bf16[864,768]{1,0:T(8,128)(2,1)S(1)}, u32[]{:S(2)}, u32[]{:S(2)}) collective-permute-start(bf16[864,768]{1,0:T(8,128)(2,1)} %collective-permute-done.15.refs_1_), channel_id=1, source_target_pairs={{0,1},{1,0},{2,3},{3,2},{4,5},{5,4},{6,7},{7,6},{8,9},{9,8},{10,11... | collective-permute-start | bytes 3981320 | tf_op jit(solution)/shard_map/ppermute | solution.py:761
  127.4 27.6 %collective-permute-start.21 = (bf16[864,768]{1,0:T(8,128)(2,1)}, bf16[864,768]{1,0:T(8,128)(2,1)}, u32[]{:S(2)}, u32[]{:S(2)}) collective-permute-start(bf16[864,768]{1,0:T(8,128)(2,1)} %collective-permute-done.19.refs_5_), channel_id=1, source_target_pairs={{0,1},{1,0},{2,3},{3,2},{4,5},{5,4},{6,7},{7,6},{8,9},{9,8},{10,11... | collective-permute-start | bytes 3981320 | tf_op jit(solution)/shard_map/ppermute | solution.py:761
  231.0 84.8 %collective-permute-start.30 = (bf16[4,864,768]{2,1,0:T(8,128)(2,1)}, bf16[4,864,768]{2,1,0:T(8,128)(2,1)}, u32[]{:S(2)}, u32[]{:S(2)}) collective-permute-start(bf16[4,864,768]{2,1,0:T(8,128)(2,1)} %get-tuple-element.67), channel_id=1, source_target_pairs={{0,1},{1,0},{2,3},{3,2},{4,5},{5,4},{6,7},{7,6},{8,9},{9,8},{10,11... | collective-permute-start | bytes 15925256 | tf_op jit(solution)/shard_map/ppermute | solution.py:761
  295.0 41.5 %collective-permute-start.22 = (bf16[4,288,768]{2,1,0:T(8,128)(2,1)}, bf16[4,288,768]{2,1,0:T(8,128)(2,1)S(1)}, u32[]{:S(2)}, u32[]{:S(2)}) collective-permute-start(bf16[4,288,768]{2,1,0:T(8,128)(2,1)} %get-tuple-element.61), channel_id=1, source_target_pairs={{0,1},{1,0},{2,3},{3,2},{4,5},{5,4},{6,7},{7,6},{8,9},{9,8},{10,11... | collective-permute-start | bytes 5308424 | tf_op jit(solution)/shard_map/ppermute | solution.py:761
  320.2 44.3 %collective-permute-start.33 = (bf16[2,432,768]{2,1,0:T(8,128)(2,1)}, bf16[2,432,768]{2,1,0:T(8,128)(2,1)}, u32[]{:S(2)}, u32[]{:S(2)}) collective-permute-start(bf16[2,432,768]{2,1,0:T(8,128)(2,1)} %pad_maximum_fusion.1), channel_id=1, source_target_pairs={{0,2},{1,3},{2,0},{3,1},{4,6},{5,7},{6,4},{7,5},{8,10},{9,11},{10,... | collective-permute-start | bytes 3981320 | tf_op jit(solution)/shard_map/ppermute | solution.py:761
  322.8 41.7 %collective-permute-start.31 = (bf16[2,432,768]{2,1,0:T(8,128)(2,1)}, bf16[2,432,768]{2,1,0:T(8,128)(2,1)}, u32[]{:S(2)}, u32[]{:S(2)}) collective-permute-start(bf16[2,432,768]{2,1,0:T(8,128)(2,1)} %pad_maximum_fusion), channel_id=1, source_target_pairs={{0,4},{1,5},{2,6},{3,7},{4,0},{5,1},{6,2},{7,3},{8,12},{9,13},{10,... | collective-permute-start | bytes 3981320 | tf_op jit(solution)/shard_map/ppermute | solution.py:761
  336.8 23.0 %collective-permute-start.25 = (bf16[2,144,768]{2,1,0:T(8,128)(2,1)S(1)}, bf16[2,144,768]{2,1,0:T(8,128)(2,1)S(1)}, u32[]{:S(2)}, u32[]{:S(2)}) collective-permute-start(bf16[2,144,768]{2,1,0:T(8,128)(2,1)S(1)} %pad_maximum_fusion.3), channel_id=1, source_target_pairs={{0,2},{1,3},{2,0},{3,1},{4,6},{5,7},{6,4},{7,5},{8,10},{9,11},{10,... | collective-permute-start | bytes 1327112 | tf_op jit(solution)/shard_map/ppermute | solution.py:761
  337.5 24.7 %collective-permute-start.23 = (bf16[2,144,768]{2,1,0:T(8,128)(2,1)S(1)}, bf16[2,144,768]{2,1,0:T(8,128)(2,1)S(1)}, u32[]{:S(2)}, u32[]{:S(2)}) collective-permute-start(bf16[2,144,768]{2,1,0:T(8,128)(2,1)S(1)} %pad_maximum_fusion.2), channel_id=1, source_target_pairs={{0,4},{1,5},{2,6},{3,7},{4,0},{5,1},{6,2},{7,3},{8,12},{9,13},{10,... | collective-permute-start | bytes 1327112 | tf_op jit(solution)/shard_map/ppermute | solution.py:761
  392.7 23.6 %collective-permute-start.41 = (bf16[768,96]{0,1:T(8,128)(2,1)}, bf16[768,96]{0,1:T(8,128)(2,1)}, u32[]{:S(2)}, u32[]{:S(2)}) collective-permute-start(bf16[768,96]{0,1:T(8,128)(2,1)} %get-tuple-element.85), channel_id=1, source_target_pairs={{0,8},{8,0},{16,24},{24,16},{1,9},{9,1},{17,25},{25,17},{2,10},{10... | collective-permute-start | bytes 442376 | tf_op jit(solution)/shard_map/ppermute | solution.py:761
  394.9 21.5 %collective-permute-start.42 = (bf16[768,96]{0,1:T(8,128)(2,1)}, bf16[768,96]{0,1:T(8,128)(2,1)}, u32[]{:S(2)}, u32[]{:S(2)}) collective-permute-start(bf16[768,96]{0,1:T(8,128)(2,1)} %get-tuple-element.87), channel_id=1, source_target_pairs={{0,16},{8,24},{16,0},{24,8},{1,17},{9,25},{17,1},{25,9},{2,18},{10... | collective-permute-start | bytes 442376 | tf_op jit(solution)/shard_map/ppermute | solution.py:761
  (53 other events, 593.7 us)

commit v2 on v1

v2 whole, which is shorter than its diff:
```python
import functools

import jax
import jax.numpy as jnp
from jax import lax
from jax.experimental import pallas as pl
from jax.experimental.pallas import tpu as pltpu
from jax.sharding import PartitionSpec as P

HEADS = 12
HEAD_DIM = 64
PAIR = 2 * HEAD_DIM
EPSILON = 1e-06
NEG_FILL = -1e30
BF = jnp.bfloat16
F32 = jnp.float32
AXES = ("gx", "gy")
BLOCKS = 8
AUX = 16
VMEM_BYTES = 60 << 20
MASKS_A = (0, 2, 4, 6, 1, 3, 5, 7)
MASKS_B = (0, 4, 2, 6, 1, 5, 3, 7)
PLANES = (0, 2, 1, 3)
ANY = pl.BlockSpec(memory_space=pl.ANY)


def nt(left, right):
    return lax.dot_general(left, right, (((1,), (1,)), ((), ())), preferred_element_type=F32)


def nn(left, right):
    return lax.dot_general(left, right, (((1,), (0,)), ((), ())), preferred_element_type=F32)


def tn(left, right):
    return lax.dot_general(left, right, (((0,), (0,)), ((), ())), preferred_element_type=F32)


def params(**extra):
    return pltpu.CompilerParams(vmem_limit_bytes=VMEM_BYTES, **extra)


def cost(flops, bytes_moved, transcendentals=0):
    return pl.CostEstimate(
        flops=int(flops), bytes_accessed=int(bytes_moved), transcendentals=int(transcendentals)
    )


def whole(shape):
    return pl.BlockSpec(shape, lambda *_: (0,) * len(shape))


def normalise(values):
    centre = values - jnp.mean(values, axis=-1, keepdims=True)
    spread = jnp.mean(centre * centre, axis=-1, keepdims=True)
    scale = lax.rsqrt(spread + EPSILON)
    return centre * scale, scale


def norm_back(grads, nhat, scale, gain):
    e = grads * gain
    return scale * (
        e
        - jnp.mean(e, axis=-1, keepdims=True)
        - nhat * jnp.mean(e * nhat, axis=-1, keepdims=True)
    )


def pack_kernel(w_ref, *refs):
    vectors, out_ref = refs[:-1], refs[-1]
    rows = w_ref.shape[0]
    out_ref[0:rows, :] = w_ref[...]
    out_ref[rows:, :] = jnp.zeros((out_ref.shape[0] - rows, out_ref.shape[1]), BF)
    pieces = [ref[...].astype(F32) for ref in vectors]
    out_ref[rows : rows + 8, :] = jnp.broadcast_to(
        jnp.concatenate(pieces, axis=1), (8, out_ref.shape[1])
    ).astype(BF)


def pack(w_qkv, vectors):
    rows, columns = w_qkv.shape
    shape = (rows + 8, columns)
    return pl.pallas_call(
        pack_kernel,
        out_shape=jax.ShapeDtypeStruct(shape, BF),
        compiler_params=params(),
        cost_estimate=cost(1e4, rows * columns * 4),
        name="pack",
    )(w_qkv, *[v[None, :] for v in vectors])


def pack_rest_kernel(up_ref, out_ref, down_ref, both_ref, turned_ref):
    wide, narrow = up_ref.shape[1], out_ref.shape[1]
    both_ref[:, 0:wide] = up_ref[...]
    both_ref[:, wide : wide + narrow] = out_ref[...]
    both_ref[:, wide + narrow :] = jnp.zeros(
        (both_ref.shape[0], both_ref.shape[1] - wide - narrow), BF
    )
    turned_ref[...] = down_ref[...].astype(F32).T.astype(BF)


def pack_rest(w_up, w_out, w_down):
    rows = w_up.shape[0]
    columns = -(-(w_up.shape[1] + w_out.shape[1]) // 128) * 128
    return pl.pallas_call(
        pack_rest_kernel,
        out_shape=[
            jax.ShapeDtypeStruct((rows, columns), BF),
            jax.ShapeDtypeStruct(w_down.shape[::-1], BF),
        ],
        compiler_params=params(),
        cost_estimate=cost(1e4, rows * columns * 4 + w_down.size * 4),
        name="pack_rest",
    )(w_up, w_out, w_down)


def arrange_qkv_kernel(pos, *refs):
    pieces, (first_ref, second_ref), stacked = refs[:4], refs[4:6], refs[6]
    width, columns = first_ref.shape[1], pieces[0].shape[1]
    half = columns // 2
    rows = width // 4
    vec_rows = []
    for k in range(4):
        place = pos[0] ^ k
        stacked[pl.ds(pl.multiple_of(place * rows, 8), rows), :] = pieces[k][0:rows, :].astype(F32)
        vec_rows.append(pieces[k][rows : rows + 1, :].astype(F32))
    turned = stacked[...].T.astype(BF)
    first_ref[0:half, :] = turned[0:half]
    second_ref[...] = turned[half:columns]
    vec = jnp.concatenate(vec_rows, axis=0).astype(BF)
    lane = lax.broadcasted_iota(jnp.int32, (columns, width), 1)
    source = lax.broadcasted_iota(jnp.int32, (columns, width), 0)
    lane4 = lax.broadcasted_iota(jnp.int32, (4, width), 1)
    order = lax.broadcasted_iota(jnp.int32, (4, 1), 0)
    piece = width // (4 * BLOCKS)
    device = (pos[0] ^ order) * BLOCKS + pos[1]
    here = lane4 // piece == device
    base = lane % piece
    rows_out = []
    for j in range(8):
        spread = nn(vec, (source == piece * j + base).astype(BF))
        rows_out.append(jnp.sum(jnp.where(here, spread, 0.0), axis=0, keepdims=True))
    pick = (source == piece * 8 + lane % (4 * piece)).astype(BF)
    spread = jnp.where(lane4 // (4 * piece) == pos[1], nn(vec, pick), 0.0)
    for row in range(4):
        rows_out.append(
            jnp.sum(jnp.where((pos[0] ^ order) == row, spread, 0.0), axis=0, keepdims=True)
        )
    rows_out.append(jnp.zeros((AUX - 12, width), F32))
    first_ref[half : half + AUX, :] = jnp.concatenate(rows_out, axis=0).astype(BF)


def arrange_qkv(pos, pieces, width):
    rows, columns = pieces[0].shape
    out = [
        jax.ShapeDtypeStruct((columns // 2 + AUX, width), BF),
        jax.ShapeDtypeStruct((columns // 2, width), BF),
    ]
    return pl.pallas_call(
        arrange_qkv_kernel,
        grid_spec=pltpu.PrefetchScalarGridSpec(
            num_scalar_prefetch=1,
            grid=(1,),
            in_specs=[whole((rows, columns))] * 4,
            out_specs=[whole(o.shape) for o in out],
            scratch_shapes=[pltpu.VMEM((width, columns), F32)],
        ),
        out_shape=out,
        compiler_params=params(),
        cost_estimate=cost(4e6, 4 * rows * columns * 2 * 2),
        name="arrange_qkv",
    )(pos, *pieces)


def arrange_rest_kernel(pos, *refs):
    pieces, (first_ref, second_ref), stacked = refs[:4], refs[4:6], refs[6]
    rows = first_ref.shape[1] // 4
    half = first_ref.shape[0]
    for k in range(4):
        start = pl.multiple_of((pos[0] ^ k) * rows, 8)
        stacked[pl.ds(start, rows), :] = pieces[k][...].astype(F32)
    turned = stacked[...].T.astype(BF)
    first_ref[...] = turned[0:half]
    second_ref[...] = turned[half : 2 * half]


def arrange_rest(pos, pieces, width, height):
    out = jax.ShapeDtypeStruct((height // 2, width), BF)
    return pl.pallas_call(
        arrange_rest_kernel,
        grid_spec=pltpu.PrefetchScalarGridSpec(
            num_scalar_prefetch=1,
            grid=(1,),
            in_specs=[whole(pieces[0].shape)] * 4,
            out_specs=[whole(out.shape)] * 2,
            scratch_shapes=[pltpu.VMEM((width, pieces[0].shape[1]), F32)],
        ),
        out_shape=[out, out],
        compiler_params=params(),
        cost_estimate=cost(1e6, out.shape[0] * width * 2 * 4),
        name="arrange_rest",
    )(pos, *pieces)


def qkv_copies(table, halves, weights, sems):
    step = weights.shape[0] // (2 * BLOCKS)
    copies = []
    for j in range(2 * BLOCKS):
        source = halves[j // 2]
        start = table[j] * (2 * step) + j // BLOCKS * step
        copies.append(
            pltpu.make_async_copy(
                source.at[pl.ds(j % 2 * (source.shape[0] // 2), step)],
                weights.at[pl.ds(pl.multiple_of(start, 16), step)],
                sems.at[j],
            )
        )
    return copies


def project_kernel(table, x_ref, *refs):
    blocks, (proj_ref, normed_ref, vec_ref), (weights, aux, sems) = refs[:8], refs[8:11], refs[11:]
    j = pl.program_id(0)
    step = weights.shape[0] // (2 * BLOCKS)
    tile = proj_ref.shape[1]
    width = x_ref.shape[1]

    @pl.when(j == 0)
    def _():
        small = [
            pltpu.make_async_copy(
                blocks[i // 2].at[pl.ds(i % 2 * (step + AUX) + step, AUX)],
                aux.at[i],
                sems.at[2 * BLOCKS + i],
            )
            for i in range(BLOCKS)
        ]
        large = qkv_copies(table, blocks, weights, sems)
        for copy in small + large:
            copy.start()
        nhat, _ = normalise(x_ref[...].astype(F32))
        for copy in small:
            copy.wait()
        vec_ref[...] = jnp.sum(aux[...].astype(F32), axis=0)
        normed_ref[...] = (nhat * vec_ref[4:5, :] + vec_ref[5:6, :]).astype(BF)
        for copy in large:
            copy.wait()

    per = width // tile
    start = pl.multiple_of(j * tile, tile)
    lanes = pl.ds(pl.multiple_of(lax.rem(j, per) * tile, tile), tile)
    section = j // per
    bias = jnp.where(
        section == 0, vec_ref[0:1, lanes], jnp.where(section == 2, vec_ref[1:2, lanes], 0.0)
    )
    proj_ref[...] = (nt(normed_ref[...], weights[pl.ds(start, tile), :]) + bias).astype(BF)


def project(table, x, blocks, tile=256):
    slots, width = x.shape
    columns = 3 * width
    return pl.pallas_call(
        project_kernel,
        grid_spec=pltpu.PrefetchScalarGridSpec(
            num_scalar_prefetch=1,
            grid=(columns // tile,),
            in_specs=[whole((slots, width))] + [ANY] * 8,
            out_specs=[
                pl.BlockSpec((slots, tile), lambda j, _: (0, j)),
                whole((slots, width)),
                whole((AUX, width)),
            ],
            scratch_shapes=[
                pltpu.VMEM((columns, width), BF),
                pltpu.VMEM((BLOCKS, AUX, width), BF),
                pltpu.SemaphoreType.DMA((3 * BLOCKS,)),
            ],
        ),
        out_shape=[
            jax.ShapeDtypeStruct((slots, columns), BF),
            jax.ShapeDtypeStruct((slots, width), BF),
            jax.ShapeDtypeStruct((AUX, width), F32),
        ],
        compiler_params=params(),
        cost_estimate=cost(2 * slots * width * columns, slots * width * 10),
        name="project",
    )(table, x, *blocks)


def attend_kernel(len_ref, q_ref, k_ref, v_ref, *refs, slots, padded):
    o_ref, lse_ref, qp = refs[-3:]
    length = len_ref[0]
    lane = lax.broadcasted_iota(jnp.int32, (slots, PAIR), 1)
    row = lax.broadcasted_iota(jnp.int32, (slots, PAIR), 0)
    bias = jnp.where(row < length, 0.0, NEG_FILL)
    keys = k_ref[...].astype(F32)
    values = v_ref[...].astype(F32)
    queries = q_ref[...].astype(F32) * HEAD_DIM**-0.5
    outs = []
    for h in range(2):
        mine = (lane // HEAD_DIM) == h
        spare = (1 - h) * HEAD_DIM
        flag = lane == spare
        key_ext = jnp.where(mine, keys, jnp.where(flag, bias, 0.0)).astype(BF)
        value_ext = jnp.where(mine, values, jnp.where(flag, 1.0, 0.0)).astype(BF)
        qp[h, 0:slots, :] = jnp.where(mine, queries, jnp.where(flag, 1.0, 0.0)).astype(BF)
        if padded > slots:
            qp[h, slots:padded, :] = jnp.zeros((padded - slots, PAIR), BF)
        scores = nt(key_ext, qp[h])
        top = jnp.max(scores, axis=0, keepdims=True)
        weights = jnp.exp(scores - top).astype(BF)
        mixed = nn(value_ext.T, weights)
        total = mixed[spare : spare + 1, :]
        outs.append(mixed[h * HEAD_DIM : (h + 1) * HEAD_DIM, :] / total)
        lse_ref[0, h : h + 1, :] = top + jnp.log(total)
    o_ref[...] = jnp.concatenate(outs, axis=0).T[0:slots].astype(BF)


def attend(length, proj, first=0, count=None, into=()):
    slots = proj.shape[0]
    padded = -(-slots // 128) * 128
    width = proj.shape[1] // 3
    pairs = width // PAIR
    count = pairs if count is None else count

    def spec(off):
        return pl.BlockSpec((slots, PAIR), lambda p, _: (0, off + first + p))

    return pl.pallas_call(
        functools.partial(attend_kernel, slots=slots, padded=padded),
        grid_spec=pltpu.PrefetchScalarGridSpec(
            num_scalar_prefetch=1,
            grid=(count,),
            in_specs=[spec(0), spec(pairs), spec(2 * pairs)] + [ANY] * len(into),
            out_specs=[spec(0), pl.BlockSpec((1, 8, padded), lambda p, _: (first + p, 0, 0))],
            scratch_shapes=[pltpu.VMEM((2, padded, PAIR), BF)],
        ),
        out_shape=[
            jax.ShapeDtypeStruct((slots, width), BF),
            jax.ShapeDtypeStruct((pairs, 8, padded), F32),
        ],
        input_output_aliases={4 + i: i for i in range(len(into))},
        compiler_params=params(),
        cost_estimate=cost(
            2 * count * 8 * slots * slots * PAIR, slots * width * 8, 2 * count * slots * slots
        ),
        name="attend",
    )(length, proj, proj, proj, *into)


def parts(values):
    high = values.astype(BF).astype(F32)
    rest = values - high
    mid = rest.astype(BF).astype(F32)
    return high, mid, (rest - mid).astype(BF).astype(F32)


def attend_back_kernel(
    len_ref,
    q_ref,
    k_ref,
    v_ref,
    g_ref,
    o_ref,
    lse_ref,
    dq_ref,
    dk_ref,
    dv_ref,
    qp,
    gp,
    *,
    slots,
    padded,
    tile,
):
    length = len_ref[0]
    lane = lax.broadcasted_iota(jnp.int32, (slots, PAIR), 1)
    row = lax.broadcasted_iota(jnp.int32, (slots, PAIR), 0)
    bias = jnp.where(row < length, 0.0, NEG_FILL)
    keys = k_ref[...].astype(F32)
    values = v_ref[...].astype(F32)
    queries = q_ref[...].astype(F32) * HEAD_DIM**-0.5
    grads = g_ref[...].astype(F32)
    products = grads * o_ref[...].astype(F32)
    d_queries, d_keys, d_values = [], [], []
    for h in range(2):
        mine = (lane // HEAD_DIM) == h
        spare = (1 - h) * HEAD_DIM
        flag = lane == spare
        dots = jnp.sum(jnp.where(mine, products, 0.0), axis=1, keepdims=True)
        high, mid, low = parts(-dots)
        ones = (lane >= spare) & (lane < spare + 3)
        value_ext = jnp.where(mine, values, jnp.where(ones, 1.0, 0.0)).astype(BF)
        tail = jnp.where(
            flag, high, jnp.where(lane == spare + 1, mid, jnp.where(lane == spare + 2, low, 0.0))
        )
        gp[h, 0:slots, :] = jnp.where(mine, grads, tail).astype(BF)
        key_ext = jnp.where(mine, keys, jnp.where(flag, bias, 0.0)).astype(BF)
        qp[h, 0:slots, :] = jnp.where(mine, queries, jnp.where(flag, 1.0, 0.0)).astype(BF)
        if padded > slots:
            gp[h, slots:padded, :] = jnp.zeros((padded - slots, PAIR), BF)
            qp[h, slots:padded, :] = jnp.zeros((padded - slots, PAIR), BF)
        keys_turned = key_ext.T[h * HEAD_DIM : (h + 1) * HEAD_DIM]
        d_key = d_value = None
        d_query = []
        for j in range(padded // tile):
            at = slice(j * tile, (j + 1) * tile)
            weights = jnp.exp(nt(key_ext, qp[h, at, :]) - lse_ref[0, h : h + 1, at])
            d_scores = (weights * nt(value_ext, gp[h, at, :])).astype(BF)
            more_value = nn(weights.astype(BF), gp[h, at, :])
            more_key = nn(d_scores, qp[h, at, :])
            d_value = more_value if d_value is None else d_value + more_value
            d_key = more_key if d_key is None else d_key + more_key
            d_query.append(nn(keys_turned, d_scores))
        d_queries.append(jnp.concatenate(d_query, axis=1))
        d_keys.append(d_key)
        d_values.append(d_value)
    turned = jnp.concatenate(d_queries, axis=0) * HEAD_DIM**-0.5
    dq_ref[...] = turned.T[0:slots].astype(BF)
    dk_ref[...] = jnp.where(lane < HEAD_DIM, d_keys[0], d_keys[1]).astype(BF)
    dv_ref[...] = jnp.where(lane < HEAD_DIM, d_values[0], d_values[1]).astype(BF)


def attend_back(length, proj, grads, mixed, totals, tile=256, first=0, count=None):
    slots = proj.shape[0]
    padded = -(-slots // 128) * 128
    width = proj.shape[1] // 3
    pairs = width // PAIR
    count = pairs if count is None else count

    def spec(off):
        return pl.BlockSpec((slots, PAIR), lambda p, _: (0, off + p))

    return pl.pallas_call(
        functools.partial(attend_back_kernel, slots=slots, padded=padded, tile=tile),
        grid_spec=pltpu.PrefetchScalarGridSpec(
            num_scalar_prefetch=1,
            grid=(count,),
            in_specs=[
                spec(first),
                spec(first + pairs),
                spec(first + 2 * pairs),
                spec(first),
                spec(first),
                pl.BlockSpec((1, 8, padded), lambda p, _: (first + p, 0, 0)),
            ],
            out_specs=[spec(0)] * 3,
            scratch_shapes=[pltpu.VMEM((2, padded, PAIR), BF)] * 2,
        ),
        out_shape=[jax.ShapeDtypeStruct((slots, count * PAIR), BF)] * 3,
        compiler_params=params(),
        cost_estimate=cost(
            2 * count * 20 * slots * slots * PAIR, slots * width * 16, 2 * count * slots * slots
        ),
        name="attend_back",
    )(length, proj, proj, proj, grads, mixed, totals)


def rest_copies(table, halves, downs, w_out, w_up, w_down, sems):
    width = w_out.shape[0]
    narrow = width // BLOCKS
    wide = w_up.shape[0] // BLOCKS
    half = (wide + narrow) // 2
    copies_out, copies_up, copies_down = [], [], []
    for j in range(2 * BLOCKS):
        block = table[j]
        base = j % 2 * half
        size = half if j < BLOCKS else wide - half
        start = block * wide + j // BLOCKS * half
        copies_up.append(
            pltpu.make_async_copy(
                halves[j // 2].at[pl.ds(base, size)],
                w_up.at[pl.ds(pl.multiple_of(start, 16), size)],
                sems.at[j],
            )
        )
        if j >= BLOCKS:
            copies_out.append(
                pltpu.make_async_copy(
                    halves[j // 2].at[pl.ds(base + size, narrow)],
                    w_out.at[pl.ds(pl.multiple_of(block * narrow, 16), narrow)],
                    sems.at[BLOCKS + j],
                )
            )
        for k in range(2):
            plane = table[2 * BLOCKS + j // BLOCKS * 2 + k]
            copies_down.append(
                pltpu.make_async_copy(
                    downs[j // 2].at[pl.ds((j % 2 * 2 + k) * narrow, narrow)],
                    w_down.at[
                        pl.ds(pl.multiple_of(block * narrow, 16), narrow),
                        pl.ds(pl.multiple_of(plane * width, 128), width),
                    ],
                    sems.at[3 * BLOCKS + j * 2 + k],
                )
            )
    return copies_out, copies_up, copies_down


def middle_kernel(len_ref, table, x_ref, mixed_ref, cot_ref, vec_ref, *refs, chunk):
    blocks, downs = refs[:8], refs[8:16]
    (
        out_ref,
        active_ref,
        d_inner_ref,
        normed_ref,
        d_resid_ref,
        d_branch_ref,
        d_mixed_ref,
        sums_ref,
    ) = refs[16:24]
    w_out, w_up, w_down, sems = refs[24:]
    i = pl.program_id(0)
    tile, width = x_ref.shape
    hidden = w_up.shape[0]

    copies_out, copies_up, copies_down = rest_copies(
        table, blocks, downs, w_out, w_up, w_down, sems
    )

    @pl.when(i == 0)
    def _():
        for copy in copies_out + copies_up + copies_down:
            copy.start()
        sums_ref[...] = jnp.zeros_like(sums_ref)
        for copy in copies_out:
            copy.wait()

    residual = x_ref[...].astype(F32) + nt(mixed_ref[...], w_out[...]) + vec_ref[2:3, :]
    nhat, scale = normalise(residual)
    normed = (nhat * vec_ref[6:7, :] + vec_ref[7:8, :]).astype(BF)
    normed_ref[...] = normed
    rows = lax.broadcasted_iota(jnp.int32, (tile, 1), 0) + i * tile
    seed_low = jnp.where(rows < len_ref[0], cot_ref[...], jnp.zeros_like(cot_ref))
    seed = seed_low.astype(F32)
    ones = jnp.ones((8, tile), BF)

    @pl.when(i == 0)
    def _():
        for copy in copies_up + copies_down:
            copy.wait()

    per = width // chunk

    def step(c, carry):
        out_sum, d_normed = carry
        at = pl.ds(pl.multiple_of(c * chunk, chunk), chunk)
        row = pl.ds(8 + c // per, 1)
        lanes = pl.ds(pl.multiple_of(lax.rem(c, per) * chunk, chunk), chunk)
        inner = nt(normed, w_up[at, :]) + vec_ref[row, lanes]
        cdf = 0.5 + 0.5 * lax.erf(inner * 0.5**0.5)
        active = (inner * cdf).astype(BF)
        active_ref[:, at] = active
        d_active = nn(seed_low, w_down[:, at])
        slope = cdf + inner * (jnp.exp(-0.5 * inner * inner) * 0.3989422804014327)
        d_inner = (d_active * slope).astype(BF)
        d_inner_ref[:, at] = d_inner
        sums_ref[row, lanes] += nn(ones, d_inner)[0:1]
        return (out_sum + nt(active, w_down[:, at]), d_normed + nn(d_inner, w_up[at, :]))

    zero = jnp.zeros((tile, width), F32)
    out_sum, d_normed = lax.fori_loop(0, hidden // chunk, step, (zero, zero))
    out_ref[...] = (residual + out_sum + vec_ref[3:4, :]).astype(BF)
    d_resid = seed + norm_back(d_normed, nhat, scale, vec_ref[6:7, :])
    d_resid_ref[...] = d_resid
    d_branch = d_resid.astype(BF)
    d_branch_ref[...] = d_branch
    d_mixed_ref[...] = nn(d_branch, w_out[...]).astype(BF)
    sums_ref[2:3, :] += jnp.sum(d_resid, axis=0, keepdims=True)
    sums_ref[3:4, :] += jnp.sum(seed, axis=0, keepdims=True)
    sums_ref[6:7, :] += jnp.sum(d_normed * nhat, axis=0, keepdims=True)
    sums_ref[7:8, :] += jnp.sum(d_normed, axis=0, keepdims=True)


def middle(length, table, x, mixed, cot, vec, blocks, downs, hidden, tile, chunk=768):
    slots, width = x.shape

    def rows(columns):
        return pl.BlockSpec((tile, columns), lambda i, *_: (i, 0))

    return pl.pallas_call(
        functools.partial(middle_kernel, chunk=chunk),
        grid_spec=pltpu.PrefetchScalarGridSpec(
            num_scalar_prefetch=2,
            grid=(slots // tile,),
            in_specs=[rows(width)] * 3 + [whole(vec.shape)] + [ANY] * 16,
            out_specs=[
                rows(width),
                rows(hidden),
                rows(hidden),
                rows(width),
                rows(width),
                rows(width),
                rows(width),
                whole(vec.shape),
            ],
            scratch_shapes=[
                pltpu.VMEM((width, width), BF),
                pltpu.VMEM((hidden, width), BF),
                pltpu.VMEM((width, hidden), BF),
                pltpu.SemaphoreType.DMA((7 * BLOCKS,)),
            ],
        ),
        out_shape=[
            jax.ShapeDtypeStruct((slots, width), BF),
            jax.ShapeDtypeStruct((slots, hidden), BF),
            jax.ShapeDtypeStruct((slots, hidden), BF),
            jax.ShapeDtypeStruct((slots, width), BF),
            jax.ShapeDtypeStruct((slots, width), F32),
            jax.ShapeDtypeStruct((slots, width), BF),
            jax.ShapeDtypeStruct((slots, width), BF),
            jax.ShapeDtypeStruct(vec.shape, F32),
        ],
        compiler_params=params(),
        cost_estimate=cost(
            2 * slots * width * (4 * hidden + 2 * width),
            slots * (hidden * 4 + width * 18) + hidden * width * 4,
            2 * slots * hidden,
        ),
        name="middle",
    )(length, table, x, mixed, cot, vec, *blocks, *downs)


def deliver(copies):
    for copy in copies:
        copy.start()
    for copy in copies:
        copy.wait()


def down_grads_kernel(len_ref, table, active_ref, cot_ref, keep_ref, send_ref, sums, sems):
    z = pl.program_id(0)
    slots, width = cot_ref.shape
    narrow = width // BLOCKS
    rows = lax.broadcasted_iota(jnp.int32, (slots, 1), 0)
    seed = jnp.where(rows < len_ref[0], cot_ref[...], jnp.zeros_like(cot_ref))
    sums[z] = tn(seed, active_ref[...]).astype(BF)

    @pl.when(z == pl.num_programs(0) - 1)
    def _():
        copies = []
        for j in range(BLOCKS):
            target = keep_ref if j < 4 else send_ref
            at = pl.ds(pl.multiple_of(table[j] * narrow, 16), narrow)
            for k in range(4):
                copies.append(
                    pltpu.make_async_copy(
                        sums.at[table[2 * BLOCKS + PLANES[k]], at],
                        target.at[k, j % 4],
                        sems.at[j * 4 + k],
                    )
                )
        deliver(copies)


def down_grads(length, table, active, cot):
    slots, width = cot.shape
    hidden = active.shape[1]
    out = jax.ShapeDtypeStruct((4, 4, width // BLOCKS, width), BF)
    return pl.pallas_call(
        down_grads_kernel,
        grid_spec=pltpu.PrefetchScalarGridSpec(
            num_scalar_prefetch=2,
            grid=(hidden // width,),
            in_specs=[pl.BlockSpec((slots, width), lambda z, *_: (0, z)), whole((slots, width))],
            out_specs=[ANY] * 2,
            scratch_shapes=[
                pltpu.VMEM((4, width, width), BF),
                pltpu.SemaphoreType.DMA((4 * BLOCKS,)),
            ],
        ),
        out_shape=[out, out],
        compiler_params=params(),
        cost_estimate=cost(2 * slots * width * hidden, slots * hidden * 2 + out.size * 4),
        name="down_grads",
    )(length, table, active, cot)


def up_grads_kernel(
    table, d_inner_ref, normed_ref, d_branch_ref, mixed_ref, keep_ref, send_ref, sums, sems
):
    z = pl.program_id(0)
    slots, width = normed_ref.shape
    narrow = width // BLOCKS
    wide = sums.shape[1] - narrow
    up = tn(d_inner_ref[...], normed_ref[...]).astype(BF)
    per = width // wide
    for j in range(per):
        sums[z * per + j, 0:wide, :] = up[j * wide : (j + 1) * wide]

    @pl.when(z == 0)
    def _():
        out = tn(d_branch_ref[...], mixed_ref[...]).astype(BF)
        for g in range(BLOCKS):
            sums[g, wide : wide + narrow, :] = out[g * narrow : (g + 1) * narrow]

    @pl.when(z == pl.num_programs(0) - 1)
    def _():
        deliver(
            [
                pltpu.make_async_copy(
                    sums.at[table[j]], (keep_ref if j < 4 else send_ref).at[j % 4], sems.at[j]
                )
                for j in range(BLOCKS)
            ]
        )


def up_grads(table, d_inner, normed, d_branch, mixed):
    slots, width = normed.shape
    hidden = d_inner.shape[1]
    rows = hidden // BLOCKS + width // BLOCKS
    out = jax.ShapeDtypeStruct((4, rows, width), BF)
    return pl.pallas_call(
        up_grads_kernel,
        grid_spec=pltpu.PrefetchScalarGridSpec(
            num_scalar_prefetch=1,
            grid=(hidden // width,),
            in_specs=[pl.BlockSpec((slots, width), lambda z, *_: (0, z))]
            + [whole((slots, width))] * 3,
            out_specs=[ANY] * 2,
            scratch_shapes=[
                pltpu.VMEM((BLOCKS, rows, width), BF),
                pltpu.SemaphoreType.DMA((BLOCKS,)),
            ],
        ),
        out_shape=[out, out],
        compiler_params=params(),
        cost_estimate=cost(
            2 * slots * width * (hidden + width), slots * hidden * 2 + out.size * 4
        ),
        name="up_grads",
    )(table, d_inner, normed, d_branch, mixed)


def qkv_grads_kernel(table, *refs):
    parts_in, normed_ref, (keep_ref, send_ref, sums, sems) = refs[:-5], refs[-5], refs[-4:]
    width = normed_ref.shape[1]
    block = sums.shape[0] // BLOCKS
    groups = len(parts_in) // 3
    for s in range(3):
        start = s * width
        for i in range(groups):
            ref = parts_in[i * 3 + s]
            sums[start : start + ref.shape[1], :] = tn(ref[...], normed_ref[...]).astype(BF)
            start += ref.shape[1]
    deliver(
        [
            pltpu.make_async_copy(
                sums.at[pl.ds(pl.multiple_of(table[j] * block, 16), block)],
                (keep_ref if j < 4 else send_ref).at[j % 4],
                sems.at[j],
            )
            for j in range(BLOCKS)
        ]
    )


def qkv_grads(table, d_parts, normed):
    slots, width = normed.shape
    out = jax.ShapeDtypeStruct((4, 3 * width // BLOCKS, width), BF)
    return pl.pallas_call(
        qkv_grads_kernel,
        grid_spec=pltpu.PrefetchScalarGridSpec(
            num_scalar_prefetch=1,
            grid=(1,),
            in_specs=[whole(part.shape) for part in d_parts] + [whole((slots, width))],
            out_specs=[ANY] * 2,
            scratch_shapes=[
                pltpu.VMEM((3 * width, width), BF),
                pltpu.SemaphoreType.DMA((BLOCKS,)),
            ],
        ),
        out_shape=[out, out],
        compiler_params=params(),
        cost_estimate=cost(6 * slots * width * width, slots * width * 8 + out.size * 4),
        name="qkv_grads",
    )(table, *d_parts, normed)


def last_kernel(table, x_ref, d_resid_ref, vec_ref, sums_in, *refs, groups):
    parts_in, blocks = refs[: 3 * groups], refs[3 * groups : 3 * groups + 8]
    grad_ref, sums_ref, weights, sems = refs[3 * groups + 8 :]
    i = pl.program_id(0)
    tile, width = x_ref.shape
    copies = qkv_copies(table, blocks, weights, sems)

    @pl.when(i == 0)
    def _():
        for copy in copies:
            copy.start()
        sums_ref[...] = sums_in[...]
        for copy in copies:
            copy.wait()

    ones = jnp.ones((8, tile), BF)
    d_normed = jnp.zeros((tile, width), F32)
    for s in range(3):
        start = 0
        for j in range(groups):
            ref = parts_in[j * 3 + s]
            end = start + ref.shape[1]
            d_normed += nn(ref[...], weights[s * width + start : s * width + end, :])
            if s != 1:
                row = s // 2
                sums_ref[row : row + 1, start:end] += nn(ones, ref[...])[0:1]
            start = end
    nhat, scale = normalise(x_ref[...].astype(F32))
    grad_ref[...] = d_resid_ref[...] + norm_back(d_normed, nhat, scale, vec_ref[4:5, :])
    sums_ref[4:5, :] += jnp.sum(d_normed * nhat, axis=0, keepdims=True)
    sums_ref[5:6, :] += jnp.sum(d_normed, axis=0, keepdims=True)


def last(table, d_parts, x, d_resid, vec, sums, blocks, tile):
    slots, width = x.shape

    def rows(columns):
        return pl.BlockSpec((tile, columns), lambda i, _: (i, 0))

    return pl.pallas_call(
        functools.partial(last_kernel, groups=len(d_parts) // 3),
        grid_spec=pltpu.PrefetchScalarGridSpec(
            num_scalar_prefetch=1,
            grid=(slots // tile,),
            in_specs=[rows(width)] * 2
            + [whole(vec.shape)] * 2
            + [rows(part.shape[1]) for part in d_parts]
            + [ANY] * 8,
            out_specs=[rows(width), whole(vec.shape)],
            scratch_shapes=[
                pltpu.VMEM((3 * width, width), BF),
                pltpu.SemaphoreType.DMA((2 * BLOCKS,)),
            ],
        ),
        out_shape=[
            jax.ShapeDtypeStruct((slots, width), F32),
            jax.ShapeDtypeStruct(vec.shape, F32),
        ],
        compiler_params=params(),
        cost_estimate=cost(6 * slots * width * width, slots * width * 16),
        name="last",
    )(table, x, d_resid, vec, sums, *d_parts, *blocks)


def fold_kernel(table, *refs):
    terms, outs, turned = refs[:4], refs[4:-1], refs[-1]
    rows = turned.shape[0] // 4
    total = terms[0][...].astype(F32)
    for term in terms[1:]:
        total += term[...].astype(F32)
    turned[...] = total.T

    def plane(k):
        return turned[pl.ds(pl.multiple_of(table[2 * BLOCKS + k] * rows, 8), rows), :]

    if len(outs) == 4:
        for k in range(4):
            outs[k][...] = plane(k).astype(outs[k].dtype)
    else:
        for k in range(4):
            outs[k // 2][k % 2] = plane(PLANES[k]).astype(outs[k // 2].dtype)


def fold(table, terms, paired):
    columns, width = terms[0].shape
    shape = (width // 4, columns)
    if paired:
        out = [jax.ShapeDtypeStruct((2, *shape), dtype) for dtype in (F32, BF)]
    else:
        out = [jax.ShapeDtypeStruct(shape, dtype) for dtype in (F32, BF, BF, BF)]
    return pl.pallas_call(
        fold_kernel,
        grid_spec=pltpu.PrefetchScalarGridSpec(
            num_scalar_prefetch=1,
            grid=(1,),
            in_specs=[whole(terms[0].shape)] * 4,
            out_specs=[whole(o.shape) for o in out],
            scratch_shapes=[pltpu.VMEM((width, columns), F32)],
        ),
        out_shape=out,
        compiler_params=params(),
        cost_estimate=cost(1e6, columns * width * 12),
        name="fold",
    )(table, *terms)


def swap(values, axis, mask, size):
    return lax.ppermute(values, axis, [(i, i ^ mask) for i in range(size)])


def in_turn(*values):
    return lax.optimization_barrier(values)


def gather_planes(message):
    return [message] + [swap(message, "gx", k, 4) for k in (1, 2, 3)]


def near(first, second):
    return swap(first, "gy", 2, BLOCKS), swap(second, "gy", 4, BLOCKS)


def far(first, second):
    return swap(first, "gy", 4, BLOCKS), swap(second, "gy", 2, BLOCKS)


def join(first, second):
    return jnp.concatenate([first, second], axis=0)


def with_cores(a, b, a_far, b_far):
    a_core, b_core, a_other, b_other = [swap(v, "gy", 1, BLOCKS) for v in (a, b, a_far, b_far)]
    return [a, a_far, a_core, a_other, b, b_far, b_core, b_other]


def add(*terms):
    total = terms[0].astype(F32)
    for term in terms[1:]:
        total = total + term.astype(F32)
    return total


def per_device(
    patches,
    lengths,
    cotangent,
    w_qkv,
    w_out,
    w_up,
    w_down,
    bias_q,
    bias_v,
    bias_o,
    bias_up,
    bias_down,
    gain_one,
    shift_one,
    gain_two,
    shift_two,
    *,
    planes,
    columns,
):
    slots, width = patches.shape
    hidden = w_up.shape[1] * columns
    wide, narrow = hidden // BLOCKS, width // BLOCKS
    tile = slots // 3
    z, g = lax.axis_index("gx"), lax.axis_index("gy")
    fast = planes == 4 and columns == BLOCKS
    vectors = (bias_q, bias_v, bias_o, bias_down, gain_one, shift_one, gain_two, shift_two)
    if fast:
        pos = jnp.stack([z, g]).astype(jnp.int32)
        table = jnp.concatenate(
            [g ^ jnp.array(MASKS_A), g ^ jnp.array(MASKS_B), z ^ jnp.arange(4)]
        ).astype(jnp.int32)
        message = pack(w_qkv, vectors + (bias_up,))
        message, *rest = in_turn(message, w_up, w_out, w_down)
        pieces = gather_planes(message)
        both, down = pack_rest(*rest)
        qa, qb = arrange_qkv(pos, pieces, width)
        qa, qb, both = in_turn(qa, qb, both)
        qa_near, qb_near = near(qa, qb)
        pieces = gather_planes(both)
        qa, qb = join(qa, qa_near), join(qb, qb_near)
        qa_far, qb_far = far(qa, qb)
        ra, rb = arrange_rest(pos, pieces, width, wide + narrow)
        ra, rb, down = in_turn(ra, rb, down)
        qa, qb, qa_far, qb_far, ra = in_turn(qa, qb, qa_far, qb_far, ra)
        qkv_blocks = with_cores(qa, qb, qa_far, qb_far)
        ra_near, rb_near = near(ra, rb)
        down_planes = gather_planes(down)
    else:

        def everything(shard):
            return lax.all_gather(
                lax.all_gather(shard, "gx", axis=0, tiled=True), "gy", axis=1, tiled=True
            ).T

        order = jnp.arange(BLOCKS)
        table = jnp.concatenate([order, order, jnp.arange(4)]).astype(jnp.int32)
        aux = [lax.all_gather(v, AXES, axis=0, tiled=True)[None] for v in vectors]
        aux.append(lax.all_gather(bias_up, AXES, axis=0, tiled=True).reshape(4, width))
        aux.append(jnp.zeros((AUX - 12, width), BF))
        none = jnp.zeros((BLOCKS - 1, AUX, width), BF)
        aux = jnp.concatenate([jnp.concatenate(aux)[None], none])

        def halved(blocks, extra=None):
            half = blocks.shape[1] // 2
            first = blocks[:, :half]
            if extra is not None:
                first = jnp.concatenate([first, extra], axis=1)
            second = blocks[:, half:]
            return list(first.reshape(4, -1, width)) + list(second.reshape(4, -1, width))

        qkv_blocks = halved(everything(w_qkv).reshape(BLOCKS, -1, width), aux)
        up = everything(w_up).reshape(BLOCKS, wide, width)
        out = everything(w_out).reshape(BLOCKS, narrow, width)
        rest_blocks = halved(jnp.concatenate([up, out], axis=1))
        down = everything(w_down).reshape(BLOCKS, narrow, 4, width)
        downs = halved(jnp.transpose(down, (0, 2, 1, 3)).reshape(BLOCKS, wide, width))

    proj, normed, vec = project(table, patches, qkv_blocks)
    if fast:
        ra_near, rb_near, length, proj = in_turn(ra_near, rb_near, lengths, proj)
        ra, rb = join(ra, ra_near), join(rb, rb_near)
        da, db = join(*down_planes[:2]), join(*down_planes[2:])
        length, ra, rb, da, db = in_turn(length, ra, rb, da, db)
        ra_far, rb_far = far(ra, rb)
        da_near, db_near = near(da, db)
        half = HEADS // 4
        mixed, totals = attend(length, proj, 0, half)
        mixed, totals, da_near, db_near = in_turn(mixed, totals, da_near, db_near)
        da, db = join(da, da_near), join(db, db_near)
        length, da, db, mixed, totals = in_turn(length, da, db, mixed, totals)
        da_far, db_far = far(da, db)
        mixed, totals = attend(length, proj, half, half, (mixed, totals))
        mixed, ra, rb, ra_far, rb_far, da, db, da_far, db_far = in_turn(
            mixed, ra, rb, ra_far, rb_far, da, db, da_far, db_far
        )
        rest_blocks = with_cores(ra, rb, ra_far, rb_far)
        downs = with_cores(da, db, da_far, db_far)
    else:
        mixed, totals = attend(lengths, proj)
    out_rows, active, d_inner, normed_two, d_resid, d_branch, d_mixed, sums = middle(
        lengths, table, patches, mixed, cotangent, vec, rest_blocks, downs, hidden, tile
    )
    down_keep, down_send = down_grads(lengths, table, active, cotangent)
    down_keep, down_send, d_inner = in_turn(down_keep, down_send, d_inner)
    up_keep, up_send = up_grads(table, d_inner, normed_two, d_branch, mixed)

    def back(length, first, count):
        return list(
            attend_back(length, proj, d_mixed, mixed, totals, first=first, count=count)
        )

    if fast:
        down_got = swap(down_send, "gy", 1, BLOCKS)
        up_got = swap(up_send, "gy", 1, BLOCKS)
        down_keep, down_got, up_keep = in_turn(down_keep, down_got, up_keep)
        down_next = add(down_keep[2:], down_got[2:]).astype(BF)
        length, down_next = in_turn(lengths, down_next)
        down_near = swap(down_next, "gx", 1, 4)
        d_parts = back(length, 0, 2)
        d_parts[0], up_keep, up_got = in_turn(d_parts[0], up_keep, up_got)
        up_sums = [add(up_keep[r], up_got[r]).astype(BF) for r in range(4)]
        length, *up_sums = in_turn(length, *up_sums)
        up_blocks = [swap(up_sums[r], "gy", MASKS_A[r], BLOCKS) for r in (1, 2, 3)]
        more = back(length, 2, 1)
        more[0], down_near, down_keep = in_turn(more[0], down_near, down_keep)
        d_parts += more
        down_sum = add(down_keep[0], down_got[0], down_near[0])
        down_next = add(down_keep[1], down_got[1], down_near[1]).astype(BF)
        length, down_next, down_sum = in_turn(length, down_next, down_sum)
        down_far = swap(down_next, "gx", 2, 4)
        more = back(length, 3, 3)
        more[0], down_far, *up_blocks = in_turn(more[0], down_far, *up_blocks)
        d_parts += more
        down_sums = [add(down_sum[r], down_far[r]).astype(BF) for r in range(4)]
        up_keep, up_send = fold(table, up_sums[:1] + up_blocks, True)
        table, up_keep, up_send, *down_sums = in_turn(table, up_keep, up_send, *down_sums)
        down_blocks = [swap(down_sums[r], "gy", MASKS_A[r], BLOCKS) for r in (1, 2, 3)]
        up_near = swap(up_send, "gx", 1, 4)
        qkv_keep, qkv_send = qkv_grads(table, d_parts, normed)
        qkv_keep, qkv_send, up_near, *down_blocks = in_turn(
            qkv_keep, qkv_send, up_near, *down_blocks
        )
        qkv_got = swap(qkv_send, "gy", 1, BLOCKS)
        grad_down = add(down_sums[0], *down_blocks).T
        up_sum = add(up_keep[0], up_near[0])
        up_next = add(up_keep[1], up_near[1]).astype(BF)
        qkv_keep, qkv_got, up_next = in_turn(qkv_keep, qkv_got, up_next)
        up_far = swap(up_next, "gx", 2, 4)
        qkv_sums = [add(qkv_keep[r], qkv_got[r]).astype(BF) for r in range(4)]
        table, grad_down, *qkv_sums = in_turn(table, grad_down, *qkv_sums)
        qkv_got = [swap(qkv_sums[r], "gy", MASKS_A[r], BLOCKS) for r in (1, 2, 3)]
        grad_rows, sums = last(table, d_parts, patches, d_resid, vec, sums, qkv_blocks, tile)
        up_far, sums = in_turn(up_far, sums)
        up_sum = add(up_sum, up_far)
        grad_up, grad_out = up_sum[:, :wide], up_sum[:, wide:]
        steps = (("gy", 1, 8), ("gy", 2, 8), ("gy", 4, 8), ("gx", 1, 4), ("gx", 2, 4))
        for axis, mask, size in steps[:2]:
            sums = sums + swap(sums, axis, mask, size)
        table, sums = in_turn(table, sums)
        qkv_pieces = fold(table, qkv_sums[:1] + qkv_got, False)
        sums, *qkv_pieces = in_turn(sums, *qkv_pieces)
        qkv_planes = [swap(qkv_pieces[k], "gx", k, 4) for k in (1, 2, 3)]
        for axis, mask, size in steps[2:]:
            sums = sums + swap(sums, axis, mask, size)
        sums, *qkv_planes = in_turn(sums, *qkv_planes)
        grad_qkv = add(qkv_pieces[0], *qkv_planes)
        device = z * columns + g
        own = lax.dynamic_slice(sums, (0, device * (narrow // 4)), (8, narrow // 4))
        own_up = lax.dynamic_slice(sums, (8 + z, g * narrow), (1, narrow))[0]
        own = [own[j] for j in range(8)]
    else:
        d_parts = back(lengths, 0, 2) + back(lengths, 2, 1) + back(lengths, 3, 3)
        qkv_keep, qkv_send = qkv_grads(table, d_parts, normed)
        grad_rows, sums = last(table, d_parts, patches, d_resid, vec, sums, qkv_blocks, tile)

        def spread(grads):
            part = lax.psum_scatter(grads, "gy", scatter_dimension=0, tiled=True)
            return lax.psum_scatter(part.T, "gx", scatter_dimension=0, tiled=True).astype(F32)

        rest = jnp.concatenate([up_keep, up_send], axis=0)
        grad_up = spread(rest[:, :wide].reshape(hidden, width))
        grad_out = spread(rest[:, wide:].reshape(width, width))
        down = jnp.stack([down_keep, down_send])[:, jnp.array(PLANES)]
        grad_down = spread(jnp.transpose(down, (0, 2, 3, 1, 4)).reshape(width, hidden))
        grad_qkv = spread(jnp.concatenate([qkv_keep, qkv_send]).reshape(3 * width, width))

        def share(vector):
            return lax.psum_scatter(vector, AXES, scatter_dimension=0, tiled=True)

        own = [share(sums[j]) for j in range(8)]
        own_up = share(sums[8:12].reshape(hidden))

    return (
        out_rows,
        grad_rows,
        grad_qkv,
        grad_out,
        grad_up,
        grad_down,
        own[0],
        own[1],
        own[2],
        own_up,
        own[3],
        own[4],
        own[5],
        own[6],
        own[7],
    )


def solution(mesh):
    by_rows = P(AXES, None)
    by_parts = P(AXES)
    matrix = P("gx", "gy")
    in_specs = (by_rows, by_parts, by_rows) + (matrix,) * 4 + (by_parts,) * 9
    out_specs = (by_rows, by_rows) + (matrix,) * 4 + (by_parts,) * 9
    body = functools.partial(per_device, planes=mesh.shape["gx"], columns=mesh.shape["gy"])
    return jax.shard_map(body, mesh=mesh, in_specs=in_specs, out_specs=out_specs, check_vma=False)
```

time: 434 us -> 378 us (0.87); the launches traced: 425 us -> 374 us
  waiting for transfers between devices: 119 us -> 60.8 us
  Pallas kernels: 199 us -> 222 us
  other arithmetic: 24.4 us -> 16.7 us
  starting transfers between devices: 61.2 us -> 56.4 us
    ppermute x49 -> x57, waiting for transfers between devices: 119 us -> 60.8 us  [swap(): return lax.ppermute(values, axis, [(i, i ^ mask) for i in range(size)])]
    pallas_call x2 -> x7, Pallas kernels: 37.6 us -> 53.8 us  [the longest x1 15.5 us: up_grads(): pl.pallas_call(up_grads_kernel, grid_spec=pltpu.PrefetchScalarGridSpec(nu...]
    unnamed x60 -> x82, local copies, waits for them, and re-layouts: 4.67 us -> 11.6 us
    concatenate x7 -> x2, local copies, waits for them, and re-layouts: 6.38 us -> 0.03 us  [join(): return jnp.concatenate([first, second], axis=0)]
    pallas_call x1 -> x3, Pallas kernels: 52.9 us -> 58 us  [attend_back(): pl.pallas_call(functools.partial(attend_back_kernel, slots=slots, padded=...]
    ppermute x49 -> x57, starting transfers between devices: 61.2 us -> 56.4 us  [swap(): return lax.ppermute(values, axis, [(i, i ^ mask) for i in range(size)])]
    convert_element_type x8 -> x5, other arithmetic: 7.59 us -> 9.84 us  [the longest x1 3.97 us: per_device(): up_sums = [add(up_keep[r], up_got[r]).astype(BF) for r in range(4)]]
    pallas_call x1 -> x2, Pallas kernels: 27.6 us -> 29.7 us  [attend(): pl.pallas_call(functools.partial(attend_kernel, slots=slots, padded=padde...]
  transfers between devices with their start and end apart: 49 -> 57, of which waited for: 17 -> 16; matrix products, arithmetic and copies ran while one was open for 6% -> 5% of each run, Pallas kernels for 29% -> 39%
where the time goes in v2:
time: 378 us; the launch traced here: 374 us
  Pallas kernels  222 us (59%)
  waiting for transfers between devices  60.8 us (16%)
  starting transfers between devices  56.4 us (15%)
  other arithmetic  16.7 us (4%)
  local copies, waits for them, and re-layouts  15.9 us (4%)
    ppermute x57, waiting for transfers between devices, swap(): return lax.ppermute(values, axis, [(i, i ^ mask) for i in range(size)])  60.8 us
    pallas_call x3, Pallas kernels, attend_back(): pl.pallas_call(functools.partial(attend_back_kernel, slots=slots, padded=...  58 us
    ppermute x57, starting transfers between devices, swap(): return lax.ppermute(values, axis, [(i, i ^ mask) for i in range(size)])  56.4 us
    pallas_call x1, Pallas kernels, middle(): pl.pallas_call(functools.partial(middle_kernel, chunk=chunk), grid_spec=p...  50.4 us
    pallas_call x2, Pallas kernels, attend(): pl.pallas_call(functools.partial(attend_kernel, slots=slots, padded=padde...  29.7 us
    pallas_call x1, Pallas kernels, up_grads(): pl.pallas_call(up_grads_kernel, grid_spec=pltpu.PrefetchScalarGridSpec(nu...  15.5 us
    pallas_call x1, Pallas kernels, last(): pl.pallas_call(functools.partial(last_kernel, groups=len(d_parts) // 3),...  15 us
    pallas_call x1, Pallas kernels, project(): pl.pallas_call(project_kernel, grid_spec=pltpu.PrefetchScalarGridSpec(num...  12.7 us
  transfers between devices with their start and end apart: 57, of which 16 were waited for; matrix products, arithmetic and copies ran while one was open for 5% of the time, Pallas kernels for 39%

profile of v2, /device:TPU:0, one launch (start us, length us, event | category | flops | bytes accessed | tf_op | source)
XLA Modules:
  0.0 374.0 jit_solution(14173102443447437846)
XLA Ops:
  12.1 7.9 %collective-permute-done.1.refs_2_ = bf16[200,288]{1,0:T(8,128)(2,1)S(1)} collective-permute-done((bf16[200,288]{1,0:T(8,128)(2,1)}, bf16[200,288]{1,0:T(8,128)(2,1)S(1)}, u32[]{:S(2)}, u32[]{:S(2)}) %collective-permute-start.1) | collective-permute-done | bytes 115232 | tf_op jit(solution)/shard_map/ppermute | solution.py:888
  21.3 3.6 arrange_qkv.1
  42.1 9.8 %collective-permute-done.8.refs_2_ = bf16[192,512]{1,0:T(8,128)(2,1)S(1)} collective-permute-done((bf16[192,512]{1,0:T(8,128)(2,1)S(1)}, bf16[192,512]{1,0:T(8,128)(2,1)S(1)}, u32[]{:S(2)}, u32[]{:S(2)}) %collective-permute-start.8) | collective-permute-done | bytes 196640 | tf_op jit(solution)/shard_map/ppermute | solution.py:888
  56.4 3.4 collective-permute-start.17
  60.6 5.3 %collective-permute-done.17 = bf16[96,768]{1,0:T(8,128)(2,1)S(1)} collective-permute-done((bf16[96,768]{1,0:T(8,128)(2,1)S(1)}, bf16[96,768]{1,0:T(8,128)(2,1)S(1)}, u32[]{:S(2)}, u32[]{:S(2)}) %collective-permute-start.17) | collective-permute-done | bytes 147488 | tf_op jit(solution)/shard_map/ppermute | solution.py:888
  68.7 5.3 %collective-permute-done.18 = bf16[96,768]{1,0:T(8,128)(2,1)S(1)} collective-permute-done((bf16[96,768]{1,0:T(8,128)(2,1)S(1)}, bf16[96,768]{1,0:T(8,128)(2,1)S(1)}, u32[]{:S(2)}, u32[]{:S(2)}) %collective-permute-start.18) | collective-permute-done | bytes 147488 | tf_op jit(solution)/shard_map/ppermute | solution.py:888
  77.0 12.7 %project.1 = (bf16[1224,2304]{1,0:T(8,128)(2,1)}, bf16[1224,768]{1,0:T(8,128)(2,1)}, f32[16,768]{1,0:T(8,128)}) custom-call(s32[20]{0:T(128)} %pad_add_fusion.table, bf16[1224,768]{1,0:T(8,128)(2,1)} %x_ref.5, bf16[320,768]{1,0:T(8,128)(2,1)} %copy-done.25, bf16[320,768]{1,0:T(8,128)(2,1)} %copy-done.36, bf16[320,768]{1,0:T(8,128)(2,1)} %copy-done.37, ...), custom_call_target="tpu_custom_call" | custom-call | flops 4331667456 | bytes 9400320 | tf_op jit(solution)/shard_map/project/pallas_call | solution.py:262
  94.9 14.7 %attend.2 = (bf16[1224,768]{1,0:T(8,128)(2,1)}, f32[6,8,1280]{2,1,0:T(8,128)}) custom-call(s32[1]{0:T(128)S(6)} %copy.40.len_ref, bf16[1224,2304]{1,0:T(8,128)(2,1)} %get-tuple-element.190.q_ref.k_ref.v_ref, bf16[1224,2304]{1,0:T(8,128)(2,1)} %get-tuple-element.190.q_ref.k_ref.v_ref, bf16[1224,2304]{1,0:T(8,128)(2,1)} %get-tuple-element.190.q_ref.k_ref.v_ref), custom_call_target="tpu_custom_call" | custom-call | flops 9204793344 | bytes 7520256 | tf_op jit(solution)/shard_map/attend/pallas_call | solution.py:329
  112.5 14.9 %attend.3 = (bf16[1224,768]{1,0:T(8,128)(2,1)}, f32[6,8,1280]{2,1,0:T(8,128)}) custom-call(s32[1]{0:T(128)S(6)} %copy.40.len_ref, bf16[1224,2304]{1,0:T(8,128)(2,1)} %get-tuple-element.190.q_ref.k_ref.v_ref, bf16[1224,2304]{1,0:T(8,128)(2,1)} %get-tuple-element.190.q_ref.k_ref.v_ref, ...), custom_call_target="tpu_custom_call", output_to_operand_aliasing={{0}: (4, {}), {1}: (5, {})} | custom-call | flops 9204793344 | bytes 7520256 | tf_op jit(solution)/shard_map/attend/pallas_call | solution.py:329
  132.0 4.6 %collective-permute-done.32.refs_15_ = bf16[384,768]{1,0:T(8,128)(2,1)S(1)} collective-permute-done((bf16[384,768]{1,0:T(8,128)(2,1)}, bf16[384,768]{1,0:T(8,128)(2,1)S(1)}, u32[]{:S(2)}, u32[]{:S(2)}) %collective-permute-start.32) | collective-permute-done | bytes 589856 | tf_op jit(solution)/shard_map/ppermute | solution.py:888
  139.2 50.4 %middle.1 = (bf16[1224,768]{1,0:T(8,128)(2,1)}, bf16[1224,3072]{1,0:T(8,128)(2,1)}, bf16[1224,3072]{1,0:T(8,128)(2,1)}, bf16[1224,768]{1,0:T(8,128)(2,1)}, f32[1...) custom-call(s32[1]{0:T(128)S(6)} %copy.40.len_ref, ...), custom_call_target="tpu_custom_call" | custom-call | flops 25990004736 | bytes 41398272 | tf_op jit(solution)/shard_map/middle/pallas_call | solution.py:581
  189.7 12.3 %down_grads.1 = (bf16[4,4,96,768]{3,2,1,0:T(8,128)(2,1)}, bf16[4,4,96,768]{3,2,1,0:T(8,128)(2,1)}) custom-call(s32[1]{0:T(128)S(6)} %copy.40.len_ref, s32[20]{0:T(128)} %pad_add_fusion.table, bf16[1224,3072]{1,0:T(8,128)(2,1)} %get-tuple-element.217.active_ref, bf16[1224,768]{1,0:T(8,128)(2,1)} %cot_ref.3), custom_call_target="tpu_custom_call" | custom-call | flops 5775556608 | bytes 12238848 | tf_op jit(solution)/shard_map/down_grads/pallas_call | solution.py:660
  202.2 15.5 %up_grads.1 = (bf16[4,480,768]{2,1,0:T(8,128)(2,1)}, bf16[4,480,768]{2,1,0:T(8,128)(2,1)}) custom-call(s32[20]{0:T(128)} %pad_add_fusion.table, bf16[1224,3072]{1,0:T(8,128)(2,1)} %get-tuple-element.223.d_inner_ref, bf16[1224,768]{1,0:T(8,128)(2,1)} %get-tuple-element.224.normed_ref, bf16[1224,768]{1,0:T(8,128)(2,1)} %get-tuple-element.225.d_branch_ref, ...), custom_call_target="tpu_custom_call" | custom-call | flops 7219445760 | bytes 13418496 | tf_op jit(solution)/shard_map/up_grads/pallas_call | solution.py:714
  221.5 19.5 %attend_back.3 = (bf16[1224,256]{1,0:T(8,128)(2,1)}, bf16[1224,256]{1,0:T(8,128)(2,1)}, bf16[1224,256]{1,0:T(8,128)(2,1)}) custom-call(s32[1]{0:T(128)S(6)} %copy.40.len_ref, bf16[1224,2304]{1,0:T(8,128)(2,1)} %get-tuple-element.190.q_ref.k_ref.v_ref, bf16[1224,2304]{1,0:T(8,128)(2,1)} %get-tuple-element.190.q_ref.k_ref.v_ref, ...), custom_call_target="tpu_custom_call" | custom-call | flops 15341322240 | bytes 15040512 | tf_op jit(solution)/shard_map/attend_back/pallas_call | solution.py:434
  241.0 10.6 %attend_back.4 = (bf16[1224,128]{1,0:T(8,128)(2,1)}, bf16[1224,128]{1,0:T(8,128)(2,1)}, bf16[1224,128]{1,0:T(8,128)(2,1)}) custom-call(s32[1]{0:T(128)S(6)} %copy.40.len_ref, bf16[1224,2304]{1,0:T(8,128)(2,1)} %get-tuple-element.190.q_ref.k_ref.v_ref, bf16[1224,2304]{1,0:T(8,128)(2,1)} %get-tuple-element.190.q_ref.k_ref.v_ref, ...), custom_call_target="tpu_custom_call" | custom-call | flops 7670661120 | bytes 15040512 | tf_op jit(solution)/shard_map/attend_back/pallas_call | solution.py:434
  251.7 4.0 %fusion.3 = (bf16[480,768]{1,0:T(8,128)(2,1)}, bf16[480,768]{1,0:T(8,128)(2,1)}, bf16[480,768]{1,0:T(8,128)(2,1)}, bf16[480,768]{1,0:T(8,128)(2,1)}) fusion(bf16[4,480,768]{2,1,0:T(8,128)(2,1)} %collective-permute-done.34, bf16[4,480,768]{2,1,0:T(8,128)(2,1)S(1)} %copy-done), kind=kLoop, calls=%fused_computation.14 | loop fusion | flops 5898240 | bytes 8847360 | tf_op jit(solution)/shard_map/convert_element_type | solution.py:1045
  262.4 27.8 %attend_back.5 = (bf16[1224,384]{1,0:T(8,128)(2,1)}, bf16[1224,384]{1,0:T(8,128)(2,1)}, bf16[1224,384]{1,0:T(8,128)(2,1)}) custom-call(s32[1]{0:T(128)S(6)} %copy.40.len_ref, bf16[1224,2304]{1,0:T(8,128)(2,1)} %get-tuple-element.190.q_ref.k_ref.v_ref, bf16[1224,2304]{1,0:T(8,128)(2,1)} %get-tuple-element.190.q_ref.k_ref.v_ref, ...), custom_call_target="tpu_custom_call" | custom-call | flops 23011983360 | bytes 15040512 | tf_op jit(solution)/shard_map/attend_back/pallas_call | solution.py:434
  291.4 4.1 %fold.2 = (f32[2,192,480]{2,1,0:T(8,128)}, bf16[2,192,480]{2,1,0:T(8,128)(2,1)}) custom-call(s32[20]{0:T(128)} %pad_add_fusion.table, bf16[480,768]{1,0:T(8,128)(2,1)} %get-tuple-element.237.refs_0_, bf16[480,768]{1,0:T(8,128)(2,1)} %copy-done.6, bf16[480,768]{1,0:T(8,128)(2,1)} %copy-done.7, bf16[480,768]{1,0:T(8,128)(2,1)} %collective-permute-done.39.refs_3_), custom_call_target="tpu_custom_call" | custom-call | flops 1000000 | bytes 4423680 | tf_op jit(solution)/shard_map/fold/pallas_call | solution.py:871
  301.0 10.7 %qkv_grads.1 = (bf16[4,288,768]{2,1,0:T(8,128)(2,1)}, bf16[4,288,768]{2,1,0:T(8,128)(2,1)}) custom-call(s32[20]{0:T(128)} %pad_add_fusion.table, bf16[1224,256]{1,0:T(8,128)(2,1)} %get-tuple-element.258.refs_0_, bf16[1224,256]{1,0:T(8,128)(2,1)} %get-tuple-element.259.refs_1_, bf16[1224,256]{1,0:T(8,128)(2,1)} %get-tuple-element.260.refs_2_, ...), custom_call_target="tpu_custom_call" | custom-call | flops 4331667456 | bytes 11059200 | tf_op jit(solution)/shard_map/qkv_grads/pallas_call | solution.py:762
  323.3 15.0 %last.1 = (f32[1224,768]{1,0:T(8,128)}, f32[16,768]{1,0:T(8,128)}) custom-call(s32[20]{0:T(128)} %pad_add_fusion.table, bf16[1224,768]{1,0:T(8,128)(2,1)} %x_ref.5, f32[1224,768]{1,0:T(8,128)} %get-tuple-element.284.d_resid_ref, f32[16,768]{1,0:T(8,128)} %get-tuple-element.207.vec_ref, f32[16,768]{1,0:T(8,128)} %get-tuple-element.285.sums_in, ...), custom_call_target="tpu_custom_call" | custom-call | flops 4331667456 | bytes 15040512 | tf_op jit(solution)/shard_map/last/pallas_call | solution.py:820
  341.4 3.3 collective-permute-done.47
  346.4 3.3 fold.3
  350.6 3.2 collective-permute-done.51
  362.6 9.2 %collective-permute-done.53 = f32[16,768]{1,0:T(8,128)S(1)} collective-permute-done((f32[16,768]{1,0:T(8,128)S(1)}, f32[16,768]{1,0:T(8,128)S(1)}, u32[]{:S(2)}, u32[]{:S(2)}) %collective-permute-start.53) | collective-permute-done | bytes 49184 | tf_op jit(solution)/shard_map/ppermute | solution.py:888
  (221 shorter events, 100.6 us)
Async XLA Ops:
  31.8 28.0 %collective-permute-start.5 = (bf16[320,768]{1,0:T(8,128)(2,1)S(1)}, bf16[320,768]{1,0:T(8,128)(2,1)S(1)}, u32[]{:S(2)}, u32[]{:S(2)}) collective-permute-start(bf16[320,768]{1,0:T(8,128)(2,1)S(1)} %constant_dynamic-update-slice_fusion.refs_0_.refs_9_), channel_id=1, source_target_pairs={{0,4},{1,5},{2,6},{3,7},{4,0},{5,1},{6,2},{7,3},{8,12},{9,13},{10,... | collective-permute-start | bytes 1474568 | tf_op jit(solution)/shard_map/ppermute | solution.py:888
  35.0 24.8 %collective-permute-start.6 = (bf16[288,768]{1,0:T(8,128)(2,1)S(1)}, bf16[288,768]{1,0:T(8,128)(2,1)}, u32[]{:S(2)}, u32[]{:S(2)}) collective-permute-start(bf16[288,768]{1,0:T(8,128)(2,1)S(1)} %constant_dynamic-update-slice_fusion.2.refs_4_.refs_13_), channel_id=1, source_target_pairs={{0,2},{1,3},{2,0},{3,1},{4,6},{5,7},{6,4},{7,5},{8,10},{9,11},{10,... | collective-permute-start | bytes 1327112 | tf_op jit(solution)/shard_map/ppermute | solution.py:888
  59.9 17.1 %collective-permute-start.13 = (bf16[320,768]{1,0:T(8,128)(2,1)S(1)}, bf16[320,768]{1,0:T(8,128)(2,1)}, u32[]{:S(2)}, u32[]{:S(2)}) collective-permute-start(bf16[320,768]{1,0:T(8,128)(2,1)S(1)} %collective-permute-done.5.refs_1_.refs_10_), channel_id=1, source_target_pairs={{0,1},{1,0},{2,3},{3,2},{4,5},{5,4},{6,7},{7,6},{8,9},{9,8},{10,11... | collective-permute-start | bytes 1474568 | tf_op jit(solution)/shard_map/ppermute | solution.py:888
  74.0 15.7 %collective-permute-start.11 = (bf16[240,768]{1,0:T(8,128)(2,1)}, bf16[240,768]{1,0:T(8,128)(2,1)S(1)}, u32[]{:S(2)}, u32[]{:S(2)}) collective-permute-start(bf16[240,768]{1,0:T(8,128)(2,1)} %get-tuple-element.178), channel_id=1, source_target_pairs={{0,4},{1,5},{2,6},{3,7},{4,0},{5,1},{6,2},{7,3},{8,12},{9,13},{10,... | collective-permute-start | bytes 1105928 | tf_op jit(solution)/shard_map/ppermute | solution.py:888
  90.8 18.9 %collective-permute-start.19 = (bf16[192,768]{1,0:T(8,128)(2,1)S(1)}, bf16[192,768]{1,0:T(8,128)(2,1)S(1)}, u32[]{:S(2)}, u32[]{:S(2)}) collective-permute-start(bf16[192,768]{1,0:T(8,128)(2,1)S(1)} %pad_maximum_fusion.4), channel_id=1, source_target_pairs={{0,2},{1,3},{2,0},{3,1},{4,6},{5,7},{6,4},{7,5},{8,10},{9,11},{10,... | collective-permute-start | bytes 884744 | tf_op jit(solution)/shard_map/ppermute | solution.py:888
  92.0 17.6 %collective-permute-start.20 = (bf16[192,768]{1,0:T(8,128)(2,1)S(1)}, bf16[192,768]{1,0:T(8,128)(2,1)S(1)}, u32[]{:S(2)}, u32[]{:S(2)}) collective-permute-start(bf16[192,768]{1,0:T(8,128)(2,1)S(1)} %pad_maximum_fusion.5), channel_id=1, source_target_pairs={{0,4},{1,5},{2,6},{3,7},{4,0},{5,1},{6,2},{7,3},{8,12},{9,13},{10,... | collective-permute-start | bytes 884744 | tf_op jit(solution)/shard_map/ppermute | solution.py:888
  93.6 33.9 %collective-permute-start.21 = (bf16[480,768]{1,0:T(8,128)(2,1)S(1)}, bf16[480,768]{1,0:T(8,128)(2,1)}, u32[]{:S(2)}, u32[]{:S(2)}) collective-permute-start(bf16[480,768]{1,0:T(8,128)(2,1)S(1)} %pad_maximum_fusion.refs_0_), channel_id=1, source_target_pairs={{0,4},{1,5},{2,6},{3,7},{4,0},{5,1},{6,2},{7,3},{8,12},{9,13},{10,... | collective-permute-start | bytes 2211848 | tf_op jit(solution)/shard_map/ppermute | solution.py:888
  94.1 33.4 %collective-permute-start.22 = (bf16[480,768]{1,0:T(8,128)(2,1)S(1)}, bf16[480,768]{1,0:T(8,128)(2,1)}, u32[]{:S(2)}, u32[]{:S(2)}) collective-permute-start(bf16[480,768]{1,0:T(8,128)(2,1)S(1)} %pad_maximum_fusion.1.refs_4_), channel_id=1, source_target_pairs={{0,2},{1,3},{2,0},{3,1},{4,6},{5,7},{6,4},{7,5},{8,10},{9,11},{10,... | collective-permute-start | bytes 2211848 | tf_op jit(solution)/shard_map/ppermute | solution.py:888
  109.8 17.7 %collective-permute-start.23 = (bf16[384,768]{1,0:T(8,128)(2,1)S(1)}, bf16[384,768]{1,0:T(8,128)(2,1)S(1)}, u32[]{:S(2)}, u32[]{:S(2)}) collective-permute-start(bf16[384,768]{1,0:T(8,128)(2,1)S(1)} %pad_maximum_fusion.2.refs_8_), channel_id=1, source_target_pairs={{0,4},{1,5},{2,6},{3,7},{4,0},{5,1},{6,2},{7,3},{8,12},{9,13},{10,... | collective-permute-start | bytes 1769480 | tf_op jit(solution)/shard_map/ppermute | solution.py:888
  111.1 16.5 %collective-permute-start.24 = (bf16[384,768]{1,0:T(8,128)(2,1)S(1)}, bf16[384,768]{1,0:T(8,128)(2,1)}, u32[]{:S(2)}, u32[]{:S(2)}) collective-permute-start(bf16[384,768]{1,0:T(8,128)(2,1)S(1)} %pad_maximum_fusion.3.refs_12_), channel_id=1, source_target_pairs={{0,2},{1,3},{2,0},{3,1},{4,6},{5,7},{6,4},{7,5},{8,10},{9,11},{10,... | collective-permute-start | bytes 1769480 | tf_op jit(solution)/shard_map/ppermute | solution.py:888
  202.0 16.1 %collective-permute-start.33 = (bf16[4,4,96,768]{3,2,1,0:T(8,128)(2,1)}, bf16[4,4,96,768]{3,2,1,0:T(8,128)(2,1)}, u32[]{:S(2)}, u32[]{:S(2)}) collective-permute-start(bf16[4,4,96,768]{3,2,1,0:T(8,128)(2,1)} %get-tuple-element.222), channel_id=1, source_target_pairs={{0,1},{1,0},{2,3},{3,2},{4,5},{5,4},{6,7},{7,6},{8,9},{9,8},{10,11... | collective-permute-start | bytes 7077896 | tf_op jit(solution)/shard_map/ppermute | solution.py:888
  217.7 34.0 %collective-permute-start.34 = (bf16[4,480,768]{2,1,0:T(8,128)(2,1)}, bf16[4,480,768]{2,1,0:T(8,128)(2,1)}, u32[]{:S(2)}, u32[]{:S(2)}) collective-permute-start(bf16[4,480,768]{2,1,0:T(8,128)(2,1)} %get-tuple-element.234), channel_id=1, source_target_pairs={{0,1},{1,0},{2,3},{3,2},{4,5},{5,4},{6,7},{7,6},{8,9},{9,8},{10,11... | collective-permute-start | bytes 8847368 | tf_op jit(solution)/shard_map/ppermute | solution.py:888
  219.7 39.5 %collective-permute-start.35 = (bf16[2,4,96,768]{3,2,1,0:T(8,128)(2,1)S(1)}, bf16[2,4,96,768]{3,2,1,0:T(8,128)(2,1)}, u32[]{:S(2)}, u32[]{:S(2)}) collective-permute-start(bf16[2,4,96,768]{3,2,1,0:T(8,128)(2,1)S(1)} %add_convert_fusion), channel_id=1, source_target_pairs={{0,8},{8,0},{16,24},{24,16},{1,9},{9,1},{17,25},{25,17},{2,10},{10... | collective-permute-start | bytes 3538952 | tf_op jit(solution)/shard_map/ppermute | solution.py:888
  255.6 34.6 %collective-permute-start.37 = (bf16[480,768]{1,0:T(8,128)(2,1)}, bf16[480,768]{1,0:T(8,128)(2,1)S(1)}, u32[]{:S(2)}, u32[]{:S(2)}) collective-permute-start(bf16[480,768]{1,0:T(8,128)(2,1)} %get-tuple-element.246), channel_id=1, source_target_pairs={{0,2},{1,3},{2,0},{3,1},{4,6},{5,7},{6,4},{7,5},{8,10},{9,11},{10,... | collective-permute-start | bytes 2211848 | tf_op jit(solution)/shard_map/ppermute | solution.py:888
  256.2 34.0 %collective-permute-start.38 = (bf16[480,768]{1,0:T(8,128)(2,1)}, bf16[480,768]{1,0:T(8,128)(2,1)S(1)}, u32[]{:S(2)}, u32[]{:S(2)}) collective-permute-start(bf16[480,768]{1,0:T(8,128)(2,1)} %get-tuple-element.247), channel_id=1, source_target_pairs={{0,4},{1,5},{2,6},{3,7},{4,0},{5,1},{6,2},{7,3},{8,12},{9,13},{10,... | collective-permute-start | bytes 2211848 | tf_op jit(solution)/shard_map/ppermute | solution.py:888
  257.0 33.2 %collective-permute-start.39 = (bf16[480,768]{1,0:T(8,128)(2,1)}, bf16[480,768]{1,0:T(8,128)(2,1)}, u32[]{:S(2)}, u32[]{:S(2)}) collective-permute-start(bf16[480,768]{1,0:T(8,128)(2,1)} %get-tuple-element.248), channel_id=1, source_target_pairs={{0,6},{1,7},{2,4},{3,5},{4,2},{5,3},{6,0},{7,1},{8,14},{9,15},{10,... | collective-permute-start | bytes 2211848 | tf_op jit(solution)/shard_map/ppermute | solution.py:888
  261.2 29.1 %collective-permute-start.36 = (bf16[4,96,768]{2,1,0:T(8,128)(2,1)S(1)}, bf16[4,96,768]{2,1,0:T(8,128)(2,1)S(1)}, u32[]{:S(2)}, u32[]{:S(2)}) collective-permute-start(bf16[4,96,768]{2,1,0:T(8,128)(2,1)S(1)} %get-tuple-element.245), channel_id=1, source_target_pairs={{0,16},{8,24},{16,0},{24,8},{1,17},{9,25},{17,1},{25,9},{2,18},{10... | collective-permute-start | bytes 1769480 | tf_op jit(solution)/shard_map/ppermute | solution.py:888
  295.6 16.2 %collective-permute-start.40 = (bf16[2,192,480]{2,1,0:T(8,128)(2,1)}, bf16[2,192,480]{2,1,0:T(8,128)(2,1)S(1)}, u32[]{:S(2)}, u32[]{:S(2)}) collective-permute-start(bf16[2,192,480]{2,1,0:T(8,128)(2,1)} %get-tuple-element.270), channel_id=1, source_target_pairs={{0,8},{8,0},{16,24},{24,16},{1,9},{9,1},{17,25},{25,17},{2,10},{10... | collective-permute-start | bytes 1105928 | tf_op jit(solution)/shard_map/ppermute | solution.py:888
  318.4 19.9 %collective-permute-start.45 = (bf16[192,480]{1,0:T(8,128)(2,1)}, bf16[192,480]{1,0:T(8,128)(2,1)}, u32[]{:S(2)}, u32[]{:S(2)}) collective-permute-start(bf16[192,480]{1,0:T(8,128)(2,1)} %fusion.9), channel_id=1, source_target_pairs={{0,16},{8,24},{16,0},{24,8},{1,17},{9,25},{17,1},{25,9},{2,18},{10... | collective-permute-start | bytes 552968 | tf_op jit(solution)/shard_map/ppermute | solution.py:888
  319.8 24.9 %collective-permute-start.48 = (bf16[288,768]{1,0:T(8,128)(2,1)S(1)}, bf16[288,768]{1,0:T(8,128)(2,1)S(1)}, u32[]{:S(2)}, u32[]{:S(2)}) collective-permute-start(bf16[288,768]{1,0:T(8,128)(2,1)S(1)} %get-tuple-element.293), channel_id=1, source_target_pairs={{0,2},{1,3},{2,0},{3,1},{4,6},{5,7},{6,4},{7,5},{8,10},{9,11},{10,... | collective-permute-start | bytes 1327112 | tf_op jit(solution)/shard_map/ppermute | solution.py:888
  320.6 24.1 %collective-permute-start.49 = (bf16[288,768]{1,0:T(8,128)(2,1)S(1)}, bf16[288,768]{1,0:T(8,128)(2,1)S(1)}, u32[]{:S(2)}, u32[]{:S(2)}) collective-permute-start(bf16[288,768]{1,0:T(8,128)(2,1)S(1)} %get-tuple-element.294), channel_id=1, source_target_pairs={{0,4},{1,5},{2,6},{3,7},{4,0},{5,1},{6,2},{7,3},{8,12},{9,13},{10,... | collective-permute-start | bytes 1327112 | tf_op jit(solution)/shard_map/ppermute | solution.py:888
  322.1 22.6 %collective-permute-start.50 = (bf16[288,768]{1,0:T(8,128)(2,1)S(1)}, bf16[288,768]{1,0:T(8,128)(2,1)S(1)}, u32[]{:S(2)}, u32[]{:S(2)}) collective-permute-start(bf16[288,768]{1,0:T(8,128)(2,1)S(1)} %get-tuple-element.295), channel_id=1, source_target_pairs={{0,6},{1,7},{2,4},{3,5},{4,2},{5,3},{6,0},{7,1},{8,14},{9,15},{10,... | collective-permute-start | bytes 1327112 | tf_op jit(solution)/shard_map/ppermute | solution.py:888
  354.3 17.4 %collective-permute-start.54 = (bf16[192,288]{1,0:T(8,128)(2,1)}, bf16[192,288]{1,0:T(8,128)(2,1)S(1)}, u32[]{:S(2)}, u32[]{:S(2)}) collective-permute-start(bf16[192,288]{1,0:T(8,128)(2,1)} %get-tuple-element.302), channel_id=1, source_target_pairs={{0,8},{8,0},{16,24},{24,16},{1,9},{9,1},{17,25},{25,17},{2,10},{10... | collective-permute-start | bytes 331784 | tf_op jit(solution)/shard_map/ppermute | solution.py:888
  355.9 15.8 %collective-permute-start.55 = (bf16[192,288]{1,0:T(8,128)(2,1)}, bf16[192,288]{1,0:T(8,128)(2,1)S(1)}, u32[]{:S(2)}, u32[]{:S(2)}) collective-permute-start(bf16[192,288]{1,0:T(8,128)(2,1)} %get-tuple-element.303), channel_id=1, source_target_pairs={{0,16},{8,24},{16,0},{24,8},{1,17},{9,25},{17,1},{25,9},{2,18},{10... | collective-permute-start | bytes 331784 | tf_op jit(solution)/shard_map/ppermute | solution.py:888
  (73 other events, 781.8 us)

commit v3 on v2

--- a/solution.py
+++ b/solution.py
@@ -17,10 +17,12 @@
 AXES = ("gx", "gy")
 BLOCKS = 8
 AUX = 16
-VMEM_BYTES = 60 << 20
+MIB = 1 << 20
 MASKS_A = (0, 2, 4, 6, 1, 3, 5, 7)
 MASKS_B = (0, 4, 2, 6, 1, 5, 3, 7)
 PLANES = (0, 2, 1, 3)
+PLACE_AT = 2 * BLOCKS + 4
+RELATIVE_AT = PLACE_AT + 4
 ANY = pl.BlockSpec(memory_space=pl.ANY)
 
 
@@ -36,8 +38,8 @@
     return lax.dot_general(left, right, (((0,), (0,)), ((), ())), preferred_element_type=F32)
 
 
-def params(**extra):
-    return pltpu.CompilerParams(vmem_limit_bytes=VMEM_BYTES, **extra)
+def params(mebibytes):
+    return pltpu.CompilerParams(vmem_limit_bytes=mebibytes * MIB)
 
 
 def cost(flops, bytes_moved, transcendentals=0):
@@ -66,67 +68,51 @@
     )
 
 
-def pack_kernel(w_ref, *refs):
-    vectors, out_ref = refs[:-1], refs[-1]
+def pack_kernel(w_ref, up_ref, out_ref, down_ref, *refs):
+    vectors, message_ref, both_ref = refs[:-2], refs[-2], refs[-1]
     rows = w_ref.shape[0]
-    out_ref[0:rows, :] = w_ref[...]
-    out_ref[rows:, :] = jnp.zeros((out_ref.shape[0] - rows, out_ref.shape[1]), BF)
+    message_ref[0:rows, :] = w_ref[...]
     pieces = [ref[...].astype(F32) for ref in vectors]
-    out_ref[rows : rows + 8, :] = jnp.broadcast_to(
-        jnp.concatenate(pieces, axis=1), (8, out_ref.shape[1])
+    message_ref[rows : rows + 8, :] = jnp.broadcast_to(
+        jnp.concatenate(pieces, axis=1), (8, message_ref.shape[1])
     ).astype(BF)
-
-
-def pack(w_qkv, vectors):
-    rows, columns = w_qkv.shape
-    shape = (rows + 8, columns)
-    return pl.pallas_call(
-        pack_kernel,
-        out_shape=jax.ShapeDtypeStruct(shape, BF),
-        compiler_params=params(),
-        cost_estimate=cost(1e4, rows * columns * 4),
-        name="pack",
-    )(w_qkv, *[v[None, :] for v in vectors])
-
-
-def pack_rest_kernel(up_ref, out_ref, down_ref, both_ref, turned_ref):
     wide, narrow = up_ref.shape[1], out_ref.shape[1]
+    edge = both_ref.shape[1] - wide
     both_ref[:, 0:wide] = up_ref[...]
     both_ref[:, wide : wide + narrow] = out_ref[...]
-    both_ref[:, wide + narrow :] = jnp.zeros(
-        (both_ref.shape[0], both_ref.shape[1] - wide - narrow), BF
+    both_ref[:, wide + narrow : edge] = jnp.zeros(
+        (both_ref.shape[0], edge - wide - narrow), BF
     )
-    turned_ref[...] = down_ref[...].astype(F32).T.astype(BF)
-
-
-def pack_rest(w_up, w_out, w_down):
-    rows = w_up.shape[0]
-    columns = -(-(w_up.shape[1] + w_out.shape[1]) // 128) * 128
-    return pl.pallas_call(
-        pack_rest_kernel,
+    both_ref[0:narrow, edge:] = down_ref[:, 0:wide]
+    both_ref[narrow : 2 * narrow, edge:] = down_ref[:, wide : 2 * wide]
+
+
+def pack(w_qkv, w_up, w_out, w_down, vectors):
+    rows, columns = w_qkv.shape
+    wide = w_up.shape[1]
+    edge = -(-(wide + w_out.shape[1]) // 128) * 128
+    return pl.pallas_call(
+        pack_kernel,
         out_shape=[
-            jax.ShapeDtypeStruct((rows, columns), BF),
-            jax.ShapeDtypeStruct(w_down.shape[::-1], BF),
+            jax.ShapeDtypeStruct((rows + 8, columns), BF),
+            jax.ShapeDtypeStruct((rows, edge + wide), BF),
         ],
-        compiler_params=params(),
-        cost_estimate=cost(1e4, rows * columns * 4 + w_down.size * 4),
-        name="pack_rest",
-    )(w_up, w_out, w_down)
+        compiler_params=params(63),
+        cost_estimate=cost(1e4, rows * (columns + edge + wide) * 4),
+        name="pack",
+    )(w_qkv, w_up, w_out, w_down.T, *[v[None, :] for v in vectors])
 
 
 def arrange_qkv_kernel(pos, *refs):
-    pieces, (first_ref, second_ref), stacked = refs[:4], refs[4:6], refs[6]
-    width, columns = first_ref.shape[1], pieces[0].shape[1]
-    half = columns // 2
+    pieces, out_ref, stacked = refs[:4], refs[4], refs[5]
+    width, columns = out_ref.shape[1], pieces[0].shape[1]
     rows = width // 4
     vec_rows = []
     for k in range(4):
         place = pos[0] ^ k
         stacked[pl.ds(pl.multiple_of(place * rows, 8), rows), :] = pieces[k][0:rows, :].astype(F32)
         vec_rows.append(pieces[k][rows : rows + 1, :].astype(F32))
-    turned = stacked[...].T.astype(BF)
-    first_ref[0:half, :] = turned[0:half]
-    second_ref[...] = turned[half:columns]
+    out_ref[0:columns, :] = stacked[...].T.astype(BF)
     vec = jnp.concatenate(vec_rows, axis=0).astype(BF)
     lane = lax.broadcasted_iota(jnp.int32, (columns, width), 1)
     source = lax.broadcasted_iota(jnp.int32, (columns, width), 0)
@@ -147,81 +133,100 @@
             jnp.sum(jnp.where((pos[0] ^ order) == row, spread, 0.0), axis=0, keepdims=True)
         )
     rows_out.append(jnp.zeros((AUX - 12, width), F32))
-    first_ref[half : half + AUX, :] = jnp.concatenate(rows_out, axis=0).astype(BF)
+    out_ref[columns : columns + AUX, :] = jnp.concatenate(rows_out, axis=0).astype(BF)
 
 
 def arrange_qkv(pos, pieces, width):
     rows, columns = pieces[0].shape
-    out = [
-        jax.ShapeDtypeStruct((columns // 2 + AUX, width), BF),
-        jax.ShapeDtypeStruct((columns // 2, width), BF),
-    ]
+    out = jax.ShapeDtypeStruct((columns + AUX, width), BF)
     return pl.pallas_call(
         arrange_qkv_kernel,
         grid_spec=pltpu.PrefetchScalarGridSpec(
             num_scalar_prefetch=1,
             grid=(1,),
             in_specs=[whole((rows, columns))] * 4,
-            out_specs=[whole(o.shape) for o in out],
+            out_specs=whole(out.shape),
             scratch_shapes=[pltpu.VMEM((width, columns), F32)],
         ),
         out_shape=out,
-        compiler_params=params(),
+        compiler_params=params(16),
         cost_estimate=cost(4e6, 4 * rows * columns * 2 * 2),
         name="arrange_qkv",
     )(pos, *pieces)
 
 
-def arrange_rest_kernel(pos, *refs):
-    pieces, (first_ref, second_ref), stacked = refs[:4], refs[4:6], refs[6]
+def arrange_rest_kernel(pos, own_ref, near_ref, far_ref, first_ref, second_ref, stacked):
     rows = first_ref.shape[1] // 4
     half = first_ref.shape[0]
+    edge = far_ref.shape[1]
+    pieces = [own_ref[:, 0:edge], near_ref[:, 0:edge], far_ref[0:rows], far_ref[rows : 2 * rows]]
     for k in range(4):
         start = pl.multiple_of((pos[0] ^ k) * rows, 8)
-        stacked[pl.ds(start, rows), :] = pieces[k][...].astype(F32)
+        stacked[pl.ds(start, rows), :] = pieces[k].astype(F32)
     turned = stacked[...].T.astype(BF)
     first_ref[...] = turned[0:half]
     second_ref[...] = turned[half : 2 * half]
 
 
-def arrange_rest(pos, pieces, width, height):
+def arrange_rest(pos, own, near_piece, far_pieces, width, height):
     out = jax.ShapeDtypeStruct((height // 2, width), BF)
     return pl.pallas_call(
         arrange_rest_kernel,
         grid_spec=pltpu.PrefetchScalarGridSpec(
             num_scalar_prefetch=1,
             grid=(1,),
-            in_specs=[whole(pieces[0].shape)] * 4,
+            in_specs=[whole(own.shape)] * 2 + [whole(far_pieces.shape)],
             out_specs=[whole(out.shape)] * 2,
-            scratch_shapes=[pltpu.VMEM((width, pieces[0].shape[1]), F32)],
+            scratch_shapes=[pltpu.VMEM((width, far_pieces.shape[1]), F32)],
         ),
         out_shape=[out, out],
-        compiler_params=params(),
+        compiler_params=params(16),
         cost_estimate=cost(1e6, out.shape[0] * width * 2 * 4),
         name="arrange_rest",
-    )(pos, *pieces)
-
-
-def qkv_copies(table, halves, weights, sems):
-    step = weights.shape[0] // (2 * BLOCKS)
-    copies = []
-    for j in range(2 * BLOCKS):
-        source = halves[j // 2]
-        start = table[j] * (2 * step) + j // BLOCKS * step
-        copies.append(
-            pltpu.make_async_copy(
-                source.at[pl.ds(j % 2 * (source.shape[0] // 2), step)],
-                weights.at[pl.ds(pl.multiple_of(start, 16), step)],
-                sems.at[j],
-            )
+    )(pos, own, near_piece, far_pieces)
+
+
+def arrange_down_kernel(own_ref, near_ref, far_ref, first_ref, second_ref):
+    wide = far_ref.shape[1]
+    rows = own_ref.shape[0]
+    narrow = rows // 2
+    edge = own_ref.shape[1] - wide
+    pieces = [own_ref[:, edge:], near_ref[:, edge:], far_ref[0:rows], far_ref[rows : 2 * rows]]
+    for k in range(4):
+        target = (first_ref, second_ref)[k // 2]
+        at = k % 2 * narrow
+        target[at : at + narrow, 0:wide] = pieces[k][0:narrow]
+        target[at : at + narrow, wide : 2 * wide] = pieces[k][narrow:rows]
+
+
+def arrange_down(own, near_piece, far_pieces):
+    rows, wide = own.shape[0], far_pieces.shape[1]
+    out = jax.ShapeDtypeStruct((rows, 2 * wide), BF)
+    return pl.pallas_call(
+        arrange_down_kernel,
+        out_shape=[out, out],
+        compiler_params=params(16),
+        cost_estimate=cost(1e4, rows * wide * 2 * 8),
+        name="arrange_down",
+    )(own, near_piece, far_pieces)
+
+
+def qkv_copies(table, blocks, weights, sems):
+    step = weights.shape[0] // BLOCKS
+    return [
+        pltpu.make_async_copy(
+            blocks[j].at[pl.ds(0, step)],
+            weights.at[pl.ds(pl.multiple_of(table[j] * step, 16), step)],
+            sems.at[j],
         )
-    return copies
+        for j in range(BLOCKS)
+    ]
 
 
 def project_kernel(table, x_ref, *refs):
     blocks, (proj_ref, normed_ref, vec_ref), (weights, aux, sems) = refs[:8], refs[8:11], refs[11:]
     j = pl.program_id(0)
-    step = weights.shape[0] // (2 * BLOCKS)
+    step = weights.shape[0] // BLOCKS
     tile = proj_ref.shape[1]
     width = x_ref.shape[1]
 
@@ -229,9 +234,7 @@
     def _():
         small = [
             pltpu.make_async_copy(
-                blocks[i // 2].at[pl.ds(i % 2 * (step + AUX) + step, AUX)],
-                aux.at[i],
-                sems.at[2 * BLOCKS + i],
+                blocks[i].at[pl.ds(step, AUX)], aux.at[i], sems.at[BLOCKS + i]
             )
             for i in range(BLOCKS)
         ]
@@ -281,7 +284,7 @@
             jax.ShapeDtypeStruct((slots, width), BF),
             jax.ShapeDtypeStruct((AUX, width), F32),
         ],
-        compiler_params=params(),
+        compiler_params=params(32),
         cost_estimate=cost(2 * slots * width * columns, slots * width * 10),
         name="project",
     )(table, x, *blocks)
@@ -340,7 +343,7 @@
             jax.ShapeDtypeStruct((pairs, 8, padded), F32),
         ],
         input_output_aliases={4 + i: i for i in range(len(into))},
-        compiler_params=params(),
+        compiler_params=params(63),
         cost_estimate=cost(
             2 * count * 8 * slots * slots * PAIR, slots * width * 8, 2 * count * slots * slots
         ),
@@ -448,7 +451,7 @@
             scratch_shapes=[pltpu.VMEM((2, padded, PAIR), BF)] * 2,
         ),
         out_shape=[jax.ShapeDtypeStruct((slots, count * PAIR), BF)] * 3,
-        compiler_params=params(),
+        compiler_params=params(40),
         cost_estimate=cost(
             2 * count * 20 * slots * slots * PAIR, slots * width * 16, 2 * count * slots * slots
         ),
@@ -559,7 +562,7 @@
         return (out_sum + nt(active, w_down[:, at]), d_normed + nn(d_inner, w_up[at, :]))
 
     zero = jnp.zeros((tile, width), F32)
-    out_sum, d_normed = lax.fori_loop(0, hidden // chunk, step, (zero, zero))
+    out_sum, d_normed = lax.fori_loop(0, hidden // chunk, step, (zero, zero), unroll=True)
     out_ref[...] = (residual + out_sum + vec_ref[3:4, :]).astype(BF)
     d_resid = seed + norm_back(d_normed, nhat, scale, vec_ref[6:7, :])
     d_resid_ref[...] = d_resid
@@ -611,7 +614,7 @@
             jax.ShapeDtypeStruct((slots, width), BF),
             jax.ShapeDtypeStruct(vec.shape, F32),
         ],
-        compiler_params=params(),
+        compiler_params=params(63),
         cost_estimate=cost(
             2 * slots * width * (4 * hidden + 2 * width),
             slots * (hidden * 4 + width * 18) + hidden * width * 4,
@@ -624,11 +627,16 @@
 def deliver(copies):
     for copy in copies:
         copy.start()
+
+
+def collect(copies):
     for copy in copies:
         copy.wait()
 
 
-def down_grads_kernel(len_ref, table, active_ref, cot_ref, keep_ref, send_ref, sums, sems):
+def down_grads_kernel(
+    len_ref, table, active_ref, cot_ref, keep_ref, send_ref, sums, sems
+):
     z = pl.program_id(0)
     slots, width = cot_ref.shape
     narrow = width // BLOCKS
@@ -636,21 +644,26 @@
     seed = jnp.where(rows < len_ref[0], cot_ref[...], jnp.zeros_like(cot_ref))
     sums[z] = tn(seed, active_ref[...]).astype(BF)
 
-    @pl.when(z == pl.num_programs(0) - 1)
-    def _():
+    def plane(index):
         copies = []
         for j in range(BLOCKS):
             target = keep_ref if j < 4 else send_ref
             at = pl.ds(pl.multiple_of(table[j] * narrow, 16), narrow)
-            for k in range(4):
-                copies.append(
-                    pltpu.make_async_copy(
-                        sums.at[table[2 * BLOCKS + PLANES[k]], at],
-                        target.at[k, j % 4],
-                        sems.at[j * 4 + k],
-                    )
+            copies.append(
+                pltpu.make_async_copy(
+                    sums.at[index, at],
+                    target.at[table[PLACE_AT + index], j % 4],
+                    sems.at[index * BLOCKS + j],
                 )
-        deliver(copies)
+            )
+        return copies
+
+    deliver(plane(z))
+
+    @pl.when(z == pl.num_programs(0) - 1)
+    def _():
+        for index in range(4):
+            collect(plane(index))
 
 
 def down_grads(length, table, active, cot):
@@ -670,7 +683,7 @@
             ],
         ),
         out_shape=[out, out],
-        compiler_params=params(),
+        compiler_params=params(63),
         cost_estimate=cost(2 * slots * width * hidden, slots * hidden * 2 + out.size * 4),
         name="down_grads",
     )(length, table, active, cot)
@@ -694,16 +707,30 @@
         for g in range(BLOCKS):
             sums[g, wide : wide + narrow, :] = out[g * narrow : (g + 1) * narrow]
 
+    def block(g):
+        index = table[RELATIVE_AT + g]
+        source = sums.at[g]
+        return (
+            pltpu.make_async_copy(source, keep_ref.at[lax.rem(index, 4)], sems.at[g]),
+            pltpu.make_async_copy(source, send_ref.at[lax.rem(index, 4)], sems.at[g]),
+            index < 4,
+        )
+
+    for j in range(per):
+        keep, send, kept = block(z * per + j)
+
+        @pl.when(kept)
+        def _():
+            keep.start()
+
+        @pl.when(jnp.logical_not(kept))
+        def _():
+            send.start()
+
     @pl.when(z == pl.num_programs(0) - 1)
     def _():
-        deliver(
-            [
-                pltpu.make_async_copy(
-                    sums.at[table[j]], (keep_ref if j < 4 else send_ref).at[j % 4], sems.at[j]
-                )
-                for j in range(BLOCKS)
-            ]
-        )
+        for g in range(BLOCKS):
+            block(g)[0].wait()
 
 
 def up_grads(table, d_inner, normed, d_branch, mixed):
@@ -725,7 +752,7 @@
             ],
         ),
         out_shape=[out, out],
-        compiler_params=params(),
+        compiler_params=params(40),
         cost_estimate=cost(
             2 * slots * width * (hidden + width), slots * hidden * 2 + out.size * 4
         ),
@@ -733,46 +760,61 @@
     )(table, d_inner, normed, d_branch, mixed)
 
 
-def qkv_grads_kernel(table, *refs):
-    parts_in, normed_ref, (keep_ref, send_ref, sums, sems) = refs[:-5], refs[-5], refs[-4:]
+def qkv_grads_kernel(table, *refs, count):
+    parts_in, normed_ref, (keep_ref, send_ref) = (
+        refs[:count],
+        refs[count],
+        refs[count + 1 : count + 3],
+    )
+    sums, sems, loads = refs[-3:]
+    local, sources = refs[-3 - count : -3], parts_in
     width = normed_ref.shape[1]
     block = sums.shape[0] // BLOCKS
-    groups = len(parts_in) // 3
+    groups = count // 3
+    copies = [
+        pltpu.make_async_copy(sources[i], local[i], loads.at[i]) for i in range(count)
+    ]
+    for s in range(3):
+        for i in range(groups):
+            copies[i * 3 + s].start()
     for s in range(3):
         start = s * width
         for i in range(groups):
-            ref = parts_in[i * 3 + s]
-            sums[start : start + ref.shape[1], :] = tn(ref[...], normed_ref[...]).astype(BF)
-            start += ref.shape[1]
-    deliver(
-        [
-            pltpu.make_async_copy(
-                sums.at[pl.ds(pl.multiple_of(table[j] * block, 16), block)],
-                (keep_ref if j < 4 else send_ref).at[j % 4],
-                sems.at[j],
-            )
-            for j in range(BLOCKS)
-        ]
-    )
+            copies[i * 3 + s].wait()
+            part = local[i * 3 + s]
+            sums[start : start + part.shape[1], :] = tn(part[...], normed_ref[...]).astype(BF)
+            start += part.shape[1]
+    copies = [
+        pltpu.make_async_copy(
+            sums.at[pl.ds(pl.multiple_of(table[j] * block, 16), block)],
+            (keep_ref if j < 4 else send_ref).at[j % 4],
+            sems.at[j],
+        )
+        for j in range(BLOCKS)
+    ]
+    deliver(copies)
+    collect(copies)
 
 
 def qkv_grads(table, d_parts, normed):
     slots, width = normed.shape
     out = jax.ShapeDtypeStruct((4, 3 * width // BLOCKS, width), BF)
     return pl.pallas_call(
-        qkv_grads_kernel,
+        functools.partial(qkv_grads_kernel, count=len(d_parts)),
         grid_spec=pltpu.PrefetchScalarGridSpec(
             num_scalar_prefetch=1,
             grid=(1,),
-            in_specs=[whole(part.shape) for part in d_parts] + [whole((slots, width))],
+            in_specs=[ANY] * len(d_parts) + [whole((slots, width))],
             out_specs=[ANY] * 2,
-            scratch_shapes=[
+            scratch_shapes=[pltpu.VMEM(part.shape, BF) for part in d_parts]
+            + [
                 pltpu.VMEM((3 * width, width), BF),
                 pltpu.SemaphoreType.DMA((BLOCKS,)),
+                pltpu.SemaphoreType.DMA((len(d_parts),)),
             ],
         ),
         out_shape=[out, out],
-        compiler_params=params(),
+        compiler_params=params(32),
         cost_estimate=cost(6 * slots * width * width, slots * width * 8 + out.size * 4),
         name="qkv_grads",
     )(table, *d_parts, normed)
@@ -836,7 +878,7 @@
             jax.ShapeDtypeStruct((slots, width), F32),
             jax.ShapeDtypeStruct(vec.shape, F32),
         ],
-        compiler_params=params(),
+        compiler_params=params(40),
         cost_estimate=cost(6 * slots * width * width, slots * width * 16),
         name="last",
     )(table, x, d_resid, vec, sums, *d_parts, *blocks)
@@ -878,7 +920,7 @@
             scratch_shapes=[pltpu.VMEM((width, columns), F32)],
         ),
         out_shape=out,
-        compiler_params=params(),
+        compiler_params=params(16),
         cost_estimate=cost(1e6, columns * width * 12),
         name="fold",
     )(table, *terms)
@@ -894,6 +936,19 @@
 
 def gather_planes(message):
     return [message] + [swap(message, "gx", k, 4) for k in (1, 2, 3)]
+
+
+def orders(z, g):
+    planes, blocks = z ^ jnp.arange(4), g ^ jnp.arange(BLOCKS)
+    return jnp.concatenate(
+        [
+            g ^ jnp.array(MASKS_A),
+            g ^ jnp.array(MASKS_B),
+            planes,
+            planes % 2 * 2 + planes // 2,
+            blocks % 2 * 4 + blocks // 2,
+        ]
+    ).astype(jnp.int32)
 
 
 def near(first, second):
@@ -950,25 +1005,22 @@
     vectors = (bias_q, bias_v, bias_o, bias_down, gain_one, shift_one, gain_two, shift_two)
     if fast:
         pos = jnp.stack([z, g]).astype(jnp.int32)
-        table = jnp.concatenate(
-            [g ^ jnp.array(MASKS_A), g ^ jnp.array(MASKS_B), z ^ jnp.arange(4)]
-        ).astype(jnp.int32)
-        message = pack(w_qkv, vectors + (bias_up,))
-        message, *rest = in_turn(message, w_up, w_out, w_down)
+        table = orders(z, g)
+        message, own = pack(w_qkv, w_up, w_out, w_down, vectors + (bias_up,))
         pieces = gather_planes(message)
-        both, down = pack_rest(*rest)
-        qa, qb = arrange_qkv(pos, pieces, width)
-        qa, qb, both = in_turn(qa, qb, both)
-        qa_near, qb_near = near(qa, qb)
-        pieces = gather_planes(both)
-        qa, qb = join(qa, qa_near), join(qb, qb_near)
-        qa_far, qb_far = far(qa, qb)
-        ra, rb = arrange_rest(pos, pieces, width, wide + narrow)
-        ra, rb, down = in_turn(ra, rb, down)
-        qa, qb, qa_far, qb_far, ra = in_turn(qa, qb, qa_far, qb_far, ra)
-        qkv_blocks = with_cores(qa, qb, qa_far, qb_far)
+        near_piece = swap(own, "gx", 1, 4)
+        block, near_piece = in_turn(arrange_qkv(pos, pieces, width), near_piece)
+        edge = own.shape[1] - wide
+        up_message = join(own[:, :edge], near_piece[:, :edge])
+        down_message = join(own[:, edge:], near_piece[:, edge:])
+        qkv_blocks = [block] + [swap(block, "gy", mask, BLOCKS) for mask in MASKS_A[1:4]]
+        far_pieces = swap(up_message, "gx", 2, 4)
+        far_pieces, *qkv_blocks = in_turn(far_pieces, *qkv_blocks)
+        qkv_blocks += [swap(block, "gy", 1, BLOCKS) for block in qkv_blocks]
+        ra, rb = arrange_rest(pos, own, near_piece, far_pieces, width, wide + narrow)
+        ra, rb, down_message, table = in_turn(ra, rb, down_message, table)
         ra_near, rb_near = near(ra, rb)
-        down_planes = gather_planes(down)
+        down_far = swap(down_message, "gx", 2, 4)
     else:
 
         def everything(shard):
@@ -977,22 +1029,22 @@
             ).T
 
         order = jnp.arange(BLOCKS)
-        table = jnp.concatenate([order, order, jnp.arange(4)]).astype(jnp.int32)
+        place = jnp.array(PLANES)
+        table = jnp.concatenate([order, order, jnp.arange(4), place, order]).astype(jnp.int32)
         aux = [lax.all_gather(v, AXES, axis=0, tiled=True)[None] for v in vectors]
         aux.append(lax.all_gather(bias_up, AXES, axis=0, tiled=True).reshape(4, width))
         aux.append(jnp.zeros((AUX - 12, width), BF))
         none = jnp.zeros((BLOCKS - 1, AUX, width), BF)
         aux = jnp.concatenate([jnp.concatenate(aux)[None], none])
 
-        def halved(blocks, extra=None):
+        def halved(blocks):
             half = blocks.shape[1] // 2
-            first = blocks[:, :half]
-            if extra is not None:
-                first = jnp.concatenate([first, extra], axis=1)
-            second = blocks[:, half:]
+            first, second = blocks[:, :half], blocks[:, half:]
             return list(first.reshape(4, -1, width)) + list(second.reshape(4, -1, width))
 
-        qkv_blocks = halved(everything(w_qkv).reshape(BLOCKS, -1, width), aux)
+        qkv_blocks = list(
+            jnp.concatenate([everything(w_qkv).reshape(BLOCKS, -1, width), aux], axis=1)
+        )
         up = everything(w_up).reshape(BLOCKS, wide, width)
         out = everything(w_out).reshape(BLOCKS, narrow, width)
         rest_blocks = halved(jnp.concatenate([up, out], axis=1))
@@ -1001,9 +1053,11 @@
 
     proj, normed, vec = project(table, patches, qkv_blocks)
     if fast:
-        ra_near, rb_near, length, proj = in_turn(ra_near, rb_near, lengths, proj)
+        ra_near, rb_near, length, proj, down_far = in_turn(
+            ra_near, rb_near, lengths, proj, down_far
+        )
         ra, rb = join(ra, ra_near), join(rb, rb_near)
-        da, db = join(*down_planes[:2]), join(*down_planes[2:])
+        da, db = arrange_down(own, near_piece, down_far)
         length, ra, rb, da, db = in_turn(length, ra, rb, da, db)
         ra_far, rb_far = far(ra, rb)
         da_near, db_near = near(da, db)
@@ -1078,13 +1132,13 @@
         up_sum = add(up_sum, up_far)
         grad_up, grad_out = up_sum[:, :wide], up_sum[:, wide:]
         steps = (("gy", 1, 8), ("gy", 2, 8), ("gy", 4, 8), ("gx", 1, 4), ("gx", 2, 4))
-        for axis, mask, size in steps[:2]:
+        for axis, mask, size in steps[:3]:
             sums = sums + swap(sums, axis, mask, size)
         table, sums = in_turn(table, sums)
         qkv_pieces = fold(table, qkv_sums[:1] + qkv_got, False)
         sums, *qkv_pieces = in_turn(sums, *qkv_pieces)
         qkv_planes = [swap(qkv_pieces[k], "gx", k, 4) for k in (1, 2, 3)]
-        for axis, mask, size in steps[2:]:
+        for axis, mask, size in steps[3:]:
             sums = sums + swap(sums, axis, mask, size)
         sums, *qkv_planes = in_turn(sums, *qkv_planes)
         grad_qkv = add(qkv_pieces[0], *qkv_planes)

time: 378 us -> 344 us (0.910)
  Pallas kernels: 222 us -> 196 us
  starting transfers between devices: 56.4 us -> 47.4 us
  waiting for transfers between devices: 60.8 us -> 65.8 us
  other arithmetic: 16.7 us -> 12.6 us
    ppermute x57 -> x53, starting transfers between devices: 56.4 us -> 47.4 us  [swap(): return lax.ppermute(values, axis, [(i, i ^ mask) for i in range(size)])]
    pallas_call x1, Pallas kernels: 50.4 us -> 43.1 us  [middle(): pl.pallas_call(functools.partial(middle_kernel, chunk=chunk), grid_spec=p...]
    concatenate x6, other arithmetic: 0.22 us -> 5.68 us  [join(): return jnp.concatenate([first, second], axis=0)]
    pallas_call x2, Pallas kernels: 7.44 us -> 2.1 us  [fold(): pl.pallas_call(fold_kernel, grid_spec=pltpu.PrefetchScalarGridSpec(num_sc...]
    ppermute x57 -> x53, waiting for transfers between devices: 60.8 us -> 65.8 us  [swap(): return lax.ppermute(values, axis, [(i, i ^ mask) for i in range(size)])]
    pallas_call x3, Pallas kernels: 58 us -> 53.2 us  [attend_back(): pl.pallas_call(functools.partial(attend_back_kernel, slots=slots, padded=...]
    unnamed x82 -> x58, local copies, waits for them, and re-layouts: 11.6 us -> 13.2 us
  transfers between devices with their start and end apart: 57 -> 53, of which waited for: 16 -> 16; matrix products, arithmetic and copies ran while one was open for 5% -> 4% of each run, Pallas kernels for 39% -> 40%
where the time goes in v3:
time: 344 us; the launch traced here: 341 us
  Pallas kernels  196 us (57%)
  waiting for transfers between devices  65.8 us (19%)
  starting transfers between devices  47.4 us (14%)
  local copies, waits for them, and re-layouts  16.9 us (5%)
  other arithmetic  12.6 us (4%)
    ppermute x53, waiting for transfers between devices, swap(): return lax.ppermute(values, axis, [(i, i ^ mask) for i in range(size)])  65.8 us
    pallas_call x3, Pallas kernels, attend_back(): pl.pallas_call(functools.partial(attend_back_kernel, slots=slots, padded=...  53.2 us
    ppermute x53, starting transfers between devices, swap(): return lax.ppermute(values, axis, [(i, i ^ mask) for i in range(size)])  47.4 us
    pallas_call x1, Pallas kernels, middle(): pl.pallas_call(functools.partial(middle_kernel, chunk=chunk), grid_spec=p...  43.1 us
    pallas_call x2, Pallas kernels, attend(): pl.pallas_call(functools.partial(attend_kernel, slots=slots, padded=padde...  29.7 us
    pallas_call x1, Pallas kernels, up_grads(): pl.pallas_call(up_grads_kernel, grid_spec=pltpu.PrefetchScalarGridSpec(nu...  13.8 us
    pallas_call x1, Pallas kernels, last(): pl.pallas_call(functools.partial(last_kernel, groups=len(d_parts) // 3),...  13.8 us
    unnamed x58, local copies, waits for them, and re-layouts  13.2 us
  transfers between devices with their start and end apart: 53, of which 16 were waited for; matrix products, arithmetic and copies ran while one was open for 4% of the time, Pallas kernels for 40%

profile of v3, /device:TPU:0, one launch (start us, length us, event | category | flops | bytes accessed | tf_op | source)
XLA Modules:
  0.0 340.8 jit_solution(6037353524908621782)
XLA Ops:
  2.6 3.0 collective-permute-start.3
  5.7 3.0 collective-permute-start.1
  11.1 9.5 %collective-permute-done.refs_1_ = bf16[200,288]{1,0:T(8,128)(2,1)S(1)} collective-permute-done((bf16[200,288]{1,0:T(8,128)(2,1)}, bf16[200,288]{1,0:T(8,128)(2,1)S(1)}, u32[]{:S(2)}, u32[]{:S(2)}) %collective-permute-start) | collective-permute-done | bytes 115232 | tf_op jit(solution)/shard_map/ppermute | solution.py:930
  21.0 5.0 %collective-permute-done.2.refs_3_ = bf16[200,288]{1,0:T(8,128)(2,1)S(1)} collective-permute-done((bf16[200,288]{1,0:T(8,128)(2,1)}, bf16[200,288]{1,0:T(8,128)(2,1)S(1)}, u32[]{:S(2)}, u32[]{:S(2)}) %collective-permute-start.2) | collective-permute-done | bytes 115232 | tf_op jit(solution)/shard_map/ppermute | solution.py:930
  32.3 17.2 %collective-permute-done.4.far_ref = bf16[384,512]{1,0:T(8,128)(2,1)S(1)} collective-permute-done((bf16[384,512]{1,0:T(8,128)(2,1)S(1)}, bf16[384,512]{1,0:T(8,128)(2,1)S(1)}, u32[]{:S(2)}, u32[]{:S(2)}) %collective-permute-start.4) | collective-permute-done | bytes 393248 | tf_op jit(solution)/shard_map/ppermute | solution.py:930
  57.9 10.9 %project.1 = (bf16[1224,2304]{1,0:T(8,128)(2,1)S(1)}, bf16[1224,768]{1,0:T(8,128)(2,1)S(1)}, f32[16,768]{1,0:T(8,128)S(1)}) custom-call(s32[32]{0:T(128)S(1)} %concatenate.23.table, bf16[1224,768]{1,0:T(8,128)(2,1)S(1)} %copy-done.4, bf16[304,768]{1,0:T(8,128)(2,1)S(1)} %arrange_qkv.1.refs_0_.refs_9_, ...), custom_call_target="tpu_custom_call" | custom-call | flops 4331667456 | bytes 9400320 | tf_op jit(solution)/shard_map/project/pallas_call | solution.py:265
  78.0 14.8 %attend.2 = (bf16[1224,768]{1,0:T(8,128)(2,1)}, f32[6,8,1280]{2,1,0:T(8,128)}) custom-call(s32[1]{0:T(128)S(6)} %copy.37.len_ref, bf16[1224,2304]{1,0:T(8,128)(2,1)} %copy-done.10, bf16[1224,2304]{1,0:T(8,128)(2,1)} %copy-done.10, bf16[1224,2304]{1,0:T(8,128)(2,1)} %copy-done.10), custom_call_target="tpu_custom_call" | custom-call | flops 9204793344 | bytes 7520256 | tf_op jit(solution)/shard_map/attend/pallas_call | solution.py:332
  98.5 14.9 %attend.3 = (bf16[1224,768]{1,0:T(8,128)(2,1)}, f32[6,8,1280]{2,1,0:T(8,128)}) custom-call(s32[1]{0:T(128)S(6)} %copy.37.len_ref, bf16[1224,2304]{1,0:T(8,128)(2,1)} %copy-done.10, bf16[1224,2304]{1,0:T(8,128)(2,1)} %copy-done.10, bf16[1224,2304]{1,0:T(8,128)(2,1)} %copy-done.10, ...), custom_call_target="tpu_custom_call", output_to_operand_aliasing={{0}: (4, {}), {1}: (5, {})} | custom-call | flops 9204793344 | bytes 7520256 | tf_op jit(solution)/shard_map/attend/pallas_call | solution.py:332
  117.7 4.9 %collective-permute-done.28.refs_15_ = bf16[384,768]{1,0:T(8,128)(2,1)} collective-permute-done((bf16[384,768]{1,0:T(8,128)(2,1)}, bf16[384,768]{1,0:T(8,128)(2,1)}, u32[]{:S(2)}, u32[]{:S(2)}) %collective-permute-start.28) | collective-permute-done | bytes 589856 | tf_op jit(solution)/shard_map/ppermute | solution.py:930
  122.7 43.1 %middle.1 = (bf16[1224,768]{1,0:T(8,128)(2,1)}, bf16[1224,3072]{1,0:T(8,128)(2,1)}, bf16[1224,3072]{1,0:T(8,128)(2,1)}, bf16[1224,768]{1,0:T(8,128)(2,1)}, f32[1...) custom-call(s32[1]{0:T(128)S(6)} %copy.37.len_ref, s32[32]{0:T(128)} %copy-done.2, ...), custom_call_target="tpu_custom_call" | custom-call | flops 25990004736 | bytes 41398272 | tf_op jit(solution)/shard_map/middle/pallas_call | solution.py:584
  165.8 11.8 %down_grads.1 = (bf16[4,4,96,768]{3,2,1,0:T(8,128)(2,1)}, bf16[4,4,96,768]{3,2,1,0:T(8,128)(2,1)}) custom-call(s32[1]{0:T(128)S(6)} %copy.37.len_ref, s32[32]{0:T(128)} %copy-done.2, bf16[1224,3072]{1,0:T(8,128)(2,1)} %get-tuple-element.211.active_ref, bf16[1224,768]{1,0:T(8,128)(2,1)} %cot_ref.3), custom_call_target="tpu_custom_call" | custom-call | flops 5775556608 | bytes 12238848 | tf_op jit(solution)/shard_map/down_grads/pallas_call | solution.py:673
  182.3 13.8 %up_grads.1 = (bf16[4,480,768]{2,1,0:T(8,128)(2,1)S(1)}, bf16[4,480,768]{2,1,0:T(8,128)(2,1)S(1)}) custom-call(s32[32]{0:T(128)S(1)} %copy-done.3, bf16[1224,3072]{1,0:T(8,128)(2,1)} %get-tuple-element.217.d_inner_ref, bf16[1224,768]{1,0:T(8,128)(2,1)S(1)} %copy-done.20, bf16[1224,768]{1,0:T(8,128)(2,1)S(1)} %copy-done.21, bf16[1224,768]{1,0:T(8,128)(2,1)S(1)} %copy-done.16), custom_call_target="tpu_custom_call" | custom-call | flops 7219445760 | bytes 13418496 | tf_op jit(solution)/shard_map/up_grads/pallas_call | solution.py:741
  199.9 2.6 copy-done.11
  202.5 18.0 %attend_back.3 = (bf16[1224,256]{1,0:T(8,128)(2,1)S(1)}, bf16[1224,256]{1,0:T(8,128)(2,1)S(1)}, bf16[1224,256]{1,0:T(8,128)(2,1)S(1)}) custom-call(s32[1]{0:T(128)S(6)} %copy.37.len_ref, bf16[1224,2304]{1,0:T(8,128)(2,1)S(1)} %copy-done.11, bf16[1224,2304]{1,0:T(8,128)(2,1)S(1)} %copy-done.11, bf16[1224,2304]{1,0:T(8,128)(2,1)S(1)} %copy-done.11, ...), custom_call_target="tpu_custom_call" | custom-call | flops 15341322240 | bytes 15040512 | tf_op jit(solution)/shard_map/attend_back/pallas_call | solution.py:437
  220.5 8.6 %attend_back.4 = (bf16[1224,128]{1,0:T(8,128)(2,1)S(1)}, bf16[1224,128]{1,0:T(8,128)(2,1)S(1)}, bf16[1224,128]{1,0:T(8,128)(2,1)S(1)}) custom-call(s32[1]{0:T(128)S(6)} %copy.37.len_ref, bf16[1224,2304]{1,0:T(8,128)(2,1)S(1)} %copy-done.11, bf16[1224,2304]{1,0:T(8,128)(2,1)S(1)} %copy-done.11, bf16[1224,2304]{1,0:T(8,128)(2,1)S(1)} %copy-done.11, ...), custom_call_target="tpu_custom_call" | custom-call | flops 7670661120 | bytes 15040512 | tf_op jit(solution)/shard_map/attend_back/pallas_call | solution.py:437
  229.1 3.8 %fusion.3 = (bf16[480,768]{1,0:T(8,128)(2,1)S(1)}, bf16[480,768]{1,0:T(8,128)(2,1)}, bf16[480,768]{1,0:T(8,128)(2,1)}, bf16[480,768]{1,0:T(8,128)(2,1)S(1)}) fusion(bf16[4,480,768]{2,1,0:T(8,128)(2,1)} %collective-permute-done.30, bf16[4,480,768]{2,1,0:T(8,128)(2,1)S(1)} %get-tuple-element.229), kind=kLoop, calls=%fused_computation.14 | loop fusion | flops 5898240 | bytes 8847360 | tf_op jit(solution)/shard_map/convert_element_type | solution.py:1099
  238.9 26.6 %attend_back.5 = (bf16[1224,384]{1,0:T(8,128)(2,1)S(1)}, bf16[1224,384]{1,0:T(8,128)(2,1)S(1)}, bf16[1224,384]{1,0:T(8,128)(2,1)S(1)}) custom-call(s32[1]{0:T(128)S(6)} %copy.37.len_ref, bf16[1224,2304]{1,0:T(8,128)(2,1)S(1)} %copy-done.11, bf16[1224,2304]{1,0:T(8,128)(2,1)S(1)} %copy-done.11, bf16[1224,2304]{1,0:T(8,128)(2,1)S(1)} %copy-done.11, ...), custom_call_target="tpu_custom_call" | custom-call | flops 23011983360 | bytes 15040512 | tf_op jit(solution)/shard_map/attend_back/pallas_call | solution.py:437
  274.3 12.4 %qkv_grads.1 = (bf16[4,288,768]{2,1,0:T(8,128)(2,1)S(1)}, bf16[4,288,768]{2,1,0:T(8,128)(2,1)S(1)}) custom-call(s32[32]{0:T(128)S(1)} %copy-done.3, bf16[1224,256]{1,0:T(8,128)(2,1)S(1)} %get-tuple-element.252.refs_0_, bf16[1224,256]{1,0:T(8,128)(2,1)S(1)} %get-tuple-element.253.refs_1_, bf16[1224,256]{1,0:T(8,128)(2,1)S(1)} %get-tuple-element.254.refs_2_, ...), custom_call_target="tpu_custom_call" | custom-call | flops 4331667456 | bytes 11059200 | tf_op jit(solution)/shard_map/qkv_grads/pallas_call | solution.py:802
  287.7 2.8 collective-permute-done.40
  296.3 13.8 %last.1 = (f32[1224,768]{1,0:T(8,128)}, f32[16,768]{1,0:T(8,128)S(1)}) custom-call(s32[32]{0:T(128)S(1)} %copy-done.3, bf16[1224,768]{1,0:T(8,128)(2,1)S(1)} %copy-done.5, f32[1224,768]{1,0:T(8,128)} %get-tuple-element.278.d_resid_ref, f32[16,768]{1,0:T(8,128)S(1)} %copy-done.13, f32[16,768]{1,0:T(8,128)S(1)} %copy-done.14, ...), custom_call_target="tpu_custom_call" | custom-call | flops 4331667456 | bytes 15040512 | tf_op jit(solution)/shard_map/last/pallas_call | solution.py:862
  312.2 3.4 collective-permute-done.43
  316.4 3.3 collective-permute-done.44
  324.0 2.5 collective-permute-start.52
  328.0 10.6 %collective-permute-done.49 = f32[16,768]{1,0:T(8,128)S(1)} collective-permute-done((f32[16,768]{1,0:T(8,128)S(1)}, f32[16,768]{1,0:T(8,128)S(1)}, u32[]{:S(2)}, u32[]{:S(2)}) %collective-permute-start.49) | collective-permute-done | bytes 49184 | tf_op jit(solution)/shard_map/ppermute | solution.py:930
  (191 shorter events, 78.6 us)
Async XLA Ops:
  2.6 25.9 %collective-permute-start.3 = (bf16[192,896]{1,0:T(8,128)(2,1)}, bf16[192,896]{1,0:T(8,128)(2,1)S(1)}, u32[]{:S(2)}, u32[]{:S(2)}) collective-permute-start(bf16[192,896]{1,0:T(8,128)(2,1)} %get-tuple-element.160.own_ref), channel_id=1, source_target_pairs={{0,8},{8,0},{16,24},{24,16},{1,9},{9,1},{17,25},{25,17},{2,10},{10... | collective-permute-start | bytes 1032200 | tf_op jit(solution)/shard_map/ppermute | solution.py:930
  8.7 17.3 %collective-permute-start.2 = (bf16[200,288]{1,0:T(8,128)(2,1)}, bf16[200,288]{1,0:T(8,128)(2,1)S(1)}, u32[]{:S(2)}, u32[]{:S(2)}) collective-permute-start(bf16[200,288]{1,0:T(8,128)(2,1)} %get-tuple-element.161.refs_0_), channel_id=1, source_target_pairs={{0,24},{8,16},{16,8},{24,0},{1,25},{9,17},{17,9},{25,1},{2,26},{10... | collective-permute-start | bytes 345608 | tf_op jit(solution)/shard_map/ppermute | solution.py:930
  28.6 20.9 %collective-permute-start.5 = (bf16[304,768]{1,0:T(8,128)(2,1)S(1)}, bf16[304,768]{1,0:T(8,128)(2,1)S(1)}, u32[]{:S(2)}, u32[]{:S(2)}) collective-permute-start(bf16[304,768]{1,0:T(8,128)(2,1)S(1)} %arrange_qkv.1.refs_0_.refs_9_), channel_id=1, source_target_pairs={{0,2},{1,3},{2,0},{3,1},{4,6},{5,7},{6,4},{7,5},{8,10},{9,11},{10,... | collective-permute-start | bytes 1400840 | tf_op jit(solution)/shard_map/ppermute | solution.py:930
  30.1 21.3 %collective-permute-start.6 = (bf16[304,768]{1,0:T(8,128)(2,1)S(1)}, bf16[304,768]{1,0:T(8,128)(2,1)S(1)}, u32[]{:S(2)}, u32[]{:S(2)}) collective-permute-start(bf16[304,768]{1,0:T(8,128)(2,1)S(1)} %arrange_qkv.1.refs_0_.refs_9_), channel_id=1, source_target_pairs={{0,4},{1,5},{2,6},{3,7},{4,0},{5,1},{6,2},{7,3},{8,12},{9,13},{10,... | collective-permute-start | bytes 1400840 | tf_op jit(solution)/shard_map/ppermute | solution.py:930
  31.7 19.8 %collective-permute-start.7 = (bf16[304,768]{1,0:T(8,128)(2,1)S(1)}, bf16[304,768]{1,0:T(8,128)(2,1)}, u32[]{:S(2)}, u32[]{:S(2)}) collective-permute-start(bf16[304,768]{1,0:T(8,128)(2,1)S(1)} %arrange_qkv.1.refs_0_.refs_9_), channel_id=1, source_target_pairs={{0,6},{1,7},{2,4},{3,5},{4,2},{5,3},{6,0},{7,1},{8,14},{9,15},{10,... | collective-permute-start | bytes 1400840 | tf_op jit(solution)/shard_map/ppermute | solution.py:930
  32.2 17.2 %collective-permute-start.4 = (bf16[384,512]{1,0:T(8,128)(2,1)S(1)}, bf16[384,512]{1,0:T(8,128)(2,1)S(1)}, u32[]{:S(2)}, u32[]{:S(2)}) collective-permute-start(bf16[384,512]{1,0:T(8,128)(2,1)S(1)} %pad_maximum_fusion.4), channel_id=1, source_target_pairs={{0,16},{8,24},{16,0},{24,8},{1,17},{9,25},{17,1},{25,9},{2,18},{10... | collective-permute-start | bytes 1179656 | tf_op jit(solution)/shard_map/ppermute | solution.py:930
  54.2 17.0 %collective-permute-start.8 = (bf16[240,768]{1,0:T(8,128)(2,1)S(1)}, bf16[240,768]{1,0:T(8,128)(2,1)S(1)}, u32[]{:S(2)}, u32[]{:S(2)}) collective-permute-start(bf16[240,768]{1,0:T(8,128)(2,1)S(1)} %get-tuple-element.168), channel_id=1, source_target_pairs={{0,2},{1,3},{2,0},{3,1},{4,6},{5,7},{6,4},{7,5},{8,10},{9,11},{10,... | collective-permute-start | bytes 1105928 | tf_op jit(solution)/shard_map/ppermute | solution.py:930
  73.9 18.8 %collective-permute-start.15 = (bf16[192,768]{1,0:T(8,128)(2,1)S(1)}, bf16[192,768]{1,0:T(8,128)(2,1)}, u32[]{:S(2)}, u32[]{:S(2)}) collective-permute-start(bf16[192,768]{1,0:T(8,128)(2,1)S(1)} %get-tuple-element.183), channel_id=1, source_target_pairs={{0,2},{1,3},{2,0},{3,1},{4,6},{5,7},{6,4},{7,5},{8,10},{9,11},{10,... | collective-permute-start | bytes 884744 | tf_op jit(solution)/shard_map/ppermute | solution.py:930
  75.4 17.4 %collective-permute-start.16 = (bf16[192,768]{1,0:T(8,128)(2,1)}, bf16[192,768]{1,0:T(8,128)(2,1)}, u32[]{:S(2)}, u32[]{:S(2)}) collective-permute-start(bf16[192,768]{1,0:T(8,128)(2,1)} %get-tuple-element.187), channel_id=1, source_target_pairs={{0,4},{1,5},{2,6},{3,7},{4,0},{5,1},{6,2},{7,3},{8,12},{9,13},{10,... | collective-permute-start | bytes 884744 | tf_op jit(solution)/shard_map/ppermute | solution.py:930
  75.9 37.5 %collective-permute-start.17 = (bf16[480,768]{1,0:T(8,128)(2,1)}, bf16[480,768]{1,0:T(8,128)(2,1)}, u32[]{:S(2)}, u32[]{:S(2)}) collective-permute-start(bf16[480,768]{1,0:T(8,128)(2,1)} %pad_maximum_fusion.refs_0_), channel_id=1, source_target_pairs={{0,4},{1,5},{2,6},{3,7},{4,0},{5,1},{6,2},{7,3},{8,12},{9,13},{10,... | collective-permute-start | bytes 2211848 | tf_op jit(solution)/shard_map/ppermute | solution.py:930
  77.4 36.0 %collective-permute-start.18 = (bf16[480,768]{1,0:T(8,128)(2,1)}, bf16[480,768]{1,0:T(8,128)(2,1)}, u32[]{:S(2)}, u32[]{:S(2)}) collective-permute-start(bf16[480,768]{1,0:T(8,128)(2,1)} %pad_maximum_fusion.1.refs_4_), channel_id=1, source_target_pairs={{0,2},{1,3},{2,0},{3,1},{4,6},{5,7},{6,4},{7,5},{8,10},{9,11},{10,... | collective-permute-start | bytes 2211848 | tf_op jit(solution)/shard_map/ppermute | solution.py:930
  96.6 16.9 %collective-permute-start.19 = (bf16[384,768]{1,0:T(8,128)(2,1)}, bf16[384,768]{1,0:T(8,128)(2,1)}, u32[]{:S(2)}, u32[]{:S(2)}) collective-permute-start(bf16[384,768]{1,0:T(8,128)(2,1)} %pad_maximum_fusion.2.refs_8_), channel_id=1, source_target_pairs={{0,4},{1,5},{2,6},{3,7},{4,0},{5,1},{6,2},{7,3},{8,12},{9,13},{10,... | collective-permute-start | bytes 1769480 | tf_op jit(solution)/shard_map/ppermute | solution.py:930
  177.6 19.0 %collective-permute-start.29 = (bf16[4,4,96,768]{3,2,1,0:T(8,128)(2,1)}, bf16[4,4,96,768]{3,2,1,0:T(8,128)(2,1)S(1)}, u32[]{:S(2)}, u32[]{:S(2)}) collective-permute-start(bf16[4,4,96,768]{3,2,1,0:T(8,128)(2,1)} %get-tuple-element.216), channel_id=1, source_target_pairs={{0,1},{1,0},{2,3},{3,2},{4,5},{5,4},{6,7},{7,6},{8,9},{9,8},{10,11... | collective-permute-start | bytes 7077896 | tf_op jit(solution)/shard_map/ppermute | solution.py:930
  196.1 33.0 %collective-permute-start.30 = (bf16[4,480,768]{2,1,0:T(8,128)(2,1)S(1)}, bf16[4,480,768]{2,1,0:T(8,128)(2,1)}, u32[]{:S(2)}, u32[]{:S(2)}) collective-permute-start(bf16[4,480,768]{2,1,0:T(8,128)(2,1)S(1)} %get-tuple-element.228), channel_id=1, source_target_pairs={{0,1},{1,0},{2,3},{3,2},{4,5},{5,4},{6,7},{7,6},{8,9},{9,8},{10,11... | collective-permute-start | bytes 8847368 | tf_op jit(solution)/shard_map/ppermute | solution.py:930
  198.0 38.4 %collective-permute-start.31 = (bf16[2,4,96,768]{3,2,1,0:T(8,128)(2,1)S(1)}, bf16[2,4,96,768]{3,2,1,0:T(8,128)(2,1)S(1)}, u32[]{:S(2)}, u32[]{:S(2)}) collective-permute-start(bf16[2,4,96,768]{3,2,1,0:T(8,128)(2,1)S(1)} %add_convert_fusion), channel_id=1, source_target_pairs={{0,8},{8,0},{16,24},{24,16},{1,9},{9,1},{17,25},{25,17},{2,10},{10... | collective-permute-start | bytes 3538952 | tf_op jit(solution)/shard_map/ppermute | solution.py:930
  232.9 32.6 %collective-permute-start.33 = (bf16[480,768]{1,0:T(8,128)(2,1)}, bf16[480,768]{1,0:T(8,128)(2,1)S(1)}, u32[]{:S(2)}, u32[]{:S(2)}) collective-permute-start(bf16[480,768]{1,0:T(8,128)(2,1)} %get-tuple-element.240), channel_id=1, source_target_pairs={{0,2},{1,3},{2,0},{3,1},{4,6},{5,7},{6,4},{7,5},{8,10},{9,11},{10,... | collective-permute-start | bytes 2211848 | tf_op jit(solution)/shard_map/ppermute | solution.py:930
  234.3 32.5 %collective-permute-start.34 = (bf16[480,768]{1,0:T(8,128)(2,1)}, bf16[480,768]{1,0:T(8,128)(2,1)S(1)}, u32[]{:S(2)}, u32[]{:S(2)}) collective-permute-start(bf16[480,768]{1,0:T(8,128)(2,1)} %get-tuple-element.241), channel_id=1, source_target_pairs={{0,4},{1,5},{2,6},{3,7},{4,0},{5,1},{6,2},{7,3},{8,12},{9,13},{10,... | collective-permute-start | bytes 2211848 | tf_op jit(solution)/shard_map/ppermute | solution.py:930
  235.2 33.1 %collective-permute-start.35 = (bf16[480,768]{1,0:T(8,128)(2,1)S(1)}, bf16[480,768]{1,0:T(8,128)(2,1)S(1)}, u32[]{:S(2)}, u32[]{:S(2)}) collective-permute-start(bf16[480,768]{1,0:T(8,128)(2,1)S(1)} %get-tuple-element.242), channel_id=1, source_target_pairs={{0,6},{1,7},{2,4},{3,5},{4,2},{5,3},{6,0},{7,1},{8,14},{9,15},{10,... | collective-permute-start | bytes 2211848 | tf_op jit(solution)/shard_map/ppermute | solution.py:930
  236.9 31.4 %collective-permute-start.32 = (bf16[4,96,768]{2,1,0:T(8,128)(2,1)S(1)}, bf16[4,96,768]{2,1,0:T(8,128)(2,1)S(1)}, u32[]{:S(2)}, u32[]{:S(2)}) collective-permute-start(bf16[4,96,768]{2,1,0:T(8,128)(2,1)S(1)} %get-tuple-element.239), channel_id=1, source_target_pairs={{0,16},{8,24},{16,0},{24,8},{1,17},{9,25},{17,1},{25,9},{2,18},{10... | collective-permute-start | bytes 1769480 | tf_op jit(solution)/shard_map/ppermute | solution.py:930
  269.5 17.2 %collective-permute-start.36 = (bf16[2,192,480]{2,1,0:T(8,128)(2,1)S(1)}, bf16[2,192,480]{2,1,0:T(8,128)(2,1)S(1)}, u32[]{:S(2)}, u32[]{:S(2)}) collective-permute-start(bf16[2,192,480]{2,1,0:T(8,128)(2,1)S(1)} %get-tuple-element.264), channel_id=1, source_target_pairs={{0,8},{8,0},{16,24},{24,16},{1,9},{9,1},{17,25},{25,17},{2,10},{10... | collective-permute-start | bytes 1105928 | tf_op jit(solution)/shard_map/ppermute | solution.py:930
  290.9 19.2 %collective-permute-start.41 = (bf16[192,480]{1,0:T(8,128)(2,1)S(1)}, bf16[192,480]{1,0:T(8,128)(2,1)S(1)}, u32[]{:S(2)}, u32[]{:S(2)}) collective-permute-start(bf16[192,480]{1,0:T(8,128)(2,1)S(1)} %fusion.9), channel_id=1, source_target_pairs={{0,16},{8,24},{16,0},{24,8},{1,17},{9,25},{17,1},{25,9},{2,18},{10... | collective-permute-start | bytes 552968 | tf_op jit(solution)/shard_map/ppermute | solution.py:930
  292.8 26.9 %collective-permute-start.45 = (bf16[288,768]{1,0:T(8,128)(2,1)S(1)}, bf16[288,768]{1,0:T(8,128)(2,1)S(1)}, u32[]{:S(2)}, u32[]{:S(2)}) collective-permute-start(bf16[288,768]{1,0:T(8,128)(2,1)S(1)} %get-tuple-element.287), channel_id=1, source_target_pairs={{0,2},{1,3},{2,0},{3,1},{4,6},{5,7},{6,4},{7,5},{8,10},{9,11},{10,... | collective-permute-start | bytes 1327112 | tf_op jit(solution)/shard_map/ppermute | solution.py:930
  293.5 26.2 %collective-permute-start.46 = (bf16[288,768]{1,0:T(8,128)(2,1)S(1)}, bf16[288,768]{1,0:T(8,128)(2,1)S(1)}, u32[]{:S(2)}, u32[]{:S(2)}) collective-permute-start(bf16[288,768]{1,0:T(8,128)(2,1)S(1)} %get-tuple-element.288), channel_id=1, source_target_pairs={{0,4},{1,5},{2,6},{3,7},{4,0},{5,1},{6,2},{7,3},{8,12},{9,13},{10,... | collective-permute-start | bytes 1327112 | tf_op jit(solution)/shard_map/ppermute | solution.py:930
  295.1 24.7 %collective-permute-start.47 = (bf16[288,768]{1,0:T(8,128)(2,1)S(1)}, bf16[288,768]{1,0:T(8,128)(2,1)S(1)}, u32[]{:S(2)}, u32[]{:S(2)}) collective-permute-start(bf16[288,768]{1,0:T(8,128)(2,1)S(1)} %get-tuple-element.289), channel_id=1, source_target_pairs={{0,6},{1,7},{2,4},{3,5},{4,2},{5,3},{6,0},{7,1},{8,14},{9,15},{10,... | collective-permute-start | bytes 1327112 | tf_op jit(solution)/shard_map/ppermute | solution.py:930
  (58 other events, 590.6 us)

commit v4 on v3

--- a/solution.py
+++ b/solution.py
@@ -752,7 +752,7 @@
             ],
         ),
         out_shape=[out, out],
-        compiler_params=params(40),
+        compiler_params=params(63),
         cost_estimate=cost(
             2 * slots * width * (hidden + width), slots * hidden * 2 + out.size * 4
         ),
@@ -760,28 +760,15 @@
     )(table, d_inner, normed, d_branch, mixed)
 
 
-def qkv_grads_kernel(table, *refs, count):
-    parts_in, normed_ref, (keep_ref, send_ref) = (
-        refs[:count],
-        refs[count],
-        refs[count + 1 : count + 3],
-    )
-    sums, sems, loads = refs[-3:]
-    local, sources = refs[-3 - count : -3], parts_in
+def qkv_grads_kernel(table, *refs):
+    parts_in, normed_ref, (keep_ref, send_ref, sums, sems) = refs[:-5], refs[-5], refs[-4:]
     width = normed_ref.shape[1]
     block = sums.shape[0] // BLOCKS
-    groups = count // 3
-    copies = [
-        pltpu.make_async_copy(sources[i], local[i], loads.at[i]) for i in range(count)
-    ]
-    for s in range(3):
-        for i in range(groups):
-            copies[i * 3 + s].start()
+    groups = len(parts_in) // 3
     for s in range(3):
         start = s * width
         for i in range(groups):
-            copies[i * 3 + s].wait()
-            part = local[i * 3 + s]
+            part = parts_in[i * 3 + s]
             sums[start : start + part.shape[1], :] = tn(part[...], normed_ref[...]).astype(BF)
             start += part.shape[1]
     copies = [
@@ -800,21 +787,19 @@
     slots, width = normed.shape
     out = jax.ShapeDtypeStruct((4, 3 * width // BLOCKS, width), BF)
     return pl.pallas_call(
-        functools.partial(qkv_grads_kernel, count=len(d_parts)),
+        qkv_grads_kernel,
         grid_spec=pltpu.PrefetchScalarGridSpec(
             num_scalar_prefetch=1,
             grid=(1,),
-            in_specs=[ANY] * len(d_parts) + [whole((slots, width))],
+            in_specs=[whole(part.shape) for part in d_parts] + [whole((slots, width))],
             out_specs=[ANY] * 2,
-            scratch_shapes=[pltpu.VMEM(part.shape, BF) for part in d_parts]
-            + [
+            scratch_shapes=[
                 pltpu.VMEM((3 * width, width), BF),
                 pltpu.SemaphoreType.DMA((BLOCKS,)),
-                pltpu.SemaphoreType.DMA((len(d_parts),)),
             ],
         ),
         out_shape=[out, out],
-        compiler_params=params(32),
+        compiler_params=params(40),
         cost_estimate=cost(6 * slots * width * width, slots * width * 8 + out.size * 4),
         name="qkv_grads",
     )(table, *d_parts, normed)

time: 344 us -> 336 us (0.977)
  local copies, waits for them, and re-layouts: 16.9 us -> 12.7 us
  Pallas kernels: 196 us -> 192 us
    pallas_call x1, Pallas kernels: 12.4 us -> 7.47 us  [qkv_grads(): pl.pallas_call(qkv_grads_kernel, grid_spec=pltpu.PrefetchScalarGridSpec(n...]
    unnamed x58 -> x50, local copies, waits for them, and re-layouts: 13.2 us -> 9.05 us
where the time goes in v4:
time: 336 us; the launch traced here: 332 us
  Pallas kernels  192 us (57%)
  waiting for transfers between devices  64.2 us (19%)
  starting transfers between devices  46.4 us (14%)
  other arithmetic  14.9 us (4%)
  local copies, waits for them, and re-layouts  12.7 us (4%)
    ppermute x53, waiting for transfers between devices, swap(): return lax.ppermute(values, axis, [(i, i ^ mask) for i in range(size)])  64.2 us
    pallas_call x3, Pallas kernels, attend_back(): pl.pallas_call(functools.partial(attend_back_kernel, slots=slots, padded=...  53.4 us
    ppermute x53, starting transfers between devices, swap(): return lax.ppermute(values, axis, [(i, i ^ mask) for i in range(size)])  46.4 us
    pallas_call x1, Pallas kernels, middle(): pl.pallas_call(functools.partial(middle_kernel, chunk=chunk), grid_spec=p...  43.1 us
    pallas_call x2, Pallas kernels, attend(): pl.pallas_call(functools.partial(attend_kernel, slots=slots, padded=padde...  29.8 us
    pallas_call x1, Pallas kernels, up_grads(): pl.pallas_call(up_grads_kernel, grid_spec=pltpu.PrefetchScalarGridSpec(nu...  14.2 us
    pallas_call x1, Pallas kernels, last(): pl.pallas_call(functools.partial(last_kernel, groups=len(d_parts) // 3),...  13.8 us
    pallas_call x1, Pallas kernels, down_grads(): pl.pallas_call(down_grads_kernel, grid_spec=pltpu.PrefetchScalarGridSpec(...  11.7 us
  transfers between devices with their start and end apart: 53, of which 16 were waited for; matrix products, arithmetic and copies ran while one was open for 4% of the time, Pallas kernels for 40%

profile of v4, /device:TPU:0, one launch (start us, length us, event | category | flops | bytes accessed | tf_op | source)
XLA Modules:
  0.0 332.1 jit_solution(9663160052991147647)
XLA Ops:
  2.6 3.0 collective-permute-start.3
  5.7 3.0 collective-permute-start.1
  11.1 9.5 %collective-permute-done.refs_1_ = bf16[200,288]{1,0:T(8,128)(2,1)S(1)} collective-permute-done((bf16[200,288]{1,0:T(8,128)(2,1)}, bf16[200,288]{1,0:T(8,128)(2,1)S(1)}, u32[]{:S(2)}, u32[]{:S(2)}) %collective-permute-start) | collective-permute-done | bytes 115232 | tf_op jit(solution)/shard_map/ppermute | solution.py:915
  21.0 5.0 %collective-permute-done.2.refs_3_ = bf16[200,288]{1,0:T(8,128)(2,1)S(1)} collective-permute-done((bf16[200,288]{1,0:T(8,128)(2,1)}, bf16[200,288]{1,0:T(8,128)(2,1)S(1)}, u32[]{:S(2)}, u32[]{:S(2)}) %collective-permute-start.2) | collective-permute-done | bytes 115232 | tf_op jit(solution)/shard_map/ppermute | solution.py:915
  32.3 17.2 %collective-permute-done.4.far_ref = bf16[384,512]{1,0:T(8,128)(2,1)S(1)} collective-permute-done((bf16[384,512]{1,0:T(8,128)(2,1)S(1)}, bf16[384,512]{1,0:T(8,128)(2,1)S(1)}, u32[]{:S(2)}, u32[]{:S(2)}) %collective-permute-start.4) | collective-permute-done | bytes 393248 | tf_op jit(solution)/shard_map/ppermute | solution.py:915
  57.9 10.8 %project.1 = (bf16[1224,2304]{1,0:T(8,128)(2,1)S(1)}, bf16[1224,768]{1,0:T(8,128)(2,1)S(1)}, f32[16,768]{1,0:T(8,128)S(1)}) custom-call(s32[32]{0:T(128)S(1)} %concatenate.23.table, bf16[1224,768]{1,0:T(8,128)(2,1)S(1)} %copy-done.4, bf16[304,768]{1,0:T(8,128)(2,1)S(1)} %arrange_qkv.1.refs_0_.refs_9_, ...), custom_call_target="tpu_custom_call" | custom-call | flops 4331667456 | bytes 9400320 | tf_op jit(solution)/shard_map/project/pallas_call | solution.py:265
  68.8 2.4 copy-done.10
  78.0 14.8 %attend.2 = (bf16[1224,768]{1,0:T(8,128)(2,1)}, f32[6,8,1280]{2,1,0:T(8,128)}) custom-call(s32[1]{0:T(128)S(6)} %copy.37.len_ref, bf16[1224,2304]{1,0:T(8,128)(2,1)} %copy-done.10, bf16[1224,2304]{1,0:T(8,128)(2,1)} %copy-done.10, bf16[1224,2304]{1,0:T(8,128)(2,1)} %copy-done.10), custom_call_target="tpu_custom_call" | custom-call | flops 9204793344 | bytes 7520256 | tf_op jit(solution)/shard_map/attend/pallas_call | solution.py:332
  98.6 15.0 %attend.3 = (bf16[1224,768]{1,0:T(8,128)(2,1)}, f32[6,8,1280]{2,1,0:T(8,128)}) custom-call(s32[1]{0:T(128)S(6)} %copy.37.len_ref, bf16[1224,2304]{1,0:T(8,128)(2,1)} %copy-done.10, bf16[1224,2304]{1,0:T(8,128)(2,1)} %copy-done.10, bf16[1224,2304]{1,0:T(8,128)(2,1)} %copy-done.10, ...), custom_call_target="tpu_custom_call", output_to_operand_aliasing={{0}: (4, {}), {1}: (5, {})} | custom-call | flops 9204793344 | bytes 7520256 | tf_op jit(solution)/shard_map/attend/pallas_call | solution.py:332
  117.8 4.9 %collective-permute-done.28.refs_15_ = bf16[384,768]{1,0:T(8,128)(2,1)} collective-permute-done((bf16[384,768]{1,0:T(8,128)(2,1)}, bf16[384,768]{1,0:T(8,128)(2,1)}, u32[]{:S(2)}, u32[]{:S(2)}) %collective-permute-start.28) | collective-permute-done | bytes 589856 | tf_op jit(solution)/shard_map/ppermute | solution.py:915
  122.8 43.1 %middle.1 = (bf16[1224,768]{1,0:T(8,128)(2,1)}, bf16[1224,3072]{1,0:T(8,128)(2,1)}, bf16[1224,3072]{1,0:T(8,128)(2,1)}, bf16[1224,768]{1,0:T(8,128)(2,1)}, f32[1...) custom-call(s32[1]{0:T(128)S(6)} %copy.37.len_ref, s32[32]{0:T(128)} %copy-done.2, ...), custom_call_target="tpu_custom_call" | custom-call | flops 25990004736 | bytes 41398272 | tf_op jit(solution)/shard_map/middle/pallas_call | solution.py:584
  165.9 11.7 %down_grads.1 = (bf16[4,4,96,768]{3,2,1,0:T(8,128)(2,1)}, bf16[4,4,96,768]{3,2,1,0:T(8,128)(2,1)}) custom-call(s32[1]{0:T(128)S(6)} %copy.37.len_ref, s32[32]{0:T(128)} %copy-done.2, bf16[1224,3072]{1,0:T(8,128)(2,1)} %get-tuple-element.211.active_ref, bf16[1224,768]{1,0:T(8,128)(2,1)} %cot_ref.3), custom_call_target="tpu_custom_call" | custom-call | flops 5775556608 | bytes 12238848 | tf_op jit(solution)/shard_map/down_grads/pallas_call | solution.py:673
  177.8 14.2 %up_grads.1 = (bf16[4,480,768]{2,1,0:T(8,128)(2,1)}, bf16[4,480,768]{2,1,0:T(8,128)(2,1)}) custom-call(s32[32]{0:T(128)} %copy-done.2, bf16[1224,3072]{1,0:T(8,128)(2,1)} %get-tuple-element.217.d_inner_ref, bf16[1224,768]{1,0:T(8,128)(2,1)} %get-tuple-element.218.normed_ref, bf16[1224,768]{1,0:T(8,128)(2,1)} %get-tuple-element.219.d_branch_ref, ...), custom_call_target="tpu_custom_call" | custom-call | flops 7219445760 | bytes 13418496 | tf_op jit(solution)/shard_map/up_grads/pallas_call | solution.py:741
  196.5 2.6 copy-done.11
  200.6 18.0 %attend_back.3 = (bf16[1224,256]{1,0:T(8,128)(2,1)S(1)}, bf16[1224,256]{1,0:T(8,128)(2,1)S(1)}, bf16[1224,256]{1,0:T(8,128)(2,1)S(1)}) custom-call(s32[1]{0:T(128)S(6)} %copy.37.len_ref, bf16[1224,2304]{1,0:T(8,128)(2,1)S(1)} %copy-done.11, bf16[1224,2304]{1,0:T(8,128)(2,1)S(1)} %copy-done.11, bf16[1224,2304]{1,0:T(8,128)(2,1)S(1)} %copy-done.11, ...), custom_call_target="tpu_custom_call" | custom-call | flops 15341322240 | bytes 15040512 | tf_op jit(solution)/shard_map/attend_back/pallas_call | solution.py:437
  218.6 8.6 %attend_back.4 = (bf16[1224,128]{1,0:T(8,128)(2,1)S(1)}, bf16[1224,128]{1,0:T(8,128)(2,1)S(1)}, bf16[1224,128]{1,0:T(8,128)(2,1)S(1)}) custom-call(s32[1]{0:T(128)S(6)} %copy.37.len_ref, bf16[1224,2304]{1,0:T(8,128)(2,1)S(1)} %copy-done.11, bf16[1224,2304]{1,0:T(8,128)(2,1)S(1)} %copy-done.11, bf16[1224,2304]{1,0:T(8,128)(2,1)S(1)} %copy-done.11, ...), custom_call_target="tpu_custom_call" | custom-call | flops 7670661120 | bytes 15040512 | tf_op jit(solution)/shard_map/attend_back/pallas_call | solution.py:437
  235.8 26.8 %attend_back.5 = (bf16[1224,384]{1,0:T(8,128)(2,1)S(1)}, bf16[1224,384]{1,0:T(8,128)(2,1)S(1)}, bf16[1224,384]{1,0:T(8,128)(2,1)S(1)}) custom-call(s32[1]{0:T(128)S(6)} %copy.37.len_ref, bf16[1224,2304]{1,0:T(8,128)(2,1)S(1)} %copy-done.11, bf16[1224,2304]{1,0:T(8,128)(2,1)S(1)} %copy-done.11, bf16[1224,2304]{1,0:T(8,128)(2,1)S(1)} %copy-done.11, ...), custom_call_target="tpu_custom_call" | custom-call | flops 23011983360 | bytes 15040512 | tf_op jit(solution)/shard_map/attend_back/pallas_call | solution.py:437
  269.9 7.5 %qkv_grads.1 = (bf16[4,288,768]{2,1,0:T(8,128)(2,1)S(1)}, bf16[4,288,768]{2,1,0:T(8,128)(2,1)S(1)}) custom-call(s32[32]{0:T(128)S(1)} %copy-done.3, bf16[1224,256]{1,0:T(8,128)(2,1)S(1)} %get-tuple-element.252.refs_0_, bf16[1224,256]{1,0:T(8,128)(2,1)S(1)} %get-tuple-element.253.refs_1_, bf16[1224,256]{1,0:T(8,128)(2,1)S(1)} %get-tuple-element.254.refs_2_, ...), custom_call_target="tpu_custom_call" | custom-call | flops 4331667456 | bytes 11059200 | tf_op jit(solution)/shard_map/qkv_grads/pallas_call | solution.py:789
  278.3 2.8 collective-permute-done.40
  281.6 2.5 collective-permute-start.41
  287.6 13.8 %last.1 = (f32[1224,768]{1,0:T(8,128)}, f32[16,768]{1,0:T(8,128)S(1)}) custom-call(s32[32]{0:T(128)S(1)} %copy-done.3, bf16[1224,768]{1,0:T(8,128)(2,1)S(1)} %copy-done.5, f32[1224,768]{1,0:T(8,128)} %get-tuple-element.278.d_resid_ref, f32[16,768]{1,0:T(8,128)S(1)} %copy-done.13, f32[16,768]{1,0:T(8,128)S(1)} %copy-done.14, ...), custom_call_target="tpu_custom_call" | custom-call | flops 4331667456 | bytes 15040512 | tf_op jit(solution)/shard_map/last/pallas_call | solution.py:847
  303.4 3.4 %collective-permute-done.43 = f32[16,768]{1,0:T(8,128)S(1)} collective-permute-done((f32[16,768]{1,0:T(8,128)S(1)}, f32[16,768]{1,0:T(8,128)S(1)}, u32[]{:S(2)}, u32[]{:S(2)}) %collective-permute-start.43) | collective-permute-done | bytes 49184 | tf_op jit(solution)/shard_map/ppermute | solution.py:915
  307.6 3.4 %collective-permute-done.44 = f32[16,768]{1,0:T(8,128)S(1)} collective-permute-done((f32[16,768]{1,0:T(8,128)S(1)}, f32[16,768]{1,0:T(8,128)S(1)}, u32[]{:S(2)}, u32[]{:S(2)}) %collective-permute-start.44) | collective-permute-done | bytes 49184 | tf_op jit(solution)/shard_map/ppermute | solution.py:915
  319.9 9.9 %collective-permute-done.49 = f32[16,768]{1,0:T(8,128)S(1)} collective-permute-done((f32[16,768]{1,0:T(8,128)S(1)}, f32[16,768]{1,0:T(8,128)S(1)}, u32[]{:S(2)}, u32[]{:S(2)}) %collective-permute-start.49) | collective-permute-done | bytes 49184 | tf_op jit(solution)/shard_map/ppermute | solution.py:915
  (183 shorter events, 76.3 us)
Async XLA Ops:
  2.6 25.9 %collective-permute-start.3 = (bf16[192,896]{1,0:T(8,128)(2,1)}, bf16[192,896]{1,0:T(8,128)(2,1)S(1)}, u32[]{:S(2)}, u32[]{:S(2)}) collective-permute-start(bf16[192,896]{1,0:T(8,128)(2,1)} %get-tuple-element.160.own_ref), channel_id=1, source_target_pairs={{0,8},{8,0},{16,24},{24,16},{1,9},{9,1},{17,25},{25,17},{2,10},{10... | collective-permute-start | bytes 1032200 | tf_op jit(solution)/shard_map/ppermute | solution.py:915
  8.7 17.3 %collective-permute-start.2 = (bf16[200,288]{1,0:T(8,128)(2,1)}, bf16[200,288]{1,0:T(8,128)(2,1)S(1)}, u32[]{:S(2)}, u32[]{:S(2)}) collective-permute-start(bf16[200,288]{1,0:T(8,128)(2,1)} %get-tuple-element.161.refs_0_), channel_id=1, source_target_pairs={{0,24},{8,16},{16,8},{24,0},{1,25},{9,17},{17,9},{25,1},{2,26},{10... | collective-permute-start | bytes 345608 | tf_op jit(solution)/shard_map/ppermute | solution.py:915
  28.6 20.9 %collective-permute-start.5 = (bf16[304,768]{1,0:T(8,128)(2,1)S(1)}, bf16[304,768]{1,0:T(8,128)(2,1)S(1)}, u32[]{:S(2)}, u32[]{:S(2)}) collective-permute-start(bf16[304,768]{1,0:T(8,128)(2,1)S(1)} %arrange_qkv.1.refs_0_.refs_9_), channel_id=1, source_target_pairs={{0,2},{1,3},{2,0},{3,1},{4,6},{5,7},{6,4},{7,5},{8,10},{9,11},{10,... | collective-permute-start | bytes 1400840 | tf_op jit(solution)/shard_map/ppermute | solution.py:915
  30.1 21.3 %collective-permute-start.6 = (bf16[304,768]{1,0:T(8,128)(2,1)S(1)}, bf16[304,768]{1,0:T(8,128)(2,1)S(1)}, u32[]{:S(2)}, u32[]{:S(2)}) collective-permute-start(bf16[304,768]{1,0:T(8,128)(2,1)S(1)} %arrange_qkv.1.refs_0_.refs_9_), channel_id=1, source_target_pairs={{0,4},{1,5},{2,6},{3,7},{4,0},{5,1},{6,2},{7,3},{8,12},{9,13},{10,... | collective-permute-start | bytes 1400840 | tf_op jit(solution)/shard_map/ppermute | solution.py:915
  31.7 19.8 %collective-permute-start.7 = (bf16[304,768]{1,0:T(8,128)(2,1)S(1)}, bf16[304,768]{1,0:T(8,128)(2,1)}, u32[]{:S(2)}, u32[]{:S(2)}) collective-permute-start(bf16[304,768]{1,0:T(8,128)(2,1)S(1)} %arrange_qkv.1.refs_0_.refs_9_), channel_id=1, source_target_pairs={{0,6},{1,7},{2,4},{3,5},{4,2},{5,3},{6,0},{7,1},{8,14},{9,15},{10,... | collective-permute-start | bytes 1400840 | tf_op jit(solution)/shard_map/ppermute | solution.py:915
  32.2 17.2 %collective-permute-start.4 = (bf16[384,512]{1,0:T(8,128)(2,1)S(1)}, bf16[384,512]{1,0:T(8,128)(2,1)S(1)}, u32[]{:S(2)}, u32[]{:S(2)}) collective-permute-start(bf16[384,512]{1,0:T(8,128)(2,1)S(1)} %pad_maximum_fusion.4), channel_id=1, source_target_pairs={{0,16},{8,24},{16,0},{24,8},{1,17},{9,25},{17,1},{25,9},{2,18},{10... | collective-permute-start | bytes 1179656 | tf_op jit(solution)/shard_map/ppermute | solution.py:915
  54.2 17.0 %collective-permute-start.8 = (bf16[240,768]{1,0:T(8,128)(2,1)S(1)}, bf16[240,768]{1,0:T(8,128)(2,1)S(1)}, u32[]{:S(2)}, u32[]{:S(2)}) collective-permute-start(bf16[240,768]{1,0:T(8,128)(2,1)S(1)} %get-tuple-element.168), channel_id=1, source_target_pairs={{0,2},{1,3},{2,0},{3,1},{4,6},{5,7},{6,4},{7,5},{8,10},{9,11},{10,... | collective-permute-start | bytes 1105928 | tf_op jit(solution)/shard_map/ppermute | solution.py:915
  74.0 18.9 %collective-permute-start.15 = (bf16[192,768]{1,0:T(8,128)(2,1)S(1)}, bf16[192,768]{1,0:T(8,128)(2,1)}, u32[]{:S(2)}, u32[]{:S(2)}) collective-permute-start(bf16[192,768]{1,0:T(8,128)(2,1)S(1)} %get-tuple-element.183), channel_id=1, source_target_pairs={{0,2},{1,3},{2,0},{3,1},{4,6},{5,7},{6,4},{7,5},{8,10},{9,11},{10,... | collective-permute-start | bytes 884744 | tf_op jit(solution)/shard_map/ppermute | solution.py:915
  75.5 17.4 %collective-permute-start.16 = (bf16[192,768]{1,0:T(8,128)(2,1)}, bf16[192,768]{1,0:T(8,128)(2,1)}, u32[]{:S(2)}, u32[]{:S(2)}) collective-permute-start(bf16[192,768]{1,0:T(8,128)(2,1)} %get-tuple-element.187), channel_id=1, source_target_pairs={{0,4},{1,5},{2,6},{3,7},{4,0},{5,1},{6,2},{7,3},{8,12},{9,13},{10,... | collective-permute-start | bytes 884744 | tf_op jit(solution)/shard_map/ppermute | solution.py:915
  76.0 37.6 %collective-permute-start.17 = (bf16[480,768]{1,0:T(8,128)(2,1)}, bf16[480,768]{1,0:T(8,128)(2,1)}, u32[]{:S(2)}, u32[]{:S(2)}) collective-permute-start(bf16[480,768]{1,0:T(8,128)(2,1)} %pad_maximum_fusion.refs_0_), channel_id=1, source_target_pairs={{0,4},{1,5},{2,6},{3,7},{4,0},{5,1},{6,2},{7,3},{8,12},{9,13},{10,... | collective-permute-start | bytes 2211848 | tf_op jit(solution)/shard_map/ppermute | solution.py:915
  77.5 36.1 %collective-permute-start.18 = (bf16[480,768]{1,0:T(8,128)(2,1)}, bf16[480,768]{1,0:T(8,128)(2,1)}, u32[]{:S(2)}, u32[]{:S(2)}) collective-permute-start(bf16[480,768]{1,0:T(8,128)(2,1)} %pad_maximum_fusion.1.refs_4_), channel_id=1, source_target_pairs={{0,2},{1,3},{2,0},{3,1},{4,6},{5,7},{6,4},{7,5},{8,10},{9,11},{10,... | collective-permute-start | bytes 2211848 | tf_op jit(solution)/shard_map/ppermute | solution.py:915
  96.6 17.0 %collective-permute-start.19 = (bf16[384,768]{1,0:T(8,128)(2,1)}, bf16[384,768]{1,0:T(8,128)(2,1)}, u32[]{:S(2)}, u32[]{:S(2)}) collective-permute-start(bf16[384,768]{1,0:T(8,128)(2,1)} %pad_maximum_fusion.2.refs_8_), channel_id=1, source_target_pairs={{0,4},{1,5},{2,6},{3,7},{4,0},{5,1},{6,2},{7,3},{8,12},{9,13},{10,... | collective-permute-start | bytes 1769480 | tf_op jit(solution)/shard_map/ppermute | solution.py:915
  192.0 35.2 %collective-permute-start.30 = (bf16[4,480,768]{2,1,0:T(8,128)(2,1)}, bf16[4,480,768]{2,1,0:T(8,128)(2,1)S(1)}, u32[]{:S(2)}, u32[]{:S(2)}) collective-permute-start(bf16[4,480,768]{2,1,0:T(8,128)(2,1)} %get-tuple-element.228), channel_id=1, source_target_pairs={{0,1},{1,0},{2,3},{3,2},{4,5},{5,4},{6,7},{7,6},{8,9},{9,8},{10,11... | collective-permute-start | bytes 8847368 | tf_op jit(solution)/shard_map/ppermute | solution.py:915
  194.5 38.1 %collective-permute-start.31 = (bf16[2,4,96,768]{3,2,1,0:T(8,128)(2,1)S(1)}, bf16[2,4,96,768]{3,2,1,0:T(8,128)(2,1)}, u32[]{:S(2)}, u32[]{:S(2)}) collective-permute-start(bf16[2,4,96,768]{3,2,1,0:T(8,128)(2,1)S(1)} %add_convert_fusion), channel_id=1, source_target_pairs={{0,8},{8,0},{16,24},{24,16},{1,9},{9,1},{17,25},{25,17},{2,10},{10... | collective-permute-start | bytes 3538952 | tf_op jit(solution)/shard_map/ppermute | solution.py:915
  229.1 33.6 %collective-permute-start.33 = (bf16[480,768]{1,0:T(8,128)(2,1)}, bf16[480,768]{1,0:T(8,128)(2,1)S(1)}, u32[]{:S(2)}, u32[]{:S(2)}) collective-permute-start(bf16[480,768]{1,0:T(8,128)(2,1)} %get-tuple-element.240), channel_id=1, source_target_pairs={{0,2},{1,3},{2,0},{3,1},{4,6},{5,7},{6,4},{7,5},{8,10},{9,11},{10,... | collective-permute-start | bytes 2211848 | tf_op jit(solution)/shard_map/ppermute | solution.py:915
  230.4 32.6 %collective-permute-start.34 = (bf16[480,768]{1,0:T(8,128)(2,1)}, bf16[480,768]{1,0:T(8,128)(2,1)S(1)}, u32[]{:S(2)}, u32[]{:S(2)}) collective-permute-start(bf16[480,768]{1,0:T(8,128)(2,1)} %get-tuple-element.241), channel_id=1, source_target_pairs={{0,4},{1,5},{2,6},{3,7},{4,0},{5,1},{6,2},{7,3},{8,12},{9,13},{10,... | collective-permute-start | bytes 2211848 | tf_op jit(solution)/shard_map/ppermute | solution.py:915
  231.3 33.1 %collective-permute-start.35 = (bf16[480,768]{1,0:T(8,128)(2,1)S(1)}, bf16[480,768]{1,0:T(8,128)(2,1)S(1)}, u32[]{:S(2)}, u32[]{:S(2)}) collective-permute-start(bf16[480,768]{1,0:T(8,128)(2,1)S(1)} %get-tuple-element.242), channel_id=1, source_target_pairs={{0,6},{1,7},{2,4},{3,5},{4,2},{5,3},{6,0},{7,1},{8,14},{9,15},{10,... | collective-permute-start | bytes 2211848 | tf_op jit(solution)/shard_map/ppermute | solution.py:915
  234.6 29.8 %collective-permute-start.32 = (bf16[4,96,768]{2,1,0:T(8,128)(2,1)S(1)}, bf16[4,96,768]{2,1,0:T(8,128)(2,1)S(1)}, u32[]{:S(2)}, u32[]{:S(2)}) collective-permute-start(bf16[4,96,768]{2,1,0:T(8,128)(2,1)S(1)} %get-tuple-element.239), channel_id=1, source_target_pairs={{0,16},{8,24},{16,0},{24,8},{1,17},{9,25},{17,1},{25,9},{2,18},{10... | collective-permute-start | bytes 1769480 | tf_op jit(solution)/shard_map/ppermute | solution.py:915
  281.6 19.8 %collective-permute-start.41 = (bf16[192,480]{1,0:T(8,128)(2,1)S(1)}, bf16[192,480]{1,0:T(8,128)(2,1)S(1)}, u32[]{:S(2)}, u32[]{:S(2)}) collective-permute-start(bf16[192,480]{1,0:T(8,128)(2,1)S(1)} %fusion.9), channel_id=1, source_target_pairs={{0,16},{8,24},{16,0},{24,8},{1,17},{9,25},{17,1},{25,9},{2,18},{10... | collective-permute-start | bytes 552968 | tf_op jit(solution)/shard_map/ppermute | solution.py:915
  284.1 26.9 %collective-permute-start.45 = (bf16[288,768]{1,0:T(8,128)(2,1)S(1)}, bf16[288,768]{1,0:T(8,128)(2,1)S(1)}, u32[]{:S(2)}, u32[]{:S(2)}) collective-permute-start(bf16[288,768]{1,0:T(8,128)(2,1)S(1)} %get-tuple-element.287), channel_id=1, source_target_pairs={{0,2},{1,3},{2,0},{3,1},{4,6},{5,7},{6,4},{7,5},{8,10},{9,11},{10,... | collective-permute-start | bytes 1327112 | tf_op jit(solution)/shard_map/ppermute | solution.py:915
  284.7 26.3 %collective-permute-start.46 = (bf16[288,768]{1,0:T(8,128)(2,1)S(1)}, bf16[288,768]{1,0:T(8,128)(2,1)S(1)}, u32[]{:S(2)}, u32[]{:S(2)}) collective-permute-start(bf16[288,768]{1,0:T(8,128)(2,1)S(1)} %get-tuple-element.288), channel_id=1, source_target_pairs={{0,4},{1,5},{2,6},{3,7},{4,0},{5,1},{6,2},{7,3},{8,12},{9,13},{10,... | collective-permute-start | bytes 1327112 | tf_op jit(solution)/shard_map/ppermute | solution.py:915
  286.3 24.7 %collective-permute-start.47 = (bf16[288,768]{1,0:T(8,128)(2,1)S(1)}, bf16[288,768]{1,0:T(8,128)(2,1)S(1)}, u32[]{:S(2)}, u32[]{:S(2)}) collective-permute-start(bf16[288,768]{1,0:T(8,128)(2,1)S(1)} %get-tuple-element.289), channel_id=1, source_target_pairs={{0,6},{1,7},{2,4},{3,5},{4,2},{5,3},{6,0},{7,1},{8,14},{9,15},{10,... | collective-permute-start | bytes 1327112 | tf_op jit(solution)/shard_map/ppermute | solution.py:915
  312.5 17.4 %collective-permute-start.50 = (bf16[192,288]{1,0:T(8,128)(2,1)S(1)}, bf16[192,288]{1,0:T(8,128)(2,1)S(1)}, u32[]{:S(2)}, u32[]{:S(2)}) collective-permute-start(bf16[192,288]{1,0:T(8,128)(2,1)S(1)} %get-tuple-element.296), channel_id=1, source_target_pairs={{0,8},{8,0},{16,24},{24,16},{1,9},{9,1},{17,25},{25,17},{2,10},{10... | collective-permute-start | bytes 331784 | tf_op jit(solution)/shard_map/ppermute | solution.py:915
  314.1 15.8 %collective-permute-start.51 = (bf16[192,288]{1,0:T(8,128)(2,1)S(1)}, bf16[192,288]{1,0:T(8,128)(2,1)S(1)}, u32[]{:S(2)}, u32[]{:S(2)}) collective-permute-start(bf16[192,288]{1,0:T(8,128)(2,1)S(1)} %get-tuple-element.297), channel_id=1, source_target_pairs={{0,16},{8,24},{16,0},{24,8},{1,17},{9,25},{17,1},{25,9},{2,18},{10... | collective-permute-start | bytes 331784 | tf_op jit(solution)/shard_map/ppermute | solution.py:915
  (54 other events, 537.9 us)

commit v5 on v4

--- a/solution.py
+++ b/solution.py
@@ -451,7 +451,7 @@
             scratch_shapes=[pltpu.VMEM((2, padded, PAIR), BF)] * 2,
         ),
         out_shape=[jax.ShapeDtypeStruct((slots, count * PAIR), BF)] * 3,
-        compiler_params=params(40),
+        compiler_params=params(32),
         cost_estimate=cost(
             2 * count * 20 * slots * slots * PAIR, slots * width * 16, 2 * count * slots * slots
         ),
@@ -863,7 +863,7 @@
             jax.ShapeDtypeStruct((slots, width), F32),
             jax.ShapeDtypeStruct(vec.shape, F32),
         ],
-        compiler_params=params(40),
+        compiler_params=params(24),
         cost_estimate=cost(6 * slots * width * width, slots * width * 16),
         name="last",
     )(table, x, d_resid, vec, sums, *d_parts, *blocks)

time: 336 us -> 334 us (level)
  no operation moved by 1% of the time
where the time goes in v5:
time: 334 us; the launch traced here: 330 us
  Pallas kernels  190 us (57%)
  waiting for transfers between devices  65.8 us (20%)
  starting transfers between devices  46.6 us (14%)
  local copies, waits for them, and re-layouts  12.7 us (4%)
  other arithmetic  12.6 us (4%)
    ppermute x53, waiting for transfers between devices, swap(): return lax.ppermute(values, axis, [(i, i ^ mask) for i in range(size)])  65.8 us
    pallas_call x3, Pallas kernels, attend_back(): pl.pallas_call(functools.partial(attend_back_kernel, slots=slots, padded=...  53.3 us
    ppermute x53, starting transfers between devices, swap(): return lax.ppermute(values, axis, [(i, i ^ mask) for i in range(size)])  46.6 us
    pallas_call x1, Pallas kernels, middle(): pl.pallas_call(functools.partial(middle_kernel, chunk=chunk), grid_spec=p...  43.1 us
    pallas_call x2, Pallas kernels, attend(): pl.pallas_call(functools.partial(attend_kernel, slots=slots, padded=padde...  29.7 us
    pallas_call x1, Pallas kernels, up_grads(): pl.pallas_call(up_grads_kernel, grid_spec=pltpu.PrefetchScalarGridSpec(nu...  14.3 us
    pallas_call x1, Pallas kernels, last(): pl.pallas_call(functools.partial(last_kernel, groups=len(d_parts) // 3),...  12.5 us
    pallas_call x1, Pallas kernels, down_grads(): pl.pallas_call(down_grads_kernel, grid_spec=pltpu.PrefetchScalarGridSpec(...  11.6 us
  transfers between devices with their start and end apart: 53, of which 16 were waited for; matrix products, arithmetic and copies ran while one was open for 4% of the time, Pallas kernels for 40%

profile of v5, /device:TPU:0, one launch (start us, length us, event | category | flops | bytes accessed | tf_op | source)
XLA Modules:
  0.0 330.3 jit_solution(12063242316176529000)
XLA Ops:
  2.6 3.0 collective-permute-start.3
  5.7 3.0 collective-permute-start.1
  11.1 9.5 %collective-permute-done.refs_1_ = bf16[200,288]{1,0:T(8,128)(2,1)S(1)} collective-permute-done((bf16[200,288]{1,0:T(8,128)(2,1)}, bf16[200,288]{1,0:T(8,128)(2,1)S(1)}, u32[]{:S(2)}, u32[]{:S(2)}) %collective-permute-start) | collective-permute-done | bytes 115232 | tf_op jit(solution)/shard_map/ppermute | solution.py:915
  21.0 5.0 %collective-permute-done.2.refs_3_ = bf16[200,288]{1,0:T(8,128)(2,1)S(1)} collective-permute-done((bf16[200,288]{1,0:T(8,128)(2,1)}, bf16[200,288]{1,0:T(8,128)(2,1)S(1)}, u32[]{:S(2)}, u32[]{:S(2)}) %collective-permute-start.2) | collective-permute-done | bytes 115232 | tf_op jit(solution)/shard_map/ppermute | solution.py:915
  32.3 17.2 %collective-permute-done.4.far_ref = bf16[384,512]{1,0:T(8,128)(2,1)S(1)} collective-permute-done((bf16[384,512]{1,0:T(8,128)(2,1)S(1)}, bf16[384,512]{1,0:T(8,128)(2,1)S(1)}, u32[]{:S(2)}, u32[]{:S(2)}) %collective-permute-start.4) | collective-permute-done | bytes 393248 | tf_op jit(solution)/shard_map/ppermute | solution.py:915
  57.9 10.9 %project.1 = (bf16[1224,2304]{1,0:T(8,128)(2,1)S(1)}, bf16[1224,768]{1,0:T(8,128)(2,1)S(1)}, f32[16,768]{1,0:T(8,128)S(1)}) custom-call(s32[32]{0:T(128)S(1)} %concatenate.23.table, bf16[1224,768]{1,0:T(8,128)(2,1)S(1)} %copy-done.4, bf16[304,768]{1,0:T(8,128)(2,1)S(1)} %arrange_qkv.1.refs_0_.refs_9_, ...), custom_call_target="tpu_custom_call" | custom-call | flops 4331667456 | bytes 9400320 | tf_op jit(solution)/shard_map/project/pallas_call | solution.py:265
  68.8 2.4 copy-done.11
  78.0 14.8 %attend.2 = (bf16[1224,768]{1,0:T(8,128)(2,1)}, f32[6,8,1280]{2,1,0:T(8,128)}) custom-call(s32[1]{0:T(128)S(6)} %copy.37.len_ref, bf16[1224,2304]{1,0:T(8,128)(2,1)} %copy-done.11, bf16[1224,2304]{1,0:T(8,128)(2,1)} %copy-done.11, bf16[1224,2304]{1,0:T(8,128)(2,1)} %copy-done.11), custom_call_target="tpu_custom_call" | custom-call | flops 9204793344 | bytes 7520256 | tf_op jit(solution)/shard_map/attend/pallas_call | solution.py:332
  98.5 14.9 %attend.3 = (bf16[1224,768]{1,0:T(8,128)(2,1)}, f32[6,8,1280]{2,1,0:T(8,128)}) custom-call(s32[1]{0:T(128)S(6)} %copy.37.len_ref, bf16[1224,2304]{1,0:T(8,128)(2,1)} %copy-done.11, bf16[1224,2304]{1,0:T(8,128)(2,1)} %copy-done.11, bf16[1224,2304]{1,0:T(8,128)(2,1)} %copy-done.11, ...), custom_call_target="tpu_custom_call", output_to_operand_aliasing={{0}: (4, {}), {1}: (5, {})} | custom-call | flops 9204793344 | bytes 7520256 | tf_op jit(solution)/shard_map/attend/pallas_call | solution.py:332
  117.7 4.9 %collective-permute-done.28.refs_15_ = bf16[384,768]{1,0:T(8,128)(2,1)} collective-permute-done((bf16[384,768]{1,0:T(8,128)(2,1)}, bf16[384,768]{1,0:T(8,128)(2,1)}, u32[]{:S(2)}, u32[]{:S(2)}) %collective-permute-start.28) | collective-permute-done | bytes 589856 | tf_op jit(solution)/shard_map/ppermute | solution.py:915
  122.6 43.1 %middle.1 = (bf16[1224,768]{1,0:T(8,128)(2,1)}, bf16[1224,3072]{1,0:T(8,128)(2,1)}, bf16[1224,3072]{1,0:T(8,128)(2,1)}, bf16[1224,768]{1,0:T(8,128)(2,1)}, f32[1...) custom-call(s32[1]{0:T(128)S(6)} %copy.37.len_ref, s32[32]{0:T(128)} %copy-done.2, ...), custom_call_target="tpu_custom_call" | custom-call | flops 25990004736 | bytes 41398272 | tf_op jit(solution)/shard_map/middle/pallas_call | solution.py:584
  165.8 11.6 %down_grads.1 = (bf16[4,4,96,768]{3,2,1,0:T(8,128)(2,1)}, bf16[4,4,96,768]{3,2,1,0:T(8,128)(2,1)}) custom-call(s32[1]{0:T(128)S(6)} %copy.37.len_ref, s32[32]{0:T(128)} %copy-done.2, bf16[1224,3072]{1,0:T(8,128)(2,1)} %get-tuple-element.211.active_ref, bf16[1224,768]{1,0:T(8,128)(2,1)} %cot_ref.3), custom_call_target="tpu_custom_call" | custom-call | flops 5775556608 | bytes 12238848 | tf_op jit(solution)/shard_map/down_grads/pallas_call | solution.py:673
  177.6 14.3 %up_grads.1 = (bf16[4,480,768]{2,1,0:T(8,128)(2,1)}, bf16[4,480,768]{2,1,0:T(8,128)(2,1)}) custom-call(s32[32]{0:T(128)} %copy-done.2, bf16[1224,3072]{1,0:T(8,128)(2,1)} %get-tuple-element.217.d_inner_ref, bf16[1224,768]{1,0:T(8,128)(2,1)} %get-tuple-element.218.normed_ref, bf16[1224,768]{1,0:T(8,128)(2,1)} %get-tuple-element.219.d_branch_ref, ...), custom_call_target="tpu_custom_call" | custom-call | flops 7219445760 | bytes 13418496 | tf_op jit(solution)/shard_map/up_grads/pallas_call | solution.py:741
  196.4 2.6 copy-done.12
  200.5 18.0 %attend_back.3 = (bf16[1224,256]{1,0:T(8,128)(2,1)S(1)}, bf16[1224,256]{1,0:T(8,128)(2,1)S(1)}, bf16[1224,256]{1,0:T(8,128)(2,1)S(1)}) custom-call(s32[1]{0:T(128)S(6)} %copy.37.len_ref, bf16[1224,2304]{1,0:T(8,128)(2,1)S(1)} %copy-done.12, bf16[1224,2304]{1,0:T(8,128)(2,1)S(1)} %copy-done.12, bf16[1224,2304]{1,0:T(8,128)(2,1)S(1)} %copy-done.12, ...), custom_call_target="tpu_custom_call" | custom-call | flops 15341322240 | bytes 15040512 | tf_op jit(solution)/shard_map/attend_back/pallas_call | solution.py:437
  218.5 8.6 %attend_back.4 = (bf16[1224,128]{1,0:T(8,128)(2,1)S(1)}, bf16[1224,128]{1,0:T(8,128)(2,1)S(1)}, bf16[1224,128]{1,0:T(8,128)(2,1)S(1)}) custom-call(s32[1]{0:T(128)S(6)} %copy.37.len_ref, bf16[1224,2304]{1,0:T(8,128)(2,1)S(1)} %copy-done.12, bf16[1224,2304]{1,0:T(8,128)(2,1)S(1)} %copy-done.12, bf16[1224,2304]{1,0:T(8,128)(2,1)S(1)} %copy-done.12, ...), custom_call_target="tpu_custom_call" | custom-call | flops 7670661120 | bytes 15040512 | tf_op jit(solution)/shard_map/attend_back/pallas_call | solution.py:437
  234.3 26.8 %attend_back.5 = (bf16[1224,384]{1,0:T(8,128)(2,1)S(1)}, bf16[1224,384]{1,0:T(8,128)(2,1)S(1)}, bf16[1224,384]{1,0:T(8,128)(2,1)S(1)}) custom-call(s32[1]{0:T(128)S(6)} %copy.37.len_ref, bf16[1224,2304]{1,0:T(8,128)(2,1)S(1)} %copy-done.12, bf16[1224,2304]{1,0:T(8,128)(2,1)S(1)} %copy-done.12, bf16[1224,2304]{1,0:T(8,128)(2,1)S(1)} %copy-done.12, ...), custom_call_target="tpu_custom_call" | custom-call | flops 23011983360 | bytes 15040512 | tf_op jit(solution)/shard_map/attend_back/pallas_call | solution.py:437
  268.4 7.4 %qkv_grads.1 = (bf16[4,288,768]{2,1,0:T(8,128)(2,1)S(1)}, bf16[4,288,768]{2,1,0:T(8,128)(2,1)S(1)}) custom-call(s32[32]{0:T(128)S(1)} %copy-done.3, bf16[1224,256]{1,0:T(8,128)(2,1)S(1)} %get-tuple-element.252.refs_0_, bf16[1224,256]{1,0:T(8,128)(2,1)S(1)} %get-tuple-element.253.refs_1_, bf16[1224,256]{1,0:T(8,128)(2,1)S(1)} %get-tuple-element.254.refs_2_, ...), custom_call_target="tpu_custom_call" | custom-call | flops 4331667456 | bytes 11059200 | tf_op jit(solution)/shard_map/qkv_grads/pallas_call | solution.py:789
  276.8 2.8 collective-permute-done.40
  280.1 2.6 collective-permute-start.41
  286.2 12.5 %last.1 = (f32[1224,768]{1,0:T(8,128)}, f32[16,768]{1,0:T(8,128)S(1)}) custom-call(s32[32]{0:T(128)S(1)} %copy-done.3, bf16[1224,768]{1,0:T(8,128)(2,1)S(1)} %copy-done.5, f32[1224,768]{1,0:T(8,128)S(1)} %copy-done.10, f32[16,768]{1,0:T(8,128)S(1)} %copy-done.14, f32[16,768]{1,0:T(8,128)S(1)} %copy-done.15, ...), custom_call_target="tpu_custom_call" | custom-call | flops 4331667456 | bytes 15040512 | tf_op jit(solution)/shard_map/last/pallas_call | solution.py:847
  300.9 4.3 %collective-permute-done.43 = f32[16,768]{1,0:T(8,128)S(1)} collective-permute-done((f32[16,768]{1,0:T(8,128)S(1)}, f32[16,768]{1,0:T(8,128)S(1)}, u32[]{:S(2)}, u32[]{:S(2)}) %collective-permute-start.43) | collective-permute-done | bytes 49184 | tf_op jit(solution)/shard_map/ppermute | solution.py:915
  306.0 3.3 %collective-permute-done.44 = f32[16,768]{1,0:T(8,128)S(1)} collective-permute-done((f32[16,768]{1,0:T(8,128)S(1)}, f32[16,768]{1,0:T(8,128)S(1)}, u32[]{:S(2)}, u32[]{:S(2)}) %collective-permute-start.44) | collective-permute-done | bytes 49184 | tf_op jit(solution)/shard_map/ppermute | solution.py:915
  317.4 10.6 %collective-permute-done.49 = f32[16,768]{1,0:T(8,128)S(1)} collective-permute-done((f32[16,768]{1,0:T(8,128)S(1)}, f32[16,768]{1,0:T(8,128)S(1)}, u32[]{:S(2)}, u32[]{:S(2)}) %collective-permute-start.49) | collective-permute-done | bytes 49184 | tf_op jit(solution)/shard_map/ppermute | solution.py:915
  (183 shorter events, 74.1 us)
Async XLA Ops:
  2.6 25.9 %collective-permute-start.3 = (bf16[192,896]{1,0:T(8,128)(2,1)}, bf16[192,896]{1,0:T(8,128)(2,1)S(1)}, u32[]{:S(2)}, u32[]{:S(2)}) collective-permute-start(bf16[192,896]{1,0:T(8,128)(2,1)} %get-tuple-element.160.own_ref), channel_id=1, source_target_pairs={{0,8},{8,0},{16,24},{24,16},{1,9},{9,1},{17,25},{25,17},{2,10},{10... | collective-permute-start | bytes 1032200 | tf_op jit(solution)/shard_map/ppermute | solution.py:915
  8.7 17.3 %collective-permute-start.2 = (bf16[200,288]{1,0:T(8,128)(2,1)}, bf16[200,288]{1,0:T(8,128)(2,1)S(1)}, u32[]{:S(2)}, u32[]{:S(2)}) collective-permute-start(bf16[200,288]{1,0:T(8,128)(2,1)} %get-tuple-element.161.refs_0_), channel_id=1, source_target_pairs={{0,24},{8,16},{16,8},{24,0},{1,25},{9,17},{17,9},{25,1},{2,26},{10... | collective-permute-start | bytes 345608 | tf_op jit(solution)/shard_map/ppermute | solution.py:915
  28.6 20.9 %collective-permute-start.5 = (bf16[304,768]{1,0:T(8,128)(2,1)S(1)}, bf16[304,768]{1,0:T(8,128)(2,1)S(1)}, u32[]{:S(2)}, u32[]{:S(2)}) collective-permute-start(bf16[304,768]{1,0:T(8,128)(2,1)S(1)} %arrange_qkv.1.refs_0_.refs_9_), channel_id=1, source_target_pairs={{0,2},{1,3},{2,0},{3,1},{4,6},{5,7},{6,4},{7,5},{8,10},{9,11},{10,... | collective-permute-start | bytes 1400840 | tf_op jit(solution)/shard_map/ppermute | solution.py:915
  30.1 21.3 %collective-permute-start.6 = (bf16[304,768]{1,0:T(8,128)(2,1)S(1)}, bf16[304,768]{1,0:T(8,128)(2,1)S(1)}, u32[]{:S(2)}, u32[]{:S(2)}) collective-permute-start(bf16[304,768]{1,0:T(8,128)(2,1)S(1)} %arrange_qkv.1.refs_0_.refs_9_), channel_id=1, source_target_pairs={{0,4},{1,5},{2,6},{3,7},{4,0},{5,1},{6,2},{7,3},{8,12},{9,13},{10,... | collective-permute-start | bytes 1400840 | tf_op jit(solution)/shard_map/ppermute | solution.py:915
  31.7 19.8 %collective-permute-start.7 = (bf16[304,768]{1,0:T(8,128)(2,1)S(1)}, bf16[304,768]{1,0:T(8,128)(2,1)}, u32[]{:S(2)}, u32[]{:S(2)}) collective-permute-start(bf16[304,768]{1,0:T(8,128)(2,1)S(1)} %arrange_qkv.1.refs_0_.refs_9_), channel_id=1, source_target_pairs={{0,6},{1,7},{2,4},{3,5},{4,2},{5,3},{6,0},{7,1},{8,14},{9,15},{10,... | collective-permute-start | bytes 1400840 | tf_op jit(solution)/shard_map/ppermute | solution.py:915
  32.2 17.2 %collective-permute-start.4 = (bf16[384,512]{1,0:T(8,128)(2,1)S(1)}, bf16[384,512]{1,0:T(8,128)(2,1)S(1)}, u32[]{:S(2)}, u32[]{:S(2)}) collective-permute-start(bf16[384,512]{1,0:T(8,128)(2,1)S(1)} %pad_maximum_fusion.4), channel_id=1, source_target_pairs={{0,16},{8,24},{16,0},{24,8},{1,17},{9,25},{17,1},{25,9},{2,18},{10... | collective-permute-start | bytes 1179656 | tf_op jit(solution)/shard_map/ppermute | solution.py:915
  54.2 17.0 %collective-permute-start.8 = (bf16[240,768]{1,0:T(8,128)(2,1)S(1)}, bf16[240,768]{1,0:T(8,128)(2,1)S(1)}, u32[]{:S(2)}, u32[]{:S(2)}) collective-permute-start(bf16[240,768]{1,0:T(8,128)(2,1)S(1)} %get-tuple-element.168), channel_id=1, source_target_pairs={{0,2},{1,3},{2,0},{3,1},{4,6},{5,7},{6,4},{7,5},{8,10},{9,11},{10,... | collective-permute-start | bytes 1105928 | tf_op jit(solution)/shard_map/ppermute | solution.py:915
  55.7 15.6 %collective-permute-start.9 = (bf16[240,768]{1,0:T(8,128)(2,1)S(1)}, bf16[240,768]{1,0:T(8,128)(2,1)S(1)}, u32[]{:S(2)}, u32[]{:S(2)}) collective-permute-start(bf16[240,768]{1,0:T(8,128)(2,1)S(1)} %get-tuple-element.169), channel_id=1, source_target_pairs={{0,4},{1,5},{2,6},{3,7},{4,0},{5,1},{6,2},{7,3},{8,12},{9,13},{10,... | collective-permute-start | bytes 1105928 | tf_op jit(solution)/shard_map/ppermute | solution.py:915
  74.0 18.8 %collective-permute-start.15 = (bf16[192,768]{1,0:T(8,128)(2,1)S(1)}, bf16[192,768]{1,0:T(8,128)(2,1)}, u32[]{:S(2)}, u32[]{:S(2)}) collective-permute-start(bf16[192,768]{1,0:T(8,128)(2,1)S(1)} %get-tuple-element.183), channel_id=1, source_target_pairs={{0,2},{1,3},{2,0},{3,1},{4,6},{5,7},{6,4},{7,5},{8,10},{9,11},{10,... | collective-permute-start | bytes 884744 | tf_op jit(solution)/shard_map/ppermute | solution.py:915
  75.5 17.4 %collective-permute-start.16 = (bf16[192,768]{1,0:T(8,128)(2,1)}, bf16[192,768]{1,0:T(8,128)(2,1)}, u32[]{:S(2)}, u32[]{:S(2)}) collective-permute-start(bf16[192,768]{1,0:T(8,128)(2,1)} %get-tuple-element.187), channel_id=1, source_target_pairs={{0,4},{1,5},{2,6},{3,7},{4,0},{5,1},{6,2},{7,3},{8,12},{9,13},{10,... | collective-permute-start | bytes 884744 | tf_op jit(solution)/shard_map/ppermute | solution.py:915
  76.0 37.4 %collective-permute-start.17 = (bf16[480,768]{1,0:T(8,128)(2,1)}, bf16[480,768]{1,0:T(8,128)(2,1)}, u32[]{:S(2)}, u32[]{:S(2)}) collective-permute-start(bf16[480,768]{1,0:T(8,128)(2,1)} %pad_maximum_fusion.refs_0_), channel_id=1, source_target_pairs={{0,4},{1,5},{2,6},{3,7},{4,0},{5,1},{6,2},{7,3},{8,12},{9,13},{10,... | collective-permute-start | bytes 2211848 | tf_op jit(solution)/shard_map/ppermute | solution.py:915
  77.5 35.9 %collective-permute-start.18 = (bf16[480,768]{1,0:T(8,128)(2,1)}, bf16[480,768]{1,0:T(8,128)(2,1)}, u32[]{:S(2)}, u32[]{:S(2)}) collective-permute-start(bf16[480,768]{1,0:T(8,128)(2,1)} %pad_maximum_fusion.1.refs_4_), channel_id=1, source_target_pairs={{0,2},{1,3},{2,0},{3,1},{4,6},{5,7},{6,4},{7,5},{8,10},{9,11},{10,... | collective-permute-start | bytes 2211848 | tf_op jit(solution)/shard_map/ppermute | solution.py:915
  96.5 16.9 %collective-permute-start.19 = (bf16[384,768]{1,0:T(8,128)(2,1)}, bf16[384,768]{1,0:T(8,128)(2,1)}, u32[]{:S(2)}, u32[]{:S(2)}) collective-permute-start(bf16[384,768]{1,0:T(8,128)(2,1)} %pad_maximum_fusion.2.refs_8_), channel_id=1, source_target_pairs={{0,4},{1,5},{2,6},{3,7},{4,0},{5,1},{6,2},{7,3},{8,12},{9,13},{10,... | collective-permute-start | bytes 1769480 | tf_op jit(solution)/shard_map/ppermute | solution.py:915
  191.9 35.2 %collective-permute-start.30 = (bf16[4,480,768]{2,1,0:T(8,128)(2,1)}, bf16[4,480,768]{2,1,0:T(8,128)(2,1)S(1)}, u32[]{:S(2)}, u32[]{:S(2)}) collective-permute-start(bf16[4,480,768]{2,1,0:T(8,128)(2,1)} %get-tuple-element.228), channel_id=1, source_target_pairs={{0,1},{1,0},{2,3},{3,2},{4,5},{5,4},{6,7},{7,6},{8,9},{9,8},{10,11... | collective-permute-start | bytes 8847368 | tf_op jit(solution)/shard_map/ppermute | solution.py:915
  194.4 37.0 %collective-permute-start.31 = (bf16[2,4,96,768]{3,2,1,0:T(8,128)(2,1)S(1)}, bf16[2,4,96,768]{3,2,1,0:T(8,128)(2,1)S(1)}, u32[]{:S(2)}, u32[]{:S(2)}) collective-permute-start(bf16[2,4,96,768]{3,2,1,0:T(8,128)(2,1)S(1)} %add_convert_fusion), channel_id=1, source_target_pairs={{0,8},{8,0},{16,24},{24,16},{1,9},{9,1},{17,25},{25,17},{2,10},{10... | collective-permute-start | bytes 3538952 | tf_op jit(solution)/shard_map/ppermute | solution.py:915
  227.9 33.2 %collective-permute-start.33 = (bf16[480,768]{1,0:T(8,128)(2,1)S(1)}, bf16[480,768]{1,0:T(8,128)(2,1)S(1)}, u32[]{:S(2)}, u32[]{:S(2)}) collective-permute-start(bf16[480,768]{1,0:T(8,128)(2,1)S(1)} %get-tuple-element.240), channel_id=1, source_target_pairs={{0,2},{1,3},{2,0},{3,1},{4,6},{5,7},{6,4},{7,5},{8,10},{9,11},{10,... | collective-permute-start | bytes 2211848 | tf_op jit(solution)/shard_map/ppermute | solution.py:915
  229.2 32.2 %collective-permute-start.34 = (bf16[480,768]{1,0:T(8,128)(2,1)S(1)}, bf16[480,768]{1,0:T(8,128)(2,1)S(1)}, u32[]{:S(2)}, u32[]{:S(2)}) collective-permute-start(bf16[480,768]{1,0:T(8,128)(2,1)S(1)} %get-tuple-element.241), channel_id=1, source_target_pairs={{0,4},{1,5},{2,6},{3,7},{4,0},{5,1},{6,2},{7,3},{8,12},{9,13},{10,... | collective-permute-start | bytes 2211848 | tf_op jit(solution)/shard_map/ppermute | solution.py:915
  230.2 32.8 %collective-permute-start.35 = (bf16[480,768]{1,0:T(8,128)(2,1)S(1)}, bf16[480,768]{1,0:T(8,128)(2,1)S(1)}, u32[]{:S(2)}, u32[]{:S(2)}) collective-permute-start(bf16[480,768]{1,0:T(8,128)(2,1)S(1)} %get-tuple-element.242), channel_id=1, source_target_pairs={{0,6},{1,7},{2,4},{3,5},{4,2},{5,3},{6,0},{7,1},{8,14},{9,15},{10,... | collective-permute-start | bytes 2211848 | tf_op jit(solution)/shard_map/ppermute | solution.py:915
  233.2 29.8 %collective-permute-start.32 = (bf16[4,96,768]{2,1,0:T(8,128)(2,1)S(1)}, bf16[4,96,768]{2,1,0:T(8,128)(2,1)S(1)}, u32[]{:S(2)}, u32[]{:S(2)}) collective-permute-start(bf16[4,96,768]{2,1,0:T(8,128)(2,1)S(1)} %get-tuple-element.239), channel_id=1, source_target_pairs={{0,16},{8,24},{16,0},{24,8},{1,17},{9,25},{17,1},{25,9},{2,18},{10... | collective-permute-start | bytes 1769480 | tf_op jit(solution)/shard_map/ppermute | solution.py:915
  280.1 18.6 %collective-permute-start.41 = (bf16[192,480]{1,0:T(8,128)(2,1)S(1)}, bf16[192,480]{1,0:T(8,128)(2,1)S(1)}, u32[]{:S(2)}, u32[]{:S(2)}) collective-permute-start(bf16[192,480]{1,0:T(8,128)(2,1)S(1)} %fusion.9), channel_id=1, source_target_pairs={{0,16},{8,24},{16,0},{24,8},{1,17},{9,25},{17,1},{25,9},{2,18},{10... | collective-permute-start | bytes 552968 | tf_op jit(solution)/shard_map/ppermute | solution.py:915
  282.7 26.7 %collective-permute-start.45 = (bf16[288,768]{1,0:T(8,128)(2,1)S(1)}, bf16[288,768]{1,0:T(8,128)(2,1)S(1)}, u32[]{:S(2)}, u32[]{:S(2)}) collective-permute-start(bf16[288,768]{1,0:T(8,128)(2,1)S(1)} %get-tuple-element.287), channel_id=1, source_target_pairs={{0,2},{1,3},{2,0},{3,1},{4,6},{5,7},{6,4},{7,5},{8,10},{9,11},{10,... | collective-permute-start | bytes 1327112 | tf_op jit(solution)/shard_map/ppermute | solution.py:915
  283.5 25.9 %collective-permute-start.46 = (bf16[288,768]{1,0:T(8,128)(2,1)S(1)}, bf16[288,768]{1,0:T(8,128)(2,1)S(1)}, u32[]{:S(2)}, u32[]{:S(2)}) collective-permute-start(bf16[288,768]{1,0:T(8,128)(2,1)S(1)} %get-tuple-element.288), channel_id=1, source_target_pairs={{0,4},{1,5},{2,6},{3,7},{4,0},{5,1},{6,2},{7,3},{8,12},{9,13},{10,... | collective-permute-start | bytes 1327112 | tf_op jit(solution)/shard_map/ppermute | solution.py:915
  285.0 24.4 %collective-permute-start.47 = (bf16[288,768]{1,0:T(8,128)(2,1)S(1)}, bf16[288,768]{1,0:T(8,128)(2,1)S(1)}, u32[]{:S(2)}, u32[]{:S(2)}) collective-permute-start(bf16[288,768]{1,0:T(8,128)(2,1)S(1)} %get-tuple-element.289), channel_id=1, source_target_pairs={{0,6},{1,7},{2,4},{3,5},{4,2},{5,3},{6,0},{7,1},{8,14},{9,15},{10,... | collective-permute-start | bytes 1327112 | tf_op jit(solution)/shard_map/ppermute | solution.py:915
  310.8 17.2 %collective-permute-start.50 = (bf16[192,288]{1,0:T(8,128)(2,1)S(1)}, bf16[192,288]{1,0:T(8,128)(2,1)S(1)}, u32[]{:S(2)}, u32[]{:S(2)}) collective-permute-start(bf16[192,288]{1,0:T(8,128)(2,1)S(1)} %get-tuple-element.296), channel_id=1, source_target_pairs={{0,8},{8,0},{16,24},{24,16},{1,9},{9,1},{17,25},{25,17},{2,10},{10... | collective-permute-start | bytes 331784 | tf_op jit(solution)/shard_map/ppermute | solution.py:915
  (54 other events, 545.3 us)
